TPU v7x, 32 devices: a whole 2x2x4 slice. The times are simulated.
32 devices in a mesh: bank: 8 (over y, x, core), blk: 4 (over z).
Axes of the slice: x: 2, y: 2, z: 4, core: 2. Of those that a mesh axis runs over, the one named last changes fastest.
Arguments:
- self_queries: bfloat16 [8, 768, 1024], P('bank', 'blk'), may hold values from -8 to 8
- cache_keys: bfloat16 [8, 1536, 1024], P('bank', 'blk'), may hold values from -8 to 8
- cache_values: bfloat16 [8, 1536, 1024], P('bank', 'blk'), may hold values from -6 to 6
- cache_lengths: int32 [8, 4], P('bank', 'blk'), may hold values from 2 to 384
- cross_queries: bfloat16 [8, 768, 1024], P('bank', 'blk'), may hold values from -8 to 8
- bank_kv: bfloat16 [16, 64, 2048], P('bank'), may hold values from -8 to 8
- span_home: int32 [16], replicated, may hold values from 0 to 15, as said below
- neighbours: int32 [8, 48, 2], P('bank', 'blk'), may hold values from 0 to 15, as said below
Outputs:
- context_out: bfloat16 [8, 768, 1024], P('bank', 'blk')
- retrieved_out: bfloat16 [8, 768, 1024], P('bank', 'blk')
Inputs may be any that keep to these rules, and one draw needn't show every extreme that they name: `span_home`: a permutation of the span ids. `neighbours`: of the 24 ids of one device, at most 3 have span_home[id] // 2 equal to any one bank index, and on every device some bank index is named exactly 3 times.
All inputs are finite; a program needn't handle non-finite values.
Results may differ from a plain program's by a relative error of at most 0.0048.
Values may be sent and summed in bfloat16 or wider, within the bound.
No kernel may reach another device: no remote copies, remote signals or barrier semaphores. Data moves between devices by JAX's collectives and lax.ppermute only.
A program may use at most 64 MiB of HBM per device.

v0:
```python
import jax
import jax.numpy as jnp
from jax import lax
from jax.sharding import PartitionSpec as P

HEADS = 8
HD = 128
SPAN = 16
NROW = 64
NEIGH = 2


def passed_along(block, axis, distance):
    devices = range(lax.axis_size(axis))
    route = [((i - distance) % len(devices), i) for i in devices]
    return lax.ppermute(block, axis, route)


def partial_scores(queries, keys, values, valid):
    rows = queries.shape[0]
    width = keys.shape[0]
    query_heads = queries.reshape(rows, HEADS, HD)
    key_heads = keys.reshape(width, HEADS, HD)
    value_heads = values.reshape(width, HEADS, HD)
    scores = jnp.einsum(
        "rhd,chd->hrc", query_heads, key_heads, preferred_element_type=jnp.float32
    ) * HD ** (-0.5)
    scores = jnp.where(valid, scores, -jnp.inf)
    top = jnp.max(scores, axis=2)
    expo = jnp.exp(scores - top[:, :, None])
    total = jnp.sum(expo, axis=2)
    weights = expo.astype(jnp.bfloat16)
    summed = jnp.einsum("hrc,chd->rhd", weights, value_heads, preferred_element_type=jnp.float32)
    return (summed, top.T, total.T)


def merge_state(state, part):
    best = jnp.maximum(state[1], part[1])
    older = jnp.exp(state[1] - best)
    newer = jnp.exp(part[1] - best)
    summed = state[0] * older[..., None] + part[0] * newer[..., None]
    return (summed, best, state[2] * older + part[2] * newer)


def cycle_pass(queries, keys, values, valid, move_queries, move_state):
    rows = queries.shape[0]
    state = (
        jnp.zeros((rows, HEADS, HD), jnp.float32),
        jnp.full((rows, HEADS), -jnp.inf, jnp.float32),
        jnp.zeros((rows, HEADS), jnp.float32),
    )

    def turn(step, carry):
        current, acc = carry
        acc = move_state(merge_state(acc, partial_scores(current, keys, values, valid)))
        return (move_queries(current), acc)

    current, state = lax.fori_loop(0, lax.axis_size("blk") - 1, turn, (queries, state))
    return move_state(merge_state(state, partial_scores(current, keys, values, valid)))


def session_attention(queries, keys, values, valid):
    rows = queries.shape[0]

    def ahead_queries(block):
        return passed_along(block, "blk", 1)

    def ahead_state(state):
        return passed_along(state, "blk", 1)

    state = cycle_pass(queries, keys, values, valid, ahead_queries, ahead_state)
    output = state[0] / state[2][..., None]
    return output.reshape(rows, HEADS * HD).astype(jnp.bfloat16)


def fetch_neighbours(cross, bank_kv, span_home, neighbours):
    spans = neighbours.shape[0]
    width = cross.shape[1]
    wanted = neighbours.reshape(-1)
    requests = wanted.shape[0]
    owners = lax.axis_size("bank")
    capacity = max(2, (requests + owners - 1) // owners)
    places = owners * capacity
    local_spans = bank_kv.shape[0]
    homes = jnp.take(span_home, wanted)
    owner = homes // local_spans
    local_slot = homes % local_spans
    hits = (owner[:, None] == jnp.arange(owners, dtype=jnp.int32)[None, :]).astype(jnp.int32)
    earlier = (jnp.arange(requests)[:, None] > jnp.arange(requests)[None, :]).astype(jnp.int32)
    rank = jnp.sum(jnp.dot(earlier, hits) * hits, axis=1)
    target = owner * capacity + rank
    placing = target[:, None] == jnp.arange(places, dtype=jnp.int32)[None, :]
    per_request = jnp.repeat(cross.reshape(spans, SPAN, width), NEIGH, axis=0)
    outgoing = jnp.einsum(
        "rs,rck->sck", placing.astype(jnp.bfloat16), per_request, preferred_element_type=jnp.float32
    ).astype(jnp.bfloat16)
    marks = jnp.sum(jnp.where(placing, local_slot[:, None], 0), axis=0).astype(jnp.bfloat16)
    outgoing = outgoing.reshape(owners, capacity, SPAN, width)
    marks = marks.reshape(owners, capacity)
    arrived, arrived_marks = (
        lax.all_to_all(outgoing, "bank", split_axis=0, concat_axis=0, tiled=True),
        lax.all_to_all(marks, "bank", split_axis=0, concat_axis=0, tiled=True),
    )
    flat_rows = arrived.reshape(owners * capacity * SPAN, width)
    row_marks = jnp.repeat(arrived_marks.reshape(-1).astype(jnp.int32), SPAN)
    bank_keys = bank_kv[:, :, :width].reshape(local_spans * NROW, width)
    bank_values = bank_kv[:, :, width:].reshape(local_spans * NROW, width)
    column_span = jnp.arange(local_spans * NROW, dtype=jnp.int32) // NROW
    valid = (row_marks[:, None] == column_span[None, :])[None]
    summed, top, total = partial_scores(flat_rows, bank_keys, bank_values, valid)
    normal = (summed / total[..., None]).astype(jnp.bfloat16).reshape(owners, capacity, SPAN, width)
    top = top.reshape(owners, capacity, SPAN, HEADS)
    total = total.reshape(owners, capacity, SPAN, HEADS)
    normal = lax.all_to_all(normal, "bank", split_axis=0, concat_axis=0, tiled=True)
    top, total = (
        lax.all_to_all(top, "bank", split_axis=0, concat_axis=0, tiled=True),
        lax.all_to_all(total, "bank", split_axis=0, concat_axis=0, tiled=True),
    )
    normal = jnp.take(normal.reshape(places, SPAN, width), target, axis=0)
    normal = normal.reshape(spans, NEIGH, SPAN, HEADS, HD).astype(jnp.float32)
    top = jnp.take(top.reshape(places, SPAN, HEADS), target, axis=0).reshape(
        spans, NEIGH, SPAN, HEADS
    )
    total = jnp.take(total.reshape(places, SPAN, HEADS), target, axis=0).reshape(
        spans, NEIGH, SPAN, HEADS
    )
    best = jnp.max(top, axis=1)
    weight = jnp.exp(top - best[:, None]) * total
    numer = jnp.sum(weight[..., None] * normal, axis=1)
    denom = jnp.sum(weight, axis=1)
    output = numer / denom[..., None]
    return output.reshape(spans * SPAN, width).astype(jnp.bfloat16)


def on_device(
    self_queries,
    cache_keys,
    cache_values,
    cache_lengths,
    cross_queries,
    bank_kv,
    span_home,
    neighbours,
):
    queries = self_queries[0]
    keys = cache_keys[0]
    values = cache_values[0]
    valid = (jnp.arange(keys.shape[0], dtype=jnp.int32) < cache_lengths[0, 0])[None, None, :]
    context = session_attention(queries, keys, values, valid)
    retrieved = fetch_neighbours(cross_queries[0], bank_kv, span_home, neighbours[0])
    return (context[None], retrieved[None])


def solution(mesh):
    return jax.shard_map(
        on_device,
        mesh=mesh,
        in_specs=(
            P("bank", "blk", None),
            P("bank", "blk", None),
            P("bank", "blk", None),
            P("bank", "blk"),
            P("bank", "blk", None),
            P("bank", None, None),
            P(),
            P("bank", "blk", None),
        ),
        out_specs=(P("bank", "blk", None), P("bank", "blk", None)),
        check_vma=False,
    )
```

profile of v0, /device:TPU:8, one launch (start us, length us, event | category | flops | bytes accessed | tf_op | source)
XLA Modules:
  0.0 177.7 jit_solution(11692034541859693077)
XLA Ops:
  0.7 0.9 copy.53
  1.8 0.7 gather_fusion
  2.8 0.7 convert_element_type.82
  3.5 3.7 %all-to-all-start = ((bf16[8,1,3]{2,1,0:T(2,128)(2,1)}), bf16[8,1,3]{2,1,0:T(2,128)(2,1)S(1)}, u32[]{:S(2)}, u32[]{:S(2)}) async-start(bf16[8,1,3]{2,1,0:T(2,128)(2,1)} %convert_element_type.82), calls=%async_computation | async-start | bytes 8192 | tf_op jit(solution)/shard_map/all_to_all | solution.py:102
  7.9 2.2 %copy.75 = bf16[48,8,8,128]{3,2,1,0:T(8,128)(2,1)} copy(bf16[48,8,8,128]{3,1,2,0:T(8,128)(2,1)} %bitcast.148) | data formatting | bytes 1572864
  10.3 1.0 broadcast_in_dim.106
  11.2 103.2 %while.17 = (s32[]{:T(128)}, bf16[192,1024]{1,0:T(8,128)(2,1)S(1)}, f32[192,8,128]{2,0,1:T(8,128)}, f32[192,8]{0,1:T(8,128)S(1)}, f32[192,8]{0,1:T(8,128)S(1)}, ...) while((s32[]{:T(128)}, bf16[192,1024]{1,0:T(8,128)(2,1)S(1)}, ...), condition=%wide.region_3.4_spmd.clone, body=%wide.region_0.3_spmd.clone.sunk | while | flops 309074304 | bytes 19404544 | solution.py:58
  11.2 0.7 compare_reduce_fusion.2
  12.9 0.9 fusion.76
  13.8 2.8 %fusion.78 = f32[192,8,128]{2,0,1:T(8,128)} fusion(f32[8,192,384]{2,1,0:T(8,128)S(1)} %get-tuple-element.165, f32[8,192]{1,0:T(8,128)S(1)} %get-tuple-element.166, pred[384]{0:T(512)(128)(4,1)S(1)} %compare_reduce_fusion.2, bf16[384,8,128]{2,1,0:T(8,128)(2,1)S(1)} %bitcast.152, f32[192,8,128]{2,0,1:T(8,128)} %get-tuple-element.182, ...), kind=kOutput, calls=%fused_computation.12.clone.1 | convolution fusion | flops 153944064 | bytes 4737408 | tf_op jit(solution)/shard_map/while/body/eval_jaxpr/hrc,chd->rhd/dot_general | solution.py:33
  16.7 1.6 collective-permute-start.1
  18.3 1.6 collective-permute-start
  20.1 1.6 collective-permute-start.3
  21.6 23.9 %collective-permute-done.2 = f32[192,8]{0,1:T(8,128)S(1)} collective-permute-done((f32[192,8]{0,1:T(8,128)S(1)}, f32[192,8]{0,1:T(8,128)S(1)}, u32[]{:S(2)}, u32[]{:S(2)}) %collective-permute-start.2) | collective-permute-done | bytes 6176 | tf_op jit(solution)/shard_map/while/body/eval_jaxpr/ppermute | solution.py:16
  45.6 0.7 compare_reduce_fusion.2
  47.3 0.9 fusion.76
  48.2 2.8 %fusion.78 = f32[192,8,128]{2,0,1:T(8,128)} fusion(f32[8,192,384]{2,1,0:T(8,128)S(1)} %get-tuple-element.165, f32[8,192]{1,0:T(8,128)S(1)} %get-tuple-element.166, pred[384]{0:T(512)(128)(4,1)S(1)} %compare_reduce_fusion.2, bf16[384,8,128]{2,1,0:T(8,128)(2,1)S(1)} %bitcast.152, f32[192,8,128]{2,0,1:T(8,128)} %get-tuple-element.182, ...), kind=kOutput, calls=%fused_computation.12.clone.1 | convolution fusion | flops 153944064 | bytes 4737408 | tf_op jit(solution)/shard_map/while/body/eval_jaxpr/hrc,chd->rhd/dot_general | solution.py:33
  51.1 1.6 collective-permute-start.1
  52.6 1.6 collective-permute-start
  54.2 2.1 %collective-permute-start.2 = (f32[192,8]{0,1:T(8,128)S(1)}, f32[192,8]{0,1:T(8,128)S(1)}, u32[]{:S(2)}, u32[]{:S(2)}) collective-permute-start(f32[192,8]{0,1:T(8,128)S(1)} %get-tuple-element.169), channel_id=1, source_target_pairs={{3,0},{0,1},{1,2},{2,3},{7,4},{4,5},{5,6},{6,7},{11,8},{8,9},{9,10... | collective-permute-start | bytes 18440 | tf_op jit(solution)/shard_map/while/body/eval_jaxpr/ppermute | solution.py:16
  56.3 23.4 %collective-permute-done.2 = f32[192,8]{0,1:T(8,128)S(1)} collective-permute-done((f32[192,8]{0,1:T(8,128)S(1)}, f32[192,8]{0,1:T(8,128)S(1)}, u32[]{:S(2)}, u32[]{:S(2)}) %collective-permute-start.2) | collective-permute-done | bytes 6176 | tf_op jit(solution)/shard_map/while/body/eval_jaxpr/ppermute | solution.py:16
  81.5 0.9 fusion.76
  82.5 2.8 %fusion.78 = f32[192,8,128]{2,0,1:T(8,128)} fusion(f32[8,192,384]{2,1,0:T(8,128)S(1)} %get-tuple-element.165, f32[8,192]{1,0:T(8,128)S(1)} %get-tuple-element.166, pred[384]{0:T(512)(128)(4,1)S(1)} %compare_reduce_fusion.2, bf16[384,8,128]{2,1,0:T(8,128)(2,1)S(1)} %bitcast.152, f32[192,8,128]{2,0,1:T(8,128)} %get-tuple-element.182, ...), kind=kOutput, calls=%fused_computation.12.clone.1 | convolution fusion | flops 153944064 | bytes 4737408 | tf_op jit(solution)/shard_map/while/body/eval_jaxpr/hrc,chd->rhd/dot_general | solution.py:33
  85.3 0.9 collective-permute-start.1
  86.2 1.6 collective-permute-start
  87.8 3.9 %collective-permute-start.2 = (f32[192,8]{0,1:T(8,128)S(1)}, f32[192,8]{0,1:T(8,128)S(1)}, u32[]{:S(2)}, u32[]{:S(2)}) collective-permute-start(f32[192,8]{0,1:T(8,128)S(1)} %get-tuple-element.169), channel_id=1, source_target_pairs={{3,0},{0,1},{1,2},{2,3},{7,4},{4,5},{5,6},{6,7},{11,8},{8,9},{9,10... | collective-permute-start | bytes 18440 | tf_op jit(solution)/shard_map/while/body/eval_jaxpr/ppermute | solution.py:16
  91.8 22.5 %collective-permute-done.2 = f32[192,8]{0,1:T(8,128)S(1)} collective-permute-done((f32[192,8]{0,1:T(8,128)S(1)}, f32[192,8]{0,1:T(8,128)S(1)}, u32[]{:S(2)}, u32[]{:S(2)}) %collective-permute-start.2) | collective-permute-done | bytes 6176 | tf_op jit(solution)/shard_map/while/body/eval_jaxpr/ppermute | solution.py:16
  114.4 1.7 fusion.21
  116.2 0.9 fusion.22
  117.1 2.8 %fusion.28 = f32[192,8,128]{2,0,1:T(8,128)} fusion(f32[8,192,384]{2,1,0:T(8,128)S(1)} %get-tuple-element.107, f32[8,192]{1,0:T(8,128)S(1)} %get-tuple-element.106, pred[384]{0:T(512)(128)(4,1)S(1)} %iota_compare_fusion.5, bf16[384,8,128]{2,1,0:T(8,128)(2,1)S(1)} %bitcast.165, f32[192,8,128]{2,0,1:T(8,128)} %get-tuple-element.48, ...), kind=kOutput, calls=%fused_computation.46 | convolution fusion | flops 153944064 | bytes 4737408 | tf_op jit(solution)/shard_map/hrc,chd->rhd/dot_general | solution.py:33
  120.0 2.2 %collective-permute-start.5 = (f32[192,8]{0,1:T(8,128)S(1)}, f32[192,8]{0,1:T(8,128)S(1)}, u32[]{:S(2)}, u32[]{:S(2)}) collective-permute-start(f32[192,8]{0,1:T(8,128)S(1)} %get-tuple-element.96), channel_id=1, source_target_pairs={{3,0},{0,1},{1,2},{2,3},{7,4},{4,5},{5,6},{6,7},{11,8},{8,9},{9,10... | collective-permute-start | bytes 18440 | tf_op jit(solution)/shard_map/ppermute | solution.py:16
  123.8 1.3 copy.57
  125.2 3.6 %all-to-all-start.1 = ((bf16[8,3,16,1024]{3,2,1,0:T(8,128)(2,1)}), bf16[8,3,16,1024]{3,2,1,0:T(8,128)(2,1)S(1)}, u32[]{:S(2)}, u32[]{:S(2)}) async-start(bf16[8,3,16,1024]{3,2,1,0:T(8,128)(2,1)} %bitcast.8), calls=%async_computation.1 | async-start | bytes 1572864 | tf_op jit(solution)/shard_map/all_to_all | solution.py:101
  129.5 11.7 %all-to-all-done.1 = bf16[8,3,16,1024]{3,2,1,0:T(8,128)(2,1)S(1)} async-done(((bf16[8,3,16,1024]{3,2,1,0:T(8,128)(2,1)}), bf16[8,3,16,1024]{3,2,1,0:T(8,128)(2,1)S(1)}, u32[]{:S(2)}, u32[]{:S(2)}) %all-to-all-start.1) | async-done | bytes 786464 | tf_op jit(solution)/shard_map/all_to_all | solution.py:101
  142.4 0.7 reshape.411
  143.1 3.3 %all-to-all-start.3 = ((f32[8,1,384]{2,1,0:T(1,128)}), f32[8,1,384]{2,1,0:T(1,128)S(1)}, u32[]{:S(2)}, u32[]{:S(2)}) async-start(f32[8,1,384]{2,1,0:T(1,128)} %reshape.411), calls=%async_computation.3 | async-start | bytes 24576 | tf_op jit(solution)/shard_map/all_to_all | solution.py:117
  146.8 0.7 reshape.413
  147.5 3.6 %all-to-all-done.3 = f32[8,1,384]{2,1,0:T(1,128)S(1)} async-done(((f32[8,1,384]{2,1,0:T(1,128)}), f32[8,1,384]{2,1,0:T(1,128)S(1)}, u32[]{:S(2)}, u32[]{:S(2)}) %all-to-all-start.3) | async-done | bytes 12320 | tf_op jit(solution)/shard_map/all_to_all | solution.py:117
  151.1 3.3 %all-to-all-start.2 = ((f32[8,1,384]{2,1,0:T(1,128)}), f32[8,1,384]{2,1,0:T(1,128)S(1)}, u32[]{:S(2)}, u32[]{:S(2)}) async-start(f32[8,1,384]{2,1,0:T(1,128)} %reshape.413), calls=%async_computation.2 | async-start | bytes 24576 | tf_op jit(solution)/shard_map/all_to_all | solution.py:116
  154.4 0.8 fusion.24
  155.7 1.2 reshape.360
  157.5 0.7 reduce.7
  158.3 0.8 all-to-all-done.2
  159.1 3.5 %all-to-all-start.4 = ((bf16[8,3,16,1024]{3,2,1,0:T(8,128)(2,1)}), bf16[8,3,16,1024]{3,2,1,0:T(8,128)(2,1)S(1)}, u32[]{:S(2)}, u32[]{:S(2)}) async-start(bf16[8,3,16,1024]{3,2,1,0:T(8,128)(2,1)} %reshape.360), calls=%async_computation.4 | async-start | bytes 1572864 | tf_op jit(solution)/shard_map/all_to_all | solution.py:114
  162.7 0.7 reduce.6
  165.6 0.9 convert_element_type.69
  166.5 8.7 %all-to-all-done.4 = bf16[8,3,16,1024]{3,2,1,0:T(8,128)(2,1)S(1)} async-done(((bf16[8,3,16,1024]{3,2,1,0:T(8,128)(2,1)}), bf16[8,3,16,1024]{3,2,1,0:T(8,128)(2,1)S(1)}, u32[]{:S(2)}, u32[]{:S(2)}) %all-to-all-start.4) | async-done | bytes 786464 | tf_op jit(solution)/shard_map/all_to_all | solution.py:114
  176.8 0.9 convert_element_type.79
  (108 shorter events, 13.6 us)
Async XLA Ops:
  0.6 1.2 copy-start
  0.6 9.4 %copy-start.2 = (bf16[1,384,1024]{2,1,0:T(8,128)(2,1)S(1)}, bf16[1,384,1024]{2,1,0:T(8,128)(2,1)}, u32[]{:S(2)}) copy-start(bf16[1,384,1024]{2,1,0:T(8,128)(2,1)} %param.14) | copy-start | bytes 2359300
  0.7 10.6 %copy-start.1 = (bf16[1,384,1024]{2,1,0:T(8,128)(2,1)S(1)}, bf16[1,384,1024]{2,1,0:T(8,128)(2,1)}, u32[]{:S(2)}) copy-start(bf16[1,384,1024]{2,1,0:T(8,128)(2,1)} %param.13) | copy-start | bytes 2359300
  0.7 10.6 %copy-start.3 = (bf16[1,192,1024]{2,1,0:T(8,128)(2,1)S(1)}, bf16[1,192,1024]{2,1,0:T(8,128)(2,1)}, u32[]{:S(2)}) copy-start(bf16[1,192,1024]{2,1,0:T(8,128)(2,1)} %param.12) | copy-start | bytes 1179652
  3.5 121.6 %all-to-all-start = ((bf16[8,1,3]{2,1,0:T(2,128)(2,1)}), bf16[8,1,3]{2,1,0:T(2,128)(2,1)S(1)}, u32[]{:S(2)}, u32[]{:S(2)}) async-start(bf16[8,1,3]{2,1,0:T(2,128)(2,1)} %convert_element_type.82), calls=%async_computation | async-start | bytes 8192 | tf_op jit(solution)/shard_map/all_to_all | solution.py:102
  16.7 29.0 %collective-permute-start.1 = (f32[192,8,128]{2,0,1:T(8,128)}, f32[192,8,128]{2,0,1:T(8,128)}, u32[]{:S(2)}, u32[]{:S(2)}) collective-permute-start(f32[192,8,128]{2,0,1:T(8,128)} %fusion.78), channel_id=1, source_target_pairs={{3,0},{0,1},{1,2},{2,3},{7,4},{4,5},{5,6},{6,7},{11,8},{8,9},{9,10... | collective-permute-start | bytes 2359304 | tf_op jit(solution)/shard_map/while/body/eval_jaxpr/ppermute | solution.py:16
  18.3 27.4 %collective-permute-start = (bf16[192,1024]{1,0:T(8,128)(2,1)S(1)}, bf16[192,1024]{1,0:T(8,128)(2,1)S(1)}, u32[]{:S(2)}, u32[]{:S(2)}) collective-permute-start(bf16[192,1024]{1,0:T(8,128)(2,1)S(1)} %copy.135), channel_id=1, source_target_pairs={{3,0},{0,1},{1,2},{2,3},{7,4},{4,5},{5,6},{6,7},{11,8},{8,9},{9,10... | collective-permute-start | bytes 1179656 | tf_op jit(solution)/shard_map/while/body/eval_jaxpr/ppermute | solution.py:16
  19.8 25.7 %collective-permute-start.2 = (f32[192,8]{0,1:T(8,128)S(1)}, f32[192,8]{0,1:T(8,128)S(1)}, u32[]{:S(2)}, u32[]{:S(2)}) collective-permute-start(f32[192,8]{0,1:T(8,128)S(1)} %get-tuple-element.169), channel_id=1, source_target_pairs={{3,0},{0,1},{1,2},{2,3},{7,4},{4,5},{5,6},{6,7},{11,8},{8,9},{9,10... | collective-permute-start | bytes 18440 | tf_op jit(solution)/shard_map/while/body/eval_jaxpr/ppermute | solution.py:16
  20.1 25.6 %collective-permute-start.3 = (f32[192,8]{0,1:T(8,128)S(1)}, f32[192,8]{0,1:T(8,128)S(1)}, u32[]{:S(2)}, u32[]{:S(2)}) collective-permute-start(f32[192,8]{0,1:T(8,128)S(1)} %get-tuple-element.170), channel_id=1, source_target_pairs={{3,0},{0,1},{1,2},{2,3},{7,4},{4,5},{5,6},{6,7},{11,8},{8,9},{9,10... | collective-permute-start | bytes 18440 | tf_op jit(solution)/shard_map/while/body/eval_jaxpr/ppermute | solution.py:16
  51.1 28.8 %collective-permute-start.1 = (f32[192,8,128]{2,0,1:T(8,128)}, f32[192,8,128]{2,0,1:T(8,128)}, u32[]{:S(2)}, u32[]{:S(2)}) collective-permute-start(f32[192,8,128]{2,0,1:T(8,128)} %fusion.78), channel_id=1, source_target_pairs={{3,0},{0,1},{1,2},{2,3},{7,4},{4,5},{5,6},{6,7},{11,8},{8,9},{9,10... | collective-permute-start | bytes 2359304 | tf_op jit(solution)/shard_map/while/body/eval_jaxpr/ppermute | solution.py:16
  52.6 27.2 %collective-permute-start = (bf16[192,1024]{1,0:T(8,128)(2,1)S(1)}, bf16[192,1024]{1,0:T(8,128)(2,1)S(1)}, u32[]{:S(2)}, u32[]{:S(2)}) collective-permute-start(bf16[192,1024]{1,0:T(8,128)(2,1)S(1)} %copy.135), channel_id=1, source_target_pairs={{3,0},{0,1},{1,2},{2,3},{7,4},{4,5},{5,6},{6,7},{11,8},{8,9},{9,10... | collective-permute-start | bytes 1179656 | tf_op jit(solution)/shard_map/while/body/eval_jaxpr/ppermute | solution.py:16
  54.2 25.6 %collective-permute-start.2 = (f32[192,8]{0,1:T(8,128)S(1)}, f32[192,8]{0,1:T(8,128)S(1)}, u32[]{:S(2)}, u32[]{:S(2)}) collective-permute-start(f32[192,8]{0,1:T(8,128)S(1)} %get-tuple-element.169), channel_id=1, source_target_pairs={{3,0},{0,1},{1,2},{2,3},{7,4},{4,5},{5,6},{6,7},{11,8},{8,9},{9,10... | collective-permute-start | bytes 18440 | tf_op jit(solution)/shard_map/while/body/eval_jaxpr/ppermute | solution.py:16
  56.3 23.6 %collective-permute-start.3 = (f32[192,8]{0,1:T(8,128)S(1)}, f32[192,8]{0,1:T(8,128)S(1)}, u32[]{:S(2)}, u32[]{:S(2)}) collective-permute-start(f32[192,8]{0,1:T(8,128)S(1)} %get-tuple-element.170), channel_id=1, source_target_pairs={{3,0},{0,1},{1,2},{2,3},{7,4},{4,5},{5,6},{6,7},{11,8},{8,9},{9,10... | collective-permute-start | bytes 18440 | tf_op jit(solution)/shard_map/while/body/eval_jaxpr/ppermute | solution.py:16
  85.3 29.2 %collective-permute-start.1 = (f32[192,8,128]{2,0,1:T(8,128)}, f32[192,8,128]{2,0,1:T(8,128)}, u32[]{:S(2)}, u32[]{:S(2)}) collective-permute-start(f32[192,8,128]{2,0,1:T(8,128)} %fusion.78), channel_id=1, source_target_pairs={{3,0},{0,1},{1,2},{2,3},{7,4},{4,5},{5,6},{6,7},{11,8},{8,9},{9,10... | collective-permute-start | bytes 2359304 | tf_op jit(solution)/shard_map/while/body/eval_jaxpr/ppermute | solution.py:16
  86.2 28.2 %collective-permute-start = (bf16[192,1024]{1,0:T(8,128)(2,1)S(1)}, bf16[192,1024]{1,0:T(8,128)(2,1)S(1)}, u32[]{:S(2)}, u32[]{:S(2)}) collective-permute-start(bf16[192,1024]{1,0:T(8,128)(2,1)S(1)} %copy.135), channel_id=1, source_target_pairs={{3,0},{0,1},{1,2},{2,3},{7,4},{4,5},{5,6},{6,7},{11,8},{8,9},{9,10... | collective-permute-start | bytes 1179656 | tf_op jit(solution)/shard_map/while/body/eval_jaxpr/ppermute | solution.py:16
  87.8 26.5 %collective-permute-start.2 = (f32[192,8]{0,1:T(8,128)S(1)}, f32[192,8]{0,1:T(8,128)S(1)}, u32[]{:S(2)}, u32[]{:S(2)}) collective-permute-start(f32[192,8]{0,1:T(8,128)S(1)} %get-tuple-element.169), channel_id=1, source_target_pairs={{3,0},{0,1},{1,2},{2,3},{7,4},{4,5},{5,6},{6,7},{11,8},{8,9},{9,10... | collective-permute-start | bytes 18440 | tf_op jit(solution)/shard_map/while/body/eval_jaxpr/ppermute | solution.py:16
  91.7 22.7 %collective-permute-start.3 = (f32[192,8]{0,1:T(8,128)S(1)}, f32[192,8]{0,1:T(8,128)S(1)}, u32[]{:S(2)}, u32[]{:S(2)}) collective-permute-start(f32[192,8]{0,1:T(8,128)S(1)} %get-tuple-element.170), channel_id=1, source_target_pairs={{3,0},{0,1},{1,2},{2,3},{7,4},{4,5},{5,6},{6,7},{11,8},{8,9},{9,10... | collective-permute-start | bytes 18440 | tf_op jit(solution)/shard_map/while/body/eval_jaxpr/ppermute | solution.py:16
  117.1 5.1 %copy-start.5 = (bf16[1,192,1024]{2,1,0:T(8,128)(2,1)S(1)}, bf16[1,192,1024]{2,1,0:T(8,128)(2,1)}, u32[]{:S(2)}) copy-start(bf16[1,192,1024]{2,1,0:T(8,128)(2,1)} %param.16) | copy-start | bytes 1179652
  120.0 45.0 %collective-permute-start.4 = (f32[192,8,128]{2,0,1:T(8,128)}, f32[192,8,128]{2,0,1:T(8,128)S(1)}, u32[]{:S(2)}, u32[]{:S(2)}) collective-permute-start(f32[192,8,128]{2,0,1:T(8,128)} %fusion.28), channel_id=1, source_target_pairs={{3,0},{0,1},{1,2},{2,3},{7,4},{4,5},{5,6},{6,7},{11,8},{8,9},{9,10... | collective-permute-start | bytes 2359304 | tf_op jit(solution)/shard_map/ppermute | solution.py:16
  120.0 45.0 %collective-permute-start.5 = (f32[192,8]{0,1:T(8,128)S(1)}, f32[192,8]{0,1:T(8,128)S(1)}, u32[]{:S(2)}, u32[]{:S(2)}) collective-permute-start(f32[192,8]{0,1:T(8,128)S(1)} %get-tuple-element.96), channel_id=1, source_target_pairs={{3,0},{0,1},{1,2},{2,3},{7,4},{4,5},{5,6},{6,7},{11,8},{8,9},{9,10... | collective-permute-start | bytes 18440 | tf_op jit(solution)/shard_map/ppermute | solution.py:16
  123.1 2.0 %copy-start.4 = (bf16[2,64,2048]{2,1,0:T(8,128)(2,1)S(1)}, bf16[2,64,2048]{2,1,0:T(8,128)(2,1)}, u32[]{:S(2)}) copy-start(bf16[2,64,2048]{2,1,0:T(8,128)(2,1)} %param.17) | copy-start | bytes 1572868
  123.7 5.4 %copy-start.6 = (s32[1,12,2]{1,2,0:T(2,128)S(1)}, s32[1,12,2]{1,2,0:T(2,128)}, u32[]{:S(2)}) copy-start(s32[1,12,2]{1,2,0:T(2,128)} %param.19) | copy-start | bytes 292
  125.2 16.1 %all-to-all-start.1 = ((bf16[8,3,16,1024]{3,2,1,0:T(8,128)(2,1)}), bf16[8,3,16,1024]{3,2,1,0:T(8,128)(2,1)S(1)}, u32[]{:S(2)}, u32[]{:S(2)}) async-start(bf16[8,3,16,1024]{3,2,1,0:T(8,128)(2,1)} %bitcast.8), calls=%async_computation.1 | async-start | bytes 1572864 | tf_op jit(solution)/shard_map/all_to_all | solution.py:101
  143.1 8.0 %all-to-all-start.3 = ((f32[8,1,384]{2,1,0:T(1,128)}), f32[8,1,384]{2,1,0:T(1,128)S(1)}, u32[]{:S(2)}, u32[]{:S(2)}) async-start(f32[8,1,384]{2,1,0:T(1,128)} %reshape.411), calls=%async_computation.3 | async-start | bytes 24576 | tf_op jit(solution)/shard_map/all_to_all | solution.py:117
  151.1 8.0 %all-to-all-start.2 = ((f32[8,1,384]{2,1,0:T(1,128)}), f32[8,1,384]{2,1,0:T(1,128)S(1)}, u32[]{:S(2)}, u32[]{:S(2)}) async-start(f32[8,1,384]{2,1,0:T(1,128)} %reshape.413), calls=%async_computation.2 | async-start | bytes 24576 | tf_op jit(solution)/shard_map/all_to_all | solution.py:116
  159.1 16.1 %all-to-all-start.4 = ((bf16[8,3,16,1024]{3,2,1,0:T(8,128)(2,1)}), bf16[8,3,16,1024]{3,2,1,0:T(8,128)(2,1)S(1)}, u32[]{:S(2)}, u32[]{:S(2)}) async-start(bf16[8,3,16,1024]{3,2,1,0:T(8,128)(2,1)} %reshape.360), calls=%async_computation.4 | async-start | bytes 1572864 | tf_op jit(solution)/shard_map/all_to_all | solution.py:114
where the time goes:
time: 181 us; the launch traced here: 178 us
  waiting for transfers between devices  95 us (52%)
  starting transfers between devices  36.4 us (20%)
  local copies, waits for them, and re-layouts  18.9 us (10%)
  matrix products  16.7 us (9%)
  other arithmetic  8.8 us (5%)
    ppermute x14, waiting for transfers between devices, passed_along(): return lax.ppermute(block, axis, route)  70.2 us
    ppermute x14, starting transfers between devices, passed_along(): return lax.ppermute(block, axis, route)  18.9 us
    dot_general x5, matrix products, partial_scores(): jnp.einsum('hrc,chd->rhd', weights, value_heads, preferred_element_type=j...  12.1 us
    all_to_all x1, waiting for transfers between devices, fetch_neighbours(): lax.all_to_all(outgoing, 'bank', split_axis=0, concat_axis=0, tiled=True)  11.7 us
    all_to_all x1, waiting for transfers between devices, fetch_neighbours(): lax.all_to_all(normal, 'bank', split_axis=0, concat_axis=0, tiled=True)  8.73 us
    unnamed x25, local copies, waits for them, and re-layouts  5.34 us
    dot_general x5, matrix products, partial_scores(): jnp.einsum('rhd,chd->hrc', query_heads, key_heads, preferred_element_type...  4.1 us
    reduce_sum x5, other arithmetic, partial_scores(): total = jnp.sum(expo, axis=2)  3.83 us
  transfers between devices with their start and end apart: 19, of which 10 were waited for; matrix products, arithmetic and copies ran while one was open for 22% of the time, Pallas kernels for 0%

commit v1 on v0

--- a/solution.py
+++ b/solution.py
@@ -1,6 +1,8 @@
 import jax
 import jax.numpy as jnp
 from jax import lax
+from jax.experimental import pallas as pl
+from jax.experimental.pallas import tpu as pltpu
 from jax.sharding import PartitionSpec as P
 
 HEADS = 8
@@ -8,6 +10,10 @@
 SPAN = 16
 NROW = 64
 NEIGH = 2
+TAIL = 8
+LOG2E = 1.4426950408889634
+LN2 = 0.6931471805599453
+FAR = -1e30
 
 
 def passed_along(block, axis, distance):
@@ -132,6 +138,301 @@
     return output.reshape(spans * SPAN, width).astype(jnp.bfloat16)
 
 
+def put_logs(out_ref, logs):
+    rows = logs.shape[0]
+    lanes = pl.cdiv(rows, 128) * 128
+    padded = jnp.concatenate((logs, jnp.zeros((lanes - rows, 128), jnp.float32)), axis=0)
+    rest = jnp.transpose(padded)[:TAIL]
+    for place in range(3):
+        piece = rest.astype(jnp.bfloat16)
+        out_ref[rows : rows + TAIL, place * lanes : (place + 1) * lanes] = piece
+        rest = rest - piece.astype(jnp.float32)
+
+
+def get_logs(part_ref):
+    rows = part_ref.shape[0] - TAIL
+    lanes = pl.cdiv(rows, 128) * 128
+    pieces = [
+        part_ref[rows : rows + TAIL, place * lanes : (place + 1) * lanes].astype(jnp.float32)
+        for place in range(3)
+    ]
+    whole = (pieces[2] + pieces[1]) + pieces[0]
+    padded = jnp.concatenate((whole, jnp.zeros((128 - TAIL, lanes), jnp.float32)), axis=0)
+    return jnp.transpose(padded)[:rows]
+
+
+def head_columns(head):
+    return slice(head * HD, (head + 1) * HD)
+
+
+def attend(query_ref, key_ref, value_ref, filled, put):
+    rows = query_ref.shape[0]
+    width = key_ref.shape[0]
+    position = lax.broadcasted_iota(jnp.int32, (1, width), 1)
+    hidden = jnp.where(position < filled, 0.0, FAR)
+    lane = lax.broadcasted_iota(jnp.int32, (rows, 128), 1)
+    tops = jnp.zeros((rows, 128), jnp.float32)
+    totals = jnp.ones((rows, 128), jnp.float32)
+    for head in range(HEADS):
+        columns = head_columns(head)
+        scores = lax.dot_general(
+            query_ref[:, columns],
+            key_ref[:, columns],
+            (((1,), (1,)), ((), ())),
+            preferred_element_type=jnp.float32,
+        )
+        scores = scores * (HD ** (-0.5) * LOG2E) + hidden
+        top = jnp.max(scores, axis=1, keepdims=True)
+        expo = jnp.exp2(scores - top)
+        total = jnp.sum(expo, axis=1, keepdims=True)
+        summed = jnp.dot(
+            expo.astype(jnp.bfloat16), value_ref[:, columns], preferred_element_type=jnp.float32
+        )
+        put(head, summed * (1.0 / total))
+        tops = jnp.where(lane == head, top, tops)
+        totals = jnp.where(lane == head, total, totals)
+    return tops + jnp.log(totals) * LOG2E
+
+
+def attend_packed(query_ref, key_ref, value_ref, filled, out_ref):
+    rows = query_ref.shape[0]
+
+    def put(head, normal):
+        out_ref[:rows, head_columns(head)] = normal.astype(jnp.bfloat16)
+
+    put_logs(out_ref, attend(query_ref, key_ref, value_ref, filled, put))
+
+
+def merge_packed(first_ref, second_ref, out_ref):
+    rows = first_ref.shape[0] - TAIL
+    first = get_logs(first_ref)
+    second = get_logs(second_ref)
+    best = jnp.maximum(first, second)
+    first = jnp.exp2(first - best)
+    second = jnp.exp2(second - best)
+    total = first + second
+    put_logs(out_ref, best + jnp.log(total) * LOG2E)
+    inverse = 1.0 / total
+    first = first * inverse
+    second = second * inverse
+    for head in range(HEADS):
+        columns = head_columns(head)
+        one = slice(head, head + 1)
+        out_ref[:rows, columns] = (
+            first_ref[:rows, columns].astype(jnp.float32) * first[:, one]
+            + second_ref[:rows, columns].astype(jnp.float32) * second[:, one]
+        ).astype(jnp.bfloat16)
+
+
+def is_outer():
+    place = lax.axis_index("blk")
+    return (place == 0) | (place == lax.axis_size("blk") - 1)
+
+
+def every_kernel(filled_ref, query_ref, key_ref, value_ref, out_ref):
+    attend_packed(query_ref, key_ref, value_ref, filled_ref[0, 0], out_ref)
+
+
+def outer_kernel(filled_ref, query_ref, key_ref, value_ref, out_ref):
+    @pl.when(is_outer())
+    def _():
+        attend_packed(query_ref, key_ref, value_ref, filled_ref[0, 0], out_ref)
+
+
+def inner_kernel(filled_ref, query_ref, key_ref, value_ref, out_ref):
+    @pl.when(jnp.logical_not(is_outer()))
+    def _():
+        attend_packed(query_ref, key_ref, value_ref, filled_ref[0, 0], out_ref)
+
+
+def turning_kernel(filled_ref, outer_ref, inner_ref, other_ref, key_ref, value_ref, out_ref, own_ref):
+    @pl.when(is_outer())
+    def _():
+        attend_packed(outer_ref, key_ref, value_ref, filled_ref[0, 0], out_ref)
+
+    @pl.when(jnp.logical_not(is_outer()))
+    def _():
+        attend_packed(inner_ref, key_ref, value_ref, filled_ref[0, 0], own_ref)
+        merge_packed(own_ref, other_ref, out_ref)
+
+
+def joining_kernel(own_a_ref, other_a_ref, own_b_ref, other_b_ref, out_a_ref, out_b_ref):
+    @pl.when(jnp.logical_not(is_outer()))
+    def _():
+        merge_packed(own_a_ref, other_a_ref, out_a_ref)
+        merge_packed(own_b_ref, other_b_ref, out_b_ref)
+
+
+def closing_kernel(own_ref, outer_ref, inner_a_ref, inner_b_ref, out_ref):
+    rows = out_ref.shape[0]
+
+    def close(refs):
+        logs = [get_logs(ref) for ref in refs]
+        best = logs[0]
+        for log in logs[1:]:
+            best = jnp.maximum(best, log)
+        factors = [jnp.exp2(log - best) for log in logs]
+        inverse = 1.0 / sum(factors[1:], factors[0])
+        factors = [factor * inverse for factor in factors]
+        for head in range(HEADS):
+            columns = head_columns(head)
+            one = slice(head, head + 1)
+            terms = [
+                ref[:rows, columns].astype(jnp.float32) * factor[:, one]
+                for ref, factor in zip(refs, factors)
+            ]
+            out_ref[:, columns] = sum(terms[1:], terms[0]).astype(jnp.bfloat16)
+
+    @pl.when(is_outer())
+    def _():
+        close((own_ref, outer_ref))
+
+    @pl.when(jnp.logical_not(is_outer()))
+    def _():
+        close((own_ref, inner_a_ref, inner_b_ref))
+
+
+def spans_kernel(home_ref, wanted_ref, cross_ref, *refs):
+    sources = refs[:8]
+    out_ref, bank_ref, arrivals = refs[8:]
+    spans = wanted_ref.shape[0]
+    held = bank_ref.shape[1]
+    width = cross_ref.shape[1]
+    copies = [
+        pltpu.make_async_copy(source, bank_ref.at[place], arrivals.at[place])
+        for place, source in enumerate(sources)
+    ]
+    for copy in copies:
+        copy.start()
+    for copy in copies:
+        copy.wait()
+    here = lax.axis_index("bank")
+    row_head = lax.broadcasted_iota(jnp.int32, (HEADS * SPAN, width), 0) // SPAN
+    column_head = lax.broadcasted_iota(jnp.int32, (HEADS * SPAN, width), 1) // HD
+    mine = row_head == column_head
+
+    def one_span(span, carry):
+        start = pl.multiple_of(span * SPAN, SPAN)
+        query = cross_ref[pl.ds(start, SPAN), :]
+        spread = jnp.concatenate([query] * HEADS, axis=0)
+        spread = jnp.where(mine, spread, jnp.zeros_like(spread))
+        pairs = []
+        for which in range(NEIGH):
+            home = home_ref[wanted_ref[span, which]]
+            owner = home // held
+            pairs.append((owner ^ here, home - owner * held))
+        keys = jnp.concatenate([bank_ref[place, slot, :, :width] for place, slot in pairs], axis=0)
+        values = jnp.concatenate([bank_ref[place, slot, :, width:] for place, slot in pairs], axis=0)
+        scores = lax.dot_general(
+            spread, keys, (((1,), (1,)), ((), ())), preferred_element_type=jnp.float32
+        ) * (HD ** (-0.5) * LOG2E)
+        top = jnp.max(scores, axis=1, keepdims=True)
+        expo = jnp.exp2(scores - top)
+        total = jnp.sum(expo, axis=1, keepdims=True)
+        weights = (expo * (1.0 / total)).astype(jnp.bfloat16)
+        for head in range(HEADS):
+            columns = head_columns(head)
+            out_ref[pl.ds(start, SPAN), columns] = jnp.dot(
+                weights[head * SPAN : (head + 1) * SPAN],
+                values[:, columns],
+                preferred_element_type=jnp.float32,
+            ).astype(jnp.bfloat16)
+        return carry
+
+    lax.fori_loop(0, spans, one_span, 0)
+
+
+SMALL = pl.BlockSpec(memory_space=pltpu.SMEM)
+WHOLE = pl.BlockSpec(memory_space=pltpu.VMEM)
+AWAY = pl.BlockSpec(memory_space=pl.ANY)
+
+
+def on_core(kernel, shapes, in_specs, scratch=(), flops=0, moved=0, name=None):
+    return pl.pallas_call(
+        kernel,
+        out_shape=shapes,
+        in_specs=in_specs,
+        out_specs=jax.tree.map(lambda _: WHOLE, shapes),
+        scratch_shapes=scratch,
+        cost_estimate=pl.CostEstimate(flops=flops, transcendentals=0, bytes_accessed=moved),
+        compiler_params=pltpu.CompilerParams(vmem_limit_bytes=40 << 20),
+        name=name,
+    )
+
+
+def after(block, *others):
+    return lax.optimization_barrier((block, *others))[0]
+
+
+def joint_pass(queries, keys, values, filled, cross, bank_kv, span_home, wanted):
+    rows, width = queries.shape
+    length = keys.shape[0]
+    packed = jax.ShapeDtypeStruct((rows + TAIL, width), jnp.bfloat16)
+    plain = jax.ShapeDtypeStruct((rows, width), jnp.bfloat16)
+    flops = 4 * rows * length * width
+    moved = 4 * (rows + length) * width
+
+    def over_blk(block, *route):
+        return lax.ppermute(block, "blk", route)
+
+    def over_bank(block, distance):
+        route = [(i, i ^ distance) for i in range(lax.axis_size("bank"))]
+        return lax.ppermute(block, "bank", route)
+
+    def attention(kernel, name, block):
+        call = on_core(kernel, packed, [SMALL] + [WHOLE] * 3, flops=flops, moved=moved, name=name)
+        return call(filled, block, keys, values)
+
+    far = over_blk(queries, (0, 3), (3, 0))
+    bank_x = over_bank(bank_kv, 2)
+    bank_y = over_bank(bank_kv, 4)
+    bank_xy = over_bank(bank_kv, 6)
+    bank_c = over_bank(bank_kv, 1)
+    own = attention(every_kernel, "own", queries)
+    near_queries = after(queries, own)
+    side = over_blk(near_queries, (0, 1), (1, 0), (2, 3), (3, 2))
+    middle = over_blk(near_queries, (1, 2), (2, 1))
+    far_part = attention(outer_kernel, "far", far)
+    far_sent = over_blk(far_part, (0, 1), (3, 2))
+    passed_out = over_blk(middle, (1, 0), (2, 3))
+    passed_in = over_blk(side, (1, 2), (2, 1))
+    side_part = attention(every_kernel, "side", side)
+    middle_part = attention(inner_kernel, "middle", middle)
+    turned = on_core(
+        turning_kernel,
+        packed,
+        [SMALL] + [WHOLE] * 5,
+        scratch=(pltpu.VMEM(packed.shape, packed.dtype),),
+        flops=flops,
+        moved=moved,
+        name="turning",
+    )(filled, passed_out, passed_in, far_sent, keys, values)
+    turned_out = over_blk(turned, (0, 1), (3, 2))
+    turned_in = over_blk(turned, (1, 2), (2, 1))
+    side_sent = over_blk(after(side_part, turned), (0, 1), (3, 2))
+    middle_joined, side_joined = on_core(
+        joining_kernel, (packed, packed), [WHOLE] * 4, flops=8 * rows * width, moved=16 * rows * width, name="joining"
+    )(middle_part, turned_out, side_part, turned_in)
+    middle_sent = over_blk(middle_joined, (1, 2), (2, 1))
+    outer_sent = over_blk(side_joined, (1, 0), (2, 3))
+    context = on_core(
+        closing_kernel, plain, [WHOLE] * 4, flops=8 * rows * width, moved=10 * rows * width, name="closing"
+    )(own, outer_sent, side_sent, middle_sent)
+
+    banks = [bank_kv, bank_c, bank_x, over_bank(bank_x, 1)]
+    banks += [bank_y, over_bank(bank_y, 1), bank_xy, over_bank(bank_xy, 1)]
+    retrieved = on_core(
+        spans_kernel,
+        plain,
+        [SMALL, SMALL, WHOLE] + [AWAY] * 8,
+        scratch=(pltpu.VMEM((8, *bank_kv.shape), bank_kv.dtype), pltpu.SemaphoreType.DMA((8,))),
+        flops=8 * rows * NEIGH * NROW * width,
+        moved=20 * bank_kv.size,
+        name="spans",
+    )(span_home, wanted, cross, *banks)
+    return context, retrieved
+
+
 def on_device(
     self_queries,
     cache_keys,
@@ -146,6 +447,11 @@
     keys = cache_keys[0]
     values = cache_values[0]
     valid = (jnp.arange(keys.shape[0], dtype=jnp.int32) < cache_lengths[0, 0])[None, None, :]
+    if lax.axis_size("blk") == 4 and lax.axis_size("bank") == 8:
+        context, retrieved = joint_pass(
+            queries, keys, values, cache_lengths, cross_queries[0], bank_kv, span_home, neighbours[0]
+        )
+        return (context[None], retrieved[None])
     context = session_attention(queries, keys, values, valid)
     retrieved = fetch_neighbours(cross_queries[0], bank_kv, span_home, neighbours[0])
     return (context[None], retrieved[None])

time: 181 us -> 94.2 us (0.52); the launches traced: 178 us -> 93.6 us
  waiting for transfers between devices: 95 us -> 25 us
  Pallas kernels: 0 us -> 27 us
  matrix products: 16.7 us -> 0 us
  local copies, waits for them, and re-layouts: 18.9 us -> 6.85 us
  other arithmetic: 8.8 us -> 0 us
  starting transfers between devices: 36.4 us -> 33.2 us
    ppermute x14 -> x18, waiting for transfers between devices: 70.2 us -> 25 us  [the longest x11 15.4 us: over_blk(): return lax.ppermute(block, 'blk', route)]
    pallas_call x0 -> x8, Pallas kernels: none -> 27 us  [the longest x1 11.5 us: joint_pass(): on_core(spans_kernel, plain, [SMALL, SMALL, WHOLE] + [AWAY] * 8, scratch=...]
    all_to_all x5 -> x0, waiting for transfers between devices: 24.9 us -> none  [the longest x1 11.7 us: fetch_neighbours(): lax.all_to_all(outgoing, 'bank', split_axis=0, concat_axis=0, tiled=True)]
    all_to_all x5 -> x0, starting transfers between devices: 17.5 us -> none  [the longest x1 3.72 us: fetch_neighbours(): lax.all_to_all(marks, 'bank', split_axis=0, concat_axis=0, tiled=True)]
    dot_general x12 -> x0, matrix products: 16.7 us -> none  [the longest x5 12.1 us: partial_scores(): jnp.einsum('hrc,chd->rhd', weights, value_heads, preferred_element_type=j...]
    ppermute x14 -> x18, starting transfers between devices: 18.9 us -> 33.2 us  [the longest x11 26.6 us: over_blk(): return lax.ppermute(block, 'blk', route)]
    convert_element_type x7 -> x0, local copies, waits for them, and re-layouts: 4.71 us -> none  [the longest x1 1.34 us: fetch_neighbours(): outgoing = jnp.einsum('rs,rck->sck', placing.astype(jnp.bfloat16), per_re...]
    reduce_sum x8 -> x0, other arithmetic: 4.48 us -> none  [the longest x5 3.83 us: partial_scores(): total = jnp.sum(expo, axis=2)]
  transfers between devices with their start and end apart: 19 -> 18, of which waited for: 10 -> 6; matrix products, arithmetic and copies ran while one was open for 22% -> 0% of each run, Pallas kernels for 0% -> 23%
where the time goes in v1:
time: 94.2 us; the launch traced here: 93.6 us
  starting transfers between devices  33.2 us (35%)
  Pallas kernels  27 us (29%)
  waiting for transfers between devices  25 us (27%)
  local copies, waits for them, and re-layouts  6.85 us (7%)
  between operations  1.46 us (2%)
    ppermute x11, starting transfers between devices, over_blk(): return lax.ppermute(block, 'blk', route)  26.6 us
    ppermute x11, waiting for transfers between devices, over_blk(): return lax.ppermute(block, 'blk', route)  15.4 us
    pallas_call x1, Pallas kernels, joint_pass(): on_core(spans_kernel, plain, [SMALL, SMALL, WHOLE] + [AWAY] * 8, scratch=...  11.5 us
    ppermute x7, waiting for transfers between devices, over_bank(): return lax.ppermute(block, 'bank', route)  9.65 us
    pallas_call x4, Pallas kernels, attention(): return call(filled, block, keys, values)  7.21 us
    unnamed x22, local copies, waits for them, and re-layouts  6.76 us
    ppermute x7, starting transfers between devices, over_bank(): return lax.ppermute(block, 'bank', route)  6.65 us
    pallas_call x1, Pallas kernels, joint_pass(): on_core(turning_kernel, packed, [SMALL] + [WHOLE] * 5, scratch=(pltpu.VME...  3.18 us
  transfers between devices with their start and end apart: 18, of which 6 were waited for; matrix products, arithmetic and copies ran while one was open for 0% of the time, Pallas kernels for 23%

profile of v1, /device:TPU:8, one launch (start us, length us, event | category | flops | bytes accessed | tf_op | source)
XLA Modules:
  0.0 93.6 jit_solution(4557728775682186023)
XLA Ops:
  1.3 1.1 %copy-done = bf16[1,384,1024]{2,1,0:T(8,128)(2,1)S(1)} copy-done((bf16[1,384,1024]{2,1,0:T(8,128)(2,1)S(1)}, bf16[1,384,1024]{2,1,0:T(8,128)(2,1)}, u32[]{:S(2)}) %copy-start) | copy-done | bytes 786456
  2.4 1.1 %copy-done.2 = bf16[1,384,1024]{2,1,0:T(8,128)(2,1)S(1)} copy-done((bf16[1,384,1024]{2,1,0:T(8,128)(2,1)S(1)}, bf16[1,384,1024]{2,1,0:T(8,128)(2,1)}, u32[]{:S(2)}) %copy-start.2) | copy-done | bytes 786456
  3.5 1.0 %copy-done.8 = bf16[1,192,1024]{2,1,0:T(8,128)(2,1)S(1)} copy-done((bf16[1,192,1024]{2,1,0:T(8,128)(2,1)S(1)}, bf16[1,192,1024]{2,1,0:T(8,128)(2,1)}, u32[]{:S(2)}) %copy-start.8) | copy-done | bytes 393240
  4.5 2.4 %own.1.own_ref = bf16[200,1024]{1,0:T(8,128)(2,1)S(1)} custom-call(s32[1,1]{1,0:T(1,128)S(6)} %copy.11.filled_ref, bf16[192,1024]{1,0:T(8,128)(2,1)S(1)} %bitcast.18, bf16[384,1024]{1,0:T(8,128)(2,1)S(1)} %bitcast.7, bf16[384,1024]{1,0:T(8,128)(2,1)S(1)} %bitcast.12), custom_call_target="tpu_custom_call" | custom-call | flops 301989888 | bytes 2359296 | tf_op jit(solution)/shard_map/own/pallas_call | solution.py:384
  6.9 0.1 collective-permute-start.2
  7.0 0.7 collective-permute-start.4
  7.7 5.0 %collective-permute-start = (bf16[192,1024]{1,0:T(8,128)(2,1)S(1)}, bf16[192,1024]{1,0:T(8,128)(2,1)S(1)}, u32[]{:S(2)}, u32[]{:S(2)}) collective-permute-start(bf16[192,1024]{1,0:T(8,128)(2,1)S(1)} %bitcast.21), channel_id=1, source_target_pairs={{1,2},{2,1},{5,6},{6,5},{9,10},{10,9},{13,14},{14,13},{17,18},{18,... | collective-permute-start | bytes 1179656 | tf_op jit(solution)/shard_map/ppermute | solution.py:376
  12.7 6.2 %collective-permute-done.2.query_ref = bf16[192,1024]{1,0:T(8,128)(2,1)S(1)} collective-permute-done((bf16[192,1024]{1,0:T(8,128)(2,1)S(1)}, bf16[192,1024]{1,0:T(8,128)(2,1)S(1)}, u32[]{:S(2)}, u32[]{:S(2)}) %collective-permute-start.2) | collective-permute-done | bytes 393248 | tf_op jit(solution)/shard_map/ppermute | solution.py:376
  19.0 3.5 %collective-permute-start.3 = (bf16[192,1024]{1,0:T(8,128)(2,1)S(1)}, bf16[192,1024]{1,0:T(8,128)(2,1)S(1)}, u32[]{:S(2)}, u32[]{:S(2)}) collective-permute-start(bf16[192,1024]{1,0:T(8,128)(2,1)S(1)} %collective-permute-done.2.query_ref), channel_id=1, source_target_pairs={{1,2},{2,1},{5,6},{6,5},{9,10},{10,9},{13,14},{14,13},{17,18},{18,... | collective-permute-start | bytes 1179656 | tf_op jit(solution)/shard_map/ppermute | solution.py:376
  22.5 1.6 %collective-permute-start.14 = (bf16[2,64,2048]{2,1,0:T(8,128)(2,1)S(1)}, bf16[2,64,2048]{2,1,0:T(8,128)(2,1)S(1)}, u32[]{:S(2)}, u32[]{:S(2)}) collective-permute-start(bf16[2,64,2048]{2,1,0:T(8,128)(2,1)S(1)} %copy-done.4), channel_id=1, source_target_pairs={{0,16},{4,20},{8,24},{12,28},{16,0},{20,4},{24,8},{28,12},{1,17},{... | collective-permute-start | bytes 1572872 | tf_op jit(solution)/shard_map/ppermute | solution.py:380
  24.1 0.0 collective-permute-done.4.query_ref
  24.1 1.3 %collective-permute-start.5 = (bf16[200,1024]{1,0:T(8,128)(2,1)S(1)}, bf16[200,1024]{1,0:T(8,128)(2,1)S(1)}, u32[]{:S(2)}, u32[]{:S(2)}) collective-permute-start(bf16[200,1024]{1,0:T(8,128)(2,1)S(1)} %far.1), channel_id=1, source_target_pairs={{0,1},{3,2},{4,5},{7,6},{8,9},{11,10},{12,13},{15,14},{16,17},{19,... | collective-permute-start | bytes 1228808 | tf_op jit(solution)/shard_map/ppermute | solution.py:376
  25.4 5.7 %collective-permute-done.query_ref = bf16[192,1024]{1,0:T(8,128)(2,1)S(1)} collective-permute-done((bf16[192,1024]{1,0:T(8,128)(2,1)S(1)}, bf16[192,1024]{1,0:T(8,128)(2,1)S(1)}, u32[]{:S(2)}, u32[]{:S(2)}) %collective-permute-start) | collective-permute-done | bytes 393248 | tf_op jit(solution)/shard_map/ppermute | solution.py:376
  31.1 3.4 %collective-permute-start.1 = (bf16[192,1024]{1,0:T(8,128)(2,1)S(1)}, bf16[192,1024]{1,0:T(8,128)(2,1)S(1)}, u32[]{:S(2)}, u32[]{:S(2)}) collective-permute-start(bf16[192,1024]{1,0:T(8,128)(2,1)S(1)} %collective-permute-done.query_ref), channel_id=1, source_target_pairs={{1,0},{2,3},{5,4},{6,7},{9,8},{10,11},{13,12},{14,15},{17,16},{18,... | collective-permute-start | bytes 1179656 | tf_op jit(solution)/shard_map/ppermute | solution.py:376
  34.5 1.6 %collective-permute-start.12 = (bf16[2,64,2048]{2,1,0:T(8,128)(2,1)S(1)}, bf16[2,64,2048]{2,1,0:T(8,128)(2,1)S(1)}, u32[]{:S(2)}, u32[]{:S(2)}) collective-permute-start(bf16[2,64,2048]{2,1,0:T(8,128)(2,1)S(1)} %copy-done.4), channel_id=1, source_target_pairs={{0,8},{4,12},{8,0},{12,4},{16,24},{20,28},{24,16},{28,20},{1,9},{5... | collective-permute-start | bytes 1572872 | tf_op jit(solution)/shard_map/ppermute | solution.py:380
  36.1 2.3 %collective-permute-done.3.inner_ref = bf16[192,1024]{1,0:T(8,128)(2,1)S(1)} collective-permute-done((bf16[192,1024]{1,0:T(8,128)(2,1)S(1)}, bf16[192,1024]{1,0:T(8,128)(2,1)S(1)}, u32[]{:S(2)}, u32[]{:S(2)}) %collective-permute-start.3) | collective-permute-done | bytes 393248 | tf_op jit(solution)/shard_map/ppermute | solution.py:376
  38.4 2.4 %collective-permute-start.16 = (bf16[2,64,2048]{2,1,0:T(8,128)(2,1)S(1)}, bf16[2,64,2048]{2,1,0:T(8,128)(2,1)S(1)}, u32[]{:S(2)}, u32[]{:S(2)}) collective-permute-start(bf16[2,64,2048]{2,1,0:T(8,128)(2,1)S(1)} %copy-done.4), channel_id=1, source_target_pairs={{0,24},{4,28},{8,16},{12,20},{16,8},{20,12},{24,0},{28,4},{1,25},{... | collective-permute-start | bytes 1572872 | tf_op jit(solution)/shard_map/ppermute | solution.py:380
  40.9 1.1 %collective-permute-done.1.outer_ref = bf16[192,1024]{1,0:T(8,128)(2,1)S(1)} collective-permute-done((bf16[192,1024]{1,0:T(8,128)(2,1)S(1)}, bf16[192,1024]{1,0:T(8,128)(2,1)S(1)}, u32[]{:S(2)}, u32[]{:S(2)}) %collective-permute-start.1) | collective-permute-done | bytes 393248 | tf_op jit(solution)/shard_map/ppermute | solution.py:376
  41.9 0.0 collective-permute-done.5.other_ref
  41.9 3.2 %turning.1 = bf16[200,1024]{1,0:T(8,128)(2,1)S(1)} custom-call(s32[1,1]{1,0:T(1,128)S(6)} %copy.11.filled_ref, bf16[192,1024]{1,0:T(8,128)(2,1)S(1)} %collective-permute-done.1.outer_ref, bf16[192,1024]{1,0:T(8,128)(2,1)S(1)} %collective-permute-done.3.inner_ref, bf16[200,1024]{1,0:T(8,128)(2,1)S(1)} %collective-permute-done.5.other_ref, ...), custom_call_target="tpu_custom_call" | custom-call | flops 301989888 | bytes 2359296 | tf_op jit(solution)/shard_map/turning/pallas_call | solution.py:401
  45.1 2.6 %collective-permute-start.7 = (bf16[200,1024]{1,0:T(8,128)(2,1)S(1)}, bf16[200,1024]{1,0:T(8,128)(2,1)S(1)}, u32[]{:S(2)}, u32[]{:S(2)}) collective-permute-start(bf16[200,1024]{1,0:T(8,128)(2,1)S(1)} %turning.1), channel_id=1, source_target_pairs={{1,2},{2,1},{5,6},{6,5},{9,10},{10,9},{13,14},{14,13},{17,18},{18,... | collective-permute-start | bytes 1228808 | tf_op jit(solution)/shard_map/ppermute | solution.py:376
  47.7 0.1 collective-permute-start.11
  47.8 0.0 collective-permute-done.14.refs_4_
  47.8 0.5 collective-permute-start.15
  48.3 1.1 %collective-permute-done.12.refs_2_ = bf16[2,64,2048]{2,1,0:T(8,128)(2,1)S(1)} collective-permute-done((bf16[2,64,2048]{2,1,0:T(8,128)(2,1)S(1)}, bf16[2,64,2048]{2,1,0:T(8,128)(2,1)S(1)}, u32[]{:S(2)}, u32[]{:S(2)}) %collective-permute-start.12) | collective-permute-done | bytes 524320 | tf_op jit(solution)/shard_map/ppermute | solution.py:380
  49.5 1.3 %collective-permute-start.6 = (bf16[200,1024]{1,0:T(8,128)(2,1)S(1)}, bf16[200,1024]{1,0:T(8,128)(2,1)S(1)}, u32[]{:S(2)}, u32[]{:S(2)}) collective-permute-start(bf16[200,1024]{1,0:T(8,128)(2,1)S(1)} %turning.1), channel_id=1, source_target_pairs={{0,1},{3,2},{4,5},{7,6},{8,9},{11,10},{12,13},{15,14},{16,17},{19,... | collective-permute-start | bytes 1228808 | tf_op jit(solution)/shard_map/ppermute | solution.py:376
  50.7 8.5 %collective-permute-done.16.refs_6_ = bf16[2,64,2048]{2,1,0:T(8,128)(2,1)S(1)} collective-permute-done((bf16[2,64,2048]{2,1,0:T(8,128)(2,1)S(1)}, bf16[2,64,2048]{2,1,0:T(8,128)(2,1)S(1)}, u32[]{:S(2)}, u32[]{:S(2)}) %collective-permute-start.16) | collective-permute-done | bytes 524320 | tf_op jit(solution)/shard_map/ppermute | solution.py:380
  59.2 0.0 collective-permute-start.13
  59.2 0.0 collective-permute-done.7.other_b_ref
  59.2 0.5 collective-permute-start.17
  59.8 2.4 %side.1.own_b_ref = bf16[200,1024]{1,0:T(8,128)(2,1)S(1)} custom-call(s32[1,1]{1,0:T(1,128)S(6)} %copy.11.filled_ref, bf16[192,1024]{1,0:T(8,128)(2,1)S(1)} %collective-permute-done.2.query_ref, bf16[384,1024]{1,0:T(8,128)(2,1)S(1)} %bitcast.10, bf16[384,1024]{1,0:T(8,128)(2,1)S(1)} %bitcast.15), custom_call_target="tpu_custom_call" | custom-call | flops 301989888 | bytes 2359296 | tf_op jit(solution)/shard_map/side/pallas_call | solution.py:384
  62.1 2.4 %middle.1.own_a_ref = bf16[200,1024]{1,0:T(8,128)(2,1)S(1)} custom-call(s32[1,1]{1,0:T(1,128)S(6)} %copy.11.filled_ref, bf16[192,1024]{1,0:T(8,128)(2,1)S(1)} %collective-permute-done.query_ref, bf16[384,1024]{1,0:T(8,128)(2,1)S(1)} %bitcast.11, bf16[384,1024]{1,0:T(8,128)(2,1)S(1)} %bitcast.16), custom_call_target="tpu_custom_call" | custom-call | flops 301989888 | bytes 2359296 | tf_op jit(solution)/shard_map/middle/pallas_call | solution.py:384
  64.6 0.0 collective-permute-done.6.other_a_ref
  64.6 1.5 %collective-permute-start.9 = (bf16[200,1024]{1,0:T(8,128)(2,1)S(1)}, bf16[200,1024]{1,0:T(8,128)(2,1)}, u32[]{:S(2)}, u32[]{:S(2)}) collective-permute-start(bf16[200,1024]{1,0:T(8,128)(2,1)S(1)} %side.1.own_b_ref), channel_id=1, source_target_pairs={{0,1},{3,2},{4,5},{7,6},{8,9},{11,10},{12,13},{15,14},{16,17},{19,... | collective-permute-start | bytes 1228808 | tf_op jit(solution)/shard_map/ppermute | solution.py:376
  66.0 2.1 %joining.1 = (bf16[200,1024]{1,0:T(8,128)(2,1)}, bf16[200,1024]{1,0:T(8,128)(2,1)}) custom-call(bf16[200,1024]{1,0:T(8,128)(2,1)S(1)} %middle.1.own_a_ref, bf16[200,1024]{1,0:T(8,128)(2,1)S(1)} %collective-permute-done.6.other_a_ref, bf16[200,1024]{1,0:T(8,128)(2,1)S(1)} %side.1.own_b_ref, bf16[200,1024]{1,0:T(8,128)(2,1)S(1)} %collective-permute-done.7.other_b_ref), custom_call_target="tpu_custom_call" | custom-call | flops 1572864 | bytes 3145728 | tf_op jit(solution)/shard_map/joining/pallas_call | solution.py:413
  68.2 0.0 collective-permute-done.11.refs_1_
  68.2 4.8 %collective-permute-start.8 = (bf16[200,1024]{1,0:T(8,128)(2,1)}, bf16[200,1024]{1,0:T(8,128)(2,1)}, u32[]{:S(2)}, u32[]{:S(2)}) collective-permute-start(bf16[200,1024]{1,0:T(8,128)(2,1)} %get-tuple-element.7), channel_id=1, source_target_pairs={{1,0},{2,3},{5,4},{6,7},{9,8},{10,11},{13,12},{14,15},{17,16},{18,... | collective-permute-start | bytes 1228808 | tf_op jit(solution)/shard_map/ppermute | solution.py:376
  73.0 0.0 collective-permute-done.15.refs_5_
  73.0 0.8 copy-done.5
  73.8 2.5 %collective-permute-start.10 = (bf16[200,1024]{1,0:T(8,128)(2,1)}, bf16[200,1024]{1,0:T(8,128)(2,1)}, u32[]{:S(2)}, u32[]{:S(2)}) collective-permute-start(bf16[200,1024]{1,0:T(8,128)(2,1)} %get-tuple-element.9), channel_id=1, source_target_pairs={{1,2},{2,1},{5,6},{6,5},{9,10},{10,9},{13,14},{14,13},{17,18},{18,... | collective-permute-start | bytes 1228808 | tf_op jit(solution)/shard_map/ppermute | solution.py:376
  76.3 0.1 copy.10.wanted_ref
  76.4 0.0 collective-permute-done.13.refs_3_
  76.4 0.6 copy-done.9
  77.1 1.0 %copy-done.6 = bf16[2,64,2048]{2,1,0:T(8,128)(2,1)S(1)} copy-done((bf16[2,64,2048]{2,1,0:T(8,128)(2,1)S(1)}, bf16[2,64,2048]{2,1,0:T(8,128)(2,1)}, u32[]{:S(2)}) %copy-start.6) | copy-done | bytes 524312
  78.1 1.0 %copy-done.7 = bf16[1,192,1024]{2,1,0:T(8,128)(2,1)S(1)} copy-done((bf16[1,192,1024]{2,1,0:T(8,128)(2,1)S(1)}, bf16[1,192,1024]{2,1,0:T(8,128)(2,1)}, u32[]{:S(2)}) %copy-start.7) | copy-done | bytes 393240
  79.1 11.5 %spans.1 = bf16[192,1024]{1,0:T(8,128)(2,1)} custom-call(s32[16]{0:T(128)S(1)} %copy-done.9, s32[12,2]{1,0:T(8,128)S(1)} %copy.10.wanted_ref, bf16[192,1024]{1,0:T(8,128)(2,1)S(1)} %bitcast.17, bf16[2,64,2048]{2,1,0:T(8,128)(2,1)S(1)} %copy-done.4, bf16[2,64,2048]{2,1,0:T(8,128)(2,1)S(1)} %collective-permute-done.11.refs_1_, ...), custom_call_target="tpu_custom_call" | custom-call | flops 201326592 | bytes 5242880 | tf_op jit(solution)/shard_map/spans/pallas_call | solution.py:424
  90.7 0.0 collective-permute-done.10.inner_b_ref
  90.7 2.9 %closing.1 = bf16[192,1024]{1,0:T(8,128)(2,1)} custom-call(bf16[200,1024]{1,0:T(8,128)(2,1)S(1)} %own.1.own_ref, bf16[200,1024]{1,0:T(8,128)(2,1)} %collective-permute-done.8.outer_ref, bf16[200,1024]{1,0:T(8,128)(2,1)} %collective-permute-done.9.inner_a_ref, bf16[200,1024]{1,0:T(8,128)(2,1)} %collective-permute-done.10.inner_b_ref), custom_call_target="tpu_custom_call" | custom-call | flops 1572864 | bytes 1966080 | tf_op jit(solution)/shard_map/closing/pallas_call | solution.py:418
  (19 shorter events, 0.0 us)
Async XLA Ops:
  1.3 1.1 %copy-start = (bf16[1,384,1024]{2,1,0:T(8,128)(2,1)S(1)}, bf16[1,384,1024]{2,1,0:T(8,128)(2,1)}, u32[]{:S(2)}) copy-start(bf16[1,384,1024]{2,1,0:T(8,128)(2,1)} %param.9) | copy-start | bytes 2359300
  2.4 1.1 %copy-start.2 = (bf16[1,384,1024]{2,1,0:T(8,128)(2,1)S(1)}, bf16[1,384,1024]{2,1,0:T(8,128)(2,1)}, u32[]{:S(2)}) copy-start(bf16[1,384,1024]{2,1,0:T(8,128)(2,1)} %param.10) | copy-start | bytes 2359300
  3.5 1.0 %copy-start.8 = (bf16[1,192,1024]{2,1,0:T(8,128)(2,1)S(1)}, bf16[1,192,1024]{2,1,0:T(8,128)(2,1)}, u32[]{:S(2)}) copy-start(bf16[1,192,1024]{2,1,0:T(8,128)(2,1)} %param.8) | copy-start | bytes 1179652
  4.5 17.9 %copy-start.4 = (bf16[2,64,2048]{2,1,0:T(8,128)(2,1)S(1)}, bf16[2,64,2048]{2,1,0:T(8,128)(2,1)}, u32[]{:S(2)}) copy-start(bf16[2,64,2048]{2,1,0:T(8,128)(2,1)} %refs_0_.1) | copy-start | bytes 1572868
  4.5 19.5 %copy-start.1 = (bf16[1,384,1024]{2,1,0:T(8,128)(2,1)S(1)}, bf16[1,384,1024]{2,1,0:T(8,128)(2,1)}, u32[]{:S(2)}) copy-start(bf16[1,384,1024]{2,1,0:T(8,128)(2,1)} %param.9) | copy-start | bytes 2359300
  4.5 19.5 %copy-start.3 = (bf16[1,384,1024]{2,1,0:T(8,128)(2,1)S(1)}, bf16[1,384,1024]{2,1,0:T(8,128)(2,1)}, u32[]{:S(2)}) copy-start(bf16[1,384,1024]{2,1,0:T(8,128)(2,1)} %param.10) | copy-start | bytes 2359300
  6.9 12.1 %collective-permute-start.2 = (bf16[192,1024]{1,0:T(8,128)(2,1)S(1)}, bf16[192,1024]{1,0:T(8,128)(2,1)S(1)}, u32[]{:S(2)}, u32[]{:S(2)}) collective-permute-start(bf16[192,1024]{1,0:T(8,128)(2,1)S(1)} %bitcast.19), channel_id=1, source_target_pairs={{0,1},{1,0},{2,3},{3,2},{4,5},{5,4},{6,7},{7,6},{8,9},{9,8},{10,11... | collective-permute-start | bytes 1179656 | tf_op jit(solution)/shard_map/ppermute | solution.py:376
  7.0 17.1 %collective-permute-start.4 = (bf16[192,1024]{1,0:T(8,128)(2,1)S(1)}, bf16[192,1024]{1,0:T(8,128)(2,1)S(1)}, u32[]{:S(2)}, u32[]{:S(2)}) collective-permute-start(bf16[192,1024]{1,0:T(8,128)(2,1)S(1)} %bitcast.20), channel_id=1, source_target_pairs={{0,3},{3,0},{4,7},{7,4},{8,11},{11,8},{12,15},{15,12},{16,19},{19,... | collective-permute-start | bytes 1179656 | tf_op jit(solution)/shard_map/ppermute | solution.py:376
  7.7 23.4 %collective-permute-start = (bf16[192,1024]{1,0:T(8,128)(2,1)S(1)}, bf16[192,1024]{1,0:T(8,128)(2,1)S(1)}, u32[]{:S(2)}, u32[]{:S(2)}) collective-permute-start(bf16[192,1024]{1,0:T(8,128)(2,1)S(1)} %bitcast.21), channel_id=1, source_target_pairs={{1,2},{2,1},{5,6},{6,5},{9,10},{10,9},{13,14},{14,13},{17,18},{18,... | collective-permute-start | bytes 1179656 | tf_op jit(solution)/shard_map/ppermute | solution.py:376
  19.0 19.4 %collective-permute-start.3 = (bf16[192,1024]{1,0:T(8,128)(2,1)S(1)}, bf16[192,1024]{1,0:T(8,128)(2,1)S(1)}, u32[]{:S(2)}, u32[]{:S(2)}) collective-permute-start(bf16[192,1024]{1,0:T(8,128)(2,1)S(1)} %collective-permute-done.2.query_ref), channel_id=1, source_target_pairs={{1,2},{2,1},{5,6},{6,5},{9,10},{10,9},{13,14},{14,13},{17,18},{18,... | collective-permute-start | bytes 1179656 | tf_op jit(solution)/shard_map/ppermute | solution.py:376
  22.5 25.3 %collective-permute-start.14 = (bf16[2,64,2048]{2,1,0:T(8,128)(2,1)S(1)}, bf16[2,64,2048]{2,1,0:T(8,128)(2,1)S(1)}, u32[]{:S(2)}, u32[]{:S(2)}) collective-permute-start(bf16[2,64,2048]{2,1,0:T(8,128)(2,1)S(1)} %copy-done.4), channel_id=1, source_target_pairs={{0,16},{4,20},{8,24},{12,28},{16,0},{20,4},{24,8},{28,12},{1,17},{... | collective-permute-start | bytes 1572872 | tf_op jit(solution)/shard_map/ppermute | solution.py:380
  24.1 17.8 %collective-permute-start.5 = (bf16[200,1024]{1,0:T(8,128)(2,1)S(1)}, bf16[200,1024]{1,0:T(8,128)(2,1)S(1)}, u32[]{:S(2)}, u32[]{:S(2)}) collective-permute-start(bf16[200,1024]{1,0:T(8,128)(2,1)S(1)} %far.1), channel_id=1, source_target_pairs={{0,1},{3,2},{4,5},{7,6},{8,9},{11,10},{12,13},{15,14},{16,17},{19,... | collective-permute-start | bytes 1228808 | tf_op jit(solution)/shard_map/ppermute | solution.py:376
  31.1 10.8 %collective-permute-start.1 = (bf16[192,1024]{1,0:T(8,128)(2,1)S(1)}, bf16[192,1024]{1,0:T(8,128)(2,1)S(1)}, u32[]{:S(2)}, u32[]{:S(2)}) collective-permute-start(bf16[192,1024]{1,0:T(8,128)(2,1)S(1)} %collective-permute-done.query_ref), channel_id=1, source_target_pairs={{1,0},{2,3},{5,4},{6,7},{9,8},{10,11},{13,12},{14,15},{17,16},{18,... | collective-permute-start | bytes 1179656 | tf_op jit(solution)/shard_map/ppermute | solution.py:376
  34.5 14.9 %collective-permute-start.12 = (bf16[2,64,2048]{2,1,0:T(8,128)(2,1)S(1)}, bf16[2,64,2048]{2,1,0:T(8,128)(2,1)S(1)}, u32[]{:S(2)}, u32[]{:S(2)}) collective-permute-start(bf16[2,64,2048]{2,1,0:T(8,128)(2,1)S(1)} %copy-done.4), channel_id=1, source_target_pairs={{0,8},{4,12},{8,0},{12,4},{16,24},{20,28},{24,16},{28,20},{1,9},{5... | collective-permute-start | bytes 1572872 | tf_op jit(solution)/shard_map/ppermute | solution.py:380
  38.4 20.8 %collective-permute-start.16 = (bf16[2,64,2048]{2,1,0:T(8,128)(2,1)S(1)}, bf16[2,64,2048]{2,1,0:T(8,128)(2,1)S(1)}, u32[]{:S(2)}, u32[]{:S(2)}) collective-permute-start(bf16[2,64,2048]{2,1,0:T(8,128)(2,1)S(1)} %copy-done.4), channel_id=1, source_target_pairs={{0,24},{4,28},{8,16},{12,20},{16,8},{20,12},{24,0},{28,4},{1,25},{... | collective-permute-start | bytes 1572872 | tf_op jit(solution)/shard_map/ppermute | solution.py:380
  45.1 14.1 %collective-permute-start.7 = (bf16[200,1024]{1,0:T(8,128)(2,1)S(1)}, bf16[200,1024]{1,0:T(8,128)(2,1)S(1)}, u32[]{:S(2)}, u32[]{:S(2)}) collective-permute-start(bf16[200,1024]{1,0:T(8,128)(2,1)S(1)} %turning.1), channel_id=1, source_target_pairs={{1,2},{2,1},{5,6},{6,5},{9,10},{10,9},{13,14},{14,13},{17,18},{18,... | collective-permute-start | bytes 1228808 | tf_op jit(solution)/shard_map/ppermute | solution.py:376
  47.7 20.4 %collective-permute-start.11 = (bf16[2,64,2048]{2,1,0:T(8,128)(2,1)S(1)}, bf16[2,64,2048]{2,1,0:T(8,128)(2,1)S(1)}, u32[]{:S(2)}, u32[]{:S(2)}) collective-permute-start(bf16[2,64,2048]{2,1,0:T(8,128)(2,1)S(1)} %copy-done.4), channel_id=1, source_target_pairs={{0,4},{4,0},{8,12},{12,8},{16,20},{20,16},{24,28},{28,24},{1,5},{5... | collective-permute-start | bytes 1572872 | tf_op jit(solution)/shard_map/ppermute | solution.py:380
  47.8 25.2 %collective-permute-start.15 = (bf16[2,64,2048]{2,1,0:T(8,128)(2,1)S(1)}, bf16[2,64,2048]{2,1,0:T(8,128)(2,1)S(1)}, u32[]{:S(2)}, u32[]{:S(2)}) collective-permute-start(bf16[2,64,2048]{2,1,0:T(8,128)(2,1)S(1)} %collective-permute-done.14.refs_4_), channel_id=1, source_target_pairs={{0,4},{4,0},{8,12},{12,8},{16,20},{20,16},{24,28},{28,24},{1,5},{5... | collective-permute-start | bytes 1572872 | tf_op jit(solution)/shard_map/ppermute | solution.py:380
  49.5 15.1 %collective-permute-start.6 = (bf16[200,1024]{1,0:T(8,128)(2,1)S(1)}, bf16[200,1024]{1,0:T(8,128)(2,1)S(1)}, u32[]{:S(2)}, u32[]{:S(2)}) collective-permute-start(bf16[200,1024]{1,0:T(8,128)(2,1)S(1)} %turning.1), channel_id=1, source_target_pairs={{0,1},{3,2},{4,5},{7,6},{8,9},{11,10},{12,13},{15,14},{16,17},{19,... | collective-permute-start | bytes 1228808 | tf_op jit(solution)/shard_map/ppermute | solution.py:376
  59.2 17.2 %collective-permute-start.13 = (bf16[2,64,2048]{2,1,0:T(8,128)(2,1)S(1)}, bf16[2,64,2048]{2,1,0:T(8,128)(2,1)}, u32[]{:S(2)}, u32[]{:S(2)}) collective-permute-start(bf16[2,64,2048]{2,1,0:T(8,128)(2,1)S(1)} %collective-permute-done.12.refs_2_), channel_id=1, source_target_pairs={{0,4},{4,0},{8,12},{12,8},{16,20},{20,16},{24,28},{28,24},{1,5},{5... | collective-permute-start | bytes 1572872 | tf_op jit(solution)/shard_map/ppermute | solution.py:380
  59.2 17.2 %collective-permute-start.17 = (bf16[2,64,2048]{2,1,0:T(8,128)(2,1)S(1)}, bf16[2,64,2048]{2,1,0:T(8,128)(2,1)}, u32[]{:S(2)}, u32[]{:S(2)}) collective-permute-start(bf16[2,64,2048]{2,1,0:T(8,128)(2,1)S(1)} %collective-permute-done.16.refs_6_), channel_id=1, source_target_pairs={{0,4},{4,0},{8,12},{12,8},{16,20},{20,16},{24,28},{28,24},{1,5},{5... | collective-permute-start | bytes 1572872 | tf_op jit(solution)/shard_map/ppermute | solution.py:380
  64.6 26.1 %collective-permute-start.9 = (bf16[200,1024]{1,0:T(8,128)(2,1)S(1)}, bf16[200,1024]{1,0:T(8,128)(2,1)}, u32[]{:S(2)}, u32[]{:S(2)}) collective-permute-start(bf16[200,1024]{1,0:T(8,128)(2,1)S(1)} %side.1.own_b_ref), channel_id=1, source_target_pairs={{0,1},{3,2},{4,5},{7,6},{8,9},{11,10},{12,13},{15,14},{16,17},{19,... | collective-permute-start | bytes 1228808 | tf_op jit(solution)/shard_map/ppermute | solution.py:376
  68.2 22.5 %collective-permute-start.8 = (bf16[200,1024]{1,0:T(8,128)(2,1)}, bf16[200,1024]{1,0:T(8,128)(2,1)}, u32[]{:S(2)}, u32[]{:S(2)}) collective-permute-start(bf16[200,1024]{1,0:T(8,128)(2,1)} %get-tuple-element.7), channel_id=1, source_target_pairs={{1,0},{2,3},{5,4},{6,7},{9,8},{10,11},{13,12},{14,15},{17,16},{18,... | collective-permute-start | bytes 1228808 | tf_op jit(solution)/shard_map/ppermute | solution.py:376
  73.0 0.8 copy-start.5
  73.8 2.5 %copy-start.10 = (s32[1,12,2]{1,2,0:T(2,128)S(1)}, s32[1,12,2]{1,2,0:T(2,128)}, u32[]{:S(2)}) copy-start(s32[1,12,2]{1,2,0:T(2,128)} %param.15) | copy-start | bytes 292
  73.8 16.9 %collective-permute-start.10 = (bf16[200,1024]{1,0:T(8,128)(2,1)}, bf16[200,1024]{1,0:T(8,128)(2,1)}, u32[]{:S(2)}, u32[]{:S(2)}) collective-permute-start(bf16[200,1024]{1,0:T(8,128)(2,1)} %get-tuple-element.9), channel_id=1, source_target_pairs={{1,2},{2,1},{5,6},{6,5},{9,10},{10,9},{13,14},{14,13},{17,18},{18,... | collective-permute-start | bytes 1228808 | tf_op jit(solution)/shard_map/ppermute | solution.py:376
  76.4 0.7 copy-start.9
  77.1 1.0 %copy-start.6 = (bf16[2,64,2048]{2,1,0:T(8,128)(2,1)S(1)}, bf16[2,64,2048]{2,1,0:T(8,128)(2,1)}, u32[]{:S(2)}) copy-start(bf16[2,64,2048]{2,1,0:T(8,128)(2,1)} %copy-done.5) | copy-start | bytes 1572868
  78.1 1.0 %copy-start.7 = (bf16[1,192,1024]{2,1,0:T(8,128)(2,1)S(1)}, bf16[1,192,1024]{2,1,0:T(8,128)(2,1)}, u32[]{:S(2)}) copy-start(bf16[1,192,1024]{2,1,0:T(8,128)(2,1)} %param.12) | copy-start | bytes 1179652

commit v2 on v0

--- a/solution.py
+++ b/solution.py
@@ -1,6 +1,10 @@
+import functools
+
 import jax
 import jax.numpy as jnp
 from jax import lax
+from jax.experimental import pallas as pl
+from jax.experimental.pallas import tpu as pltpu
 from jax.sharding import PartitionSpec as P
 
 HEADS = 8
@@ -8,6 +12,10 @@
 SPAN = 16
 NROW = 64
 NEIGH = 2
+TAIL = 8
+LOG2E = 1.4426950408889634
+LN2 = 0.6931471805599453
+FAR = -1e30
 
 
 def passed_along(block, axis, distance):
@@ -132,6 +140,294 @@
     return output.reshape(spans * SPAN, width).astype(jnp.bfloat16)
 
 
+HALF = HEADS // 2
+HALF_WIDTH = HALF * HD
+
+
+def put_logs(out_ref, logs):
+    rows = logs.shape[0]
+    lanes = pl.cdiv(rows, 128) * 128
+    padded = jnp.concatenate((logs, jnp.zeros((lanes - rows, 128), jnp.float32)), axis=0)
+    whole = jnp.transpose(padded)[:TAIL]
+    first = whole.astype(jnp.bfloat16).astype(jnp.float32)
+    rest = whole - first
+    second = rest.astype(jnp.bfloat16).astype(jnp.float32)
+    upper = lax.broadcasted_iota(jnp.int32, (TAIL, lanes), 0) < HALF
+    out_ref[rows:, :lanes] = jnp.where(upper, first, rest - second).astype(jnp.bfloat16)
+    out_ref[rows:, lanes : 2 * lanes] = second.astype(jnp.bfloat16)
+
+
+def get_logs(part_ref):
+    rows = part_ref.shape[0] - TAIL
+    lanes = pl.cdiv(rows, 128) * 128
+    first = part_ref[rows:, :lanes].astype(jnp.float32)
+    second = part_ref[rows:, lanes : 2 * lanes].astype(jnp.float32)
+    whole = (pltpu.roll(first, HALF, 0) + second) + first
+    padded = jnp.concatenate((whole, jnp.zeros((128 - TAIL, lanes), jnp.float32)), axis=0)
+    return jnp.transpose(padded)[:rows]
+
+
+def head_columns(head):
+    return slice(head * HD, (head + 1) * HD)
+
+
+def attend(query_ref, key_ref, value_ref, filled_ref, half, out_ref):
+    rows = query_ref.shape[0]
+    width = key_ref.shape[0]
+    position = lax.broadcasted_iota(jnp.int32, (1, width), 1)
+    hidden = jnp.where(position < filled_ref[0, 0], 0.0, FAR)
+    lane = lax.broadcasted_iota(jnp.int32, (rows, 128), 1)
+    tops = jnp.zeros((rows, 128), jnp.float32)
+    totals = jnp.ones((rows, 128), jnp.float32)
+    for place in range(HALF):
+        columns = head_columns(half * HALF + place)
+        scores = lax.dot_general(
+            query_ref[:, columns],
+            key_ref[:, columns],
+            (((1,), (1,)), ((), ())),
+            preferred_element_type=jnp.float32,
+        )
+        scores = scores * (HD ** (-0.5) * LOG2E) + hidden
+        top = jnp.max(scores, axis=1, keepdims=True)
+        expo = jnp.exp2(scores - top)
+        total = jnp.sum(expo, axis=1, keepdims=True)
+        summed = jnp.dot(
+            expo.astype(jnp.bfloat16), value_ref[:, columns], preferred_element_type=jnp.float32
+        )
+        out_ref[:rows, head_columns(place)] = (summed * (1.0 / total)).astype(jnp.bfloat16)
+        chosen = (lane == place) | (lane == place + HALF)
+        tops = jnp.where(chosen, top, tops)
+        totals = jnp.where(chosen, total, totals)
+    put_logs(out_ref, tops + jnp.log(totals) * LOG2E)
+
+
+def merge(refs, out_ref, columns, log_ref=None):
+    rows = refs[0].shape[0] - TAIL
+    logs = [get_logs(ref) for ref in refs]
+    best = logs[0]
+    for log in logs[1:]:
+        best = jnp.maximum(best, log)
+    factors = [jnp.exp2(log - best) for log in logs]
+    total = sum(factors[1:], factors[0])
+    if log_ref is not None:
+        put_logs(log_ref, best + jnp.log(total) * LOG2E)
+    inverse = 1.0 / total
+    factors = [factor * inverse for factor in factors]
+    for place in range(HALF):
+        terms = [
+            ref[:rows, head_columns(place)].astype(jnp.float32) * factor[:, place : place + 1]
+            for ref, factor in zip(refs, factors)
+        ]
+        joined = sum(terms[1:], terms[0]).astype(jnp.bfloat16)
+        out_ref[:rows, slice(columns + place * HD, columns + (place + 1) * HD)] = joined
+
+
+def is_outer():
+    place = lax.axis_index("blk")
+    return (place == 0) | (place == lax.axis_size("blk") - 1)
+
+
+def when_outer(body):
+    pl.when(is_outer())(body)
+
+
+def when_inner(body):
+    pl.when(jnp.logical_not(is_outer()))(body)
+
+
+def whole_kernel(filled_ref, query_ref, key_ref, value_ref, out_ref):
+    for half in range(2):
+        attend(query_ref, key_ref, value_ref, filled_ref, half, out_ref.at[half])
+
+
+def outer_kernel(*refs):
+    @when_outer
+    def _():
+        whole_kernel(*refs)
+
+
+def inner_kernel(*refs):
+    @when_inner
+    def _():
+        whole_kernel(*refs)
+
+
+def passed_kernel(filled_ref, query_ref, key_ref, value_ref, other_ref, out_ref, own_ref):
+    @when_inner
+    def _():
+        for half in range(2):
+            attend(query_ref, key_ref, value_ref, filled_ref, half, own_ref)
+            merge((own_ref, other_ref.at[half]), out_ref.at[half], 0, out_ref.at[half])
+
+
+def join_kernel(middle_ref, outer_ref, side_ref, inner_ref, to_middle_ref, to_side_ref):
+    @when_outer
+    def _():
+        to_side_ref[...] = side_ref[...]
+
+    @when_inner
+    def _():
+        for half in range(2):
+            to_middle, to_side = to_middle_ref.at[half], to_side_ref.at[half]
+            merge((middle_ref.at[half], outer_ref.at[half]), to_middle, 0, to_middle)
+            merge((side_ref.at[half], inner_ref.at[half]), to_side, 0, to_side)
+
+
+def closing_kernel(own_ref, side_ref, middle_ref, out_ref):
+    @when_outer
+    def _():
+        for half in range(2):
+            merge((own_ref.at[half], side_ref.at[half]), out_ref, half * HALF_WIDTH)
+
+    @when_inner
+    def _():
+        for half in range(2):
+            parts = (own_ref.at[half], side_ref.at[half], middle_ref.at[half])
+            merge(parts, out_ref, half * HALF_WIDTH)
+
+
+def spans_kernel(home_ref, wanted_ref, cross_ref, *refs):
+    own_ref, core_ref, others_ref, core_others_ref, out_ref, bank_ref, arrivals = refs
+    sources = [own_ref, core_ref]
+    for place in range(3):
+        sources += [others_ref.at[place], core_others_ref.at[place]]
+    spans = wanted_ref.shape[1]
+    held = bank_ref.shape[1]
+    width = cross_ref.shape[1]
+    copies = [
+        pltpu.make_async_copy(source, bank_ref.at[place], arrivals.at[place])
+        for place, source in enumerate(sources)
+    ]
+    for copy in copies:
+        copy.start()
+    for copy in copies:
+        copy.wait()
+    here = lax.axis_index("bank")
+    row_head = lax.broadcasted_iota(jnp.int32, (HEADS * SPAN, width), 0) // SPAN
+    column_head = lax.broadcasted_iota(jnp.int32, (HEADS * SPAN, width), 1) // HD
+    mine = row_head == column_head
+
+    def one_span(span, carry):
+        start = pl.multiple_of(span * SPAN, SPAN)
+        query = cross_ref[pl.ds(start, SPAN), :]
+        spread = jnp.concatenate([query] * HEADS, axis=0)
+        spread = jnp.where(mine, spread, jnp.zeros_like(spread))
+        pairs = []
+        for which in range(NEIGH):
+            home = home_ref[wanted_ref[which, span]]
+            owner = home // held
+            pairs.append((owner ^ here, home - owner * held))
+        keys = jnp.concatenate([bank_ref[place, slot, :, :width] for place, slot in pairs], axis=0)
+        values = jnp.concatenate([bank_ref[place, slot, :, width:] for place, slot in pairs], axis=0)
+        scores = lax.dot_general(
+            spread, keys, (((1,), (1,)), ((), ())), preferred_element_type=jnp.float32
+        ) * (HD ** (-0.5) * LOG2E)
+        top = jnp.max(scores, axis=1, keepdims=True)
+        expo = jnp.exp2(scores - top)
+        total = jnp.sum(expo, axis=1, keepdims=True)
+        weights = (expo * (1.0 / total)).astype(jnp.bfloat16)
+        for head in range(HEADS):
+            columns = head_columns(head)
+            out_ref[pl.ds(start, SPAN), columns] = jnp.dot(
+                weights[head * SPAN : (head + 1) * SPAN],
+                values[:, columns],
+                preferred_element_type=jnp.float32,
+            ).astype(jnp.bfloat16)
+        return carry
+
+    lax.fori_loop(0, spans, one_span, 0, unroll=True)
+
+
+SMALL = pl.BlockSpec(memory_space=pltpu.SMEM)
+WHOLE = pl.BlockSpec(memory_space=pltpu.VMEM)
+AWAY = pl.BlockSpec(memory_space=pl.ANY)
+
+
+def on_core(kernel, shapes, in_specs, scratch=(), name=None):
+    return pl.pallas_call(
+        kernel,
+        out_shape=shapes,
+        in_specs=in_specs,
+        out_specs=jax.tree.map(lambda _: WHOLE, shapes),
+        scratch_shapes=scratch,
+        cost_estimate=pl.CostEstimate(flops=1, transcendentals=0, bytes_accessed=1),
+        compiler_params=pltpu.CompilerParams(vmem_limit_bytes=(10 if name == "spans" else 5) << 20),
+        name=name,
+    )
+
+
+def after(block, *others):
+    return lax.optimization_barrier((block, *others))[0]
+
+
+def joint_pass(queries, keys, values, filled, cross, bank_kv, span_home, wanted):
+    rows, width = queries.shape
+    whole_part = jax.ShapeDtypeStruct((2, rows + TAIL, HALF_WIDTH), jnp.bfloat16)
+    plain = jax.ShapeDtypeStruct((rows, width), jnp.bfloat16)
+
+    def over_blk(block, *route):
+        return lax.ppermute(block, "blk", route)
+
+    def over_bank(block, distance):
+        route = [(i, i ^ distance) for i in range(lax.axis_size("bank"))]
+        return lax.ppermute(block, "bank", route)
+
+    def attention(kernel, name, block):
+        return on_core(kernel, whole_part, [SMALL] + [WHOLE] * 3, name=name)(filled, block, keys, values)
+
+    swap_far = ((0, 3), (3, 0))
+    swap_side = ((0, 1), (1, 0), (2, 3), (3, 2))
+    swap_middle = ((1, 2), (2, 1))
+    inward = ((0, 1), (3, 2))
+    outward = ((1, 0), (2, 3))
+
+    far = over_blk(queries, *swap_far)
+    core_c = over_bank(bank_kv, 1)
+    near = after(queries, core_c)
+    side = over_blk(near, *swap_side)
+    middle = over_blk(near, *swap_middle)
+    near_bank = after(bank_kv, core_c)
+    bank_x = over_bank(near_bank, 2)
+    bank_y = over_bank(near_bank, 4)
+    own = attention(whole_kernel, "own", near)
+    passed_in = over_blk(side, *swap_middle)
+    passed_out = over_blk(middle, *outward)
+    far_part = attention(outer_kernel, "far", after(far, own, side, middle, bank_x, bank_y))
+    far_sent = over_blk(far_part, *inward)
+    turned = attention(outer_kernel, "turned", after(passed_out, passed_in))
+    bank_xy = over_bank(after(bank_kv, far_part), 6)
+    from_outer = over_blk(turned, *inward)
+    met = on_core(
+        passed_kernel,
+        whole_part,
+        [SMALL] + [WHOLE] * 4,
+        scratch=(pltpu.VMEM(whole_part.shape[1:], whole_part.dtype),),
+        name="passed",
+    )(filled, after(passed_in, turned), keys, values, far_sent)
+    from_middle = over_blk(met, *swap_middle)
+    others = after(jnp.stack((bank_x, bank_y, bank_xy)), met)
+    core_others = over_bank(others, 1)
+    side_part = attention(whole_kernel, "side", after(side, met, from_outer))
+    middle_part = attention(inner_kernel, "middle", after(middle, side_part))
+    to_middle, to_side = on_core(join_kernel, (whole_part, whole_part), [WHOLE] * 4, name="join")(
+        middle_part, from_outer, side_part, from_middle
+    )
+    home_middle = over_blk(to_middle, *swap_middle)
+    home_side = over_blk(to_side, *swap_side)
+
+    retrieved = on_core(
+        spans_kernel,
+        plain,
+        [SMALL, SMALL, WHOLE] + [AWAY] * 4,
+        scratch=(pltpu.VMEM((8, *bank_kv.shape), bank_kv.dtype), pltpu.SemaphoreType.DMA((8,))),
+        name="spans",
+    )(span_home, wanted.T, after(cross, to_side), bank_kv, core_c, others, core_others)
+    context = on_core(closing_kernel, plain, [WHOLE] * 3, name="closing")(
+        after(own, retrieved), home_side, home_middle
+    )
+    return context, retrieved
+
+
 def on_device(
     self_queries,
     cache_keys,
@@ -146,6 +442,11 @@
     keys = cache_keys[0]
     values = cache_values[0]
     valid = (jnp.arange(keys.shape[0], dtype=jnp.int32) < cache_lengths[0, 0])[None, None, :]
+    if lax.axis_size("blk") == 4 and lax.axis_size("bank") == 8:
+        context, retrieved = joint_pass(
+            queries, keys, values, cache_lengths, cross_queries[0], bank_kv, span_home, neighbours[0]
+        )
+        return (context[None], retrieved[None])
     context = session_attention(queries, keys, values, valid)
     retrieved = fetch_neighbours(cross_queries[0], bank_kv, span_home, neighbours[0])
     return (context[None], retrieved[None])

time: 181 us -> 85.3 us (0.47); the launches traced: 178 us -> 83.9 us
  waiting for transfers between devices: 95 us -> 34.5 us
  Pallas kernels: 0 us -> 18.8 us
  matrix products: 16.7 us -> 0 us
  local copies, waits for them, and re-layouts: 18.9 us -> 3.28 us
  starting transfers between devices: 36.4 us -> 25.6 us
  other arithmetic: 8.8 us -> 0.17 us
    ppermute x14 -> x15, waiting for transfers between devices: 70.2 us -> 34.5 us  [the longest x10 32.4 us: over_blk(): return lax.ppermute(block, 'blk', route)]
    all_to_all x5 -> x0, waiting for transfers between devices: 24.9 us -> none  [the longest x1 11.7 us: fetch_neighbours(): lax.all_to_all(outgoing, 'bank', split_axis=0, concat_axis=0, tiled=True)]
    pallas_call x0 -> x9, Pallas kernels: none -> 18.8 us  [the longest x5 7.53 us: attention(): on_core(kernel, whole_part, [SMALL] + [WHOLE] * 3, name=name)]
    all_to_all x5 -> x0, starting transfers between devices: 17.5 us -> none  [the longest x1 3.72 us: fetch_neighbours(): lax.all_to_all(marks, 'bank', split_axis=0, concat_axis=0, tiled=True)]
    dot_general x12 -> x0, matrix products: 16.7 us -> none  [the longest x5 12.1 us: partial_scores(): jnp.einsum('hrc,chd->rhd', weights, value_heads, preferred_element_type=j...]
    ppermute x14 -> x15, starting transfers between devices: 18.9 us -> 25.6 us  [the longest x10 21.9 us: over_blk(): return lax.ppermute(block, 'blk', route)]
    convert_element_type x7 -> x0, local copies, waits for them, and re-layouts: 4.71 us -> none  [the longest x1 1.34 us: fetch_neighbours(): outgoing = jnp.einsum('rs,rck->sck', placing.astype(jnp.bfloat16), per_re...]
    reduce_sum x8 -> x0, other arithmetic: 4.48 us -> none  [the longest x5 3.83 us: partial_scores(): total = jnp.sum(expo, axis=2)]
  transfers between devices with their start and end apart: 19 -> 15, of which waited for: 10 -> 7; matrix products, arithmetic and copies ran while one was open for 22% -> 0% of each run, Pallas kernels for 0% -> 20%
where the time goes in v2:
time: 85.3 us; the launch traced here: 83.9 us
  waiting for transfers between devices  34.5 us (40%)
  starting transfers between devices  25.6 us (30%)
  Pallas kernels  18.8 us (22%)
  local copies, waits for them, and re-layouts  3.28 us (4%)
  between operations  1.51 us (2%)
    ppermute x10, waiting for transfers between devices, over_blk(): return lax.ppermute(block, 'blk', route)  32.4 us
    ppermute x10, starting transfers between devices, over_blk(): return lax.ppermute(block, 'blk', route)  21.9 us
    pallas_call x5, Pallas kernels, attention(): on_core(kernel, whole_part, [SMALL] + [WHOLE] * 3, name=name)  7.53 us
    pallas_call x1, Pallas kernels, joint_pass(): on_core(spans_kernel, plain, [SMALL, SMALL, WHOLE] + [AWAY] * 4, scratch=...  4.88 us
    ppermute x5, starting transfers between devices, over_bank(): return lax.ppermute(block, 'bank', route)  3.7 us
    unnamed x18, local copies, waits for them, and re-layouts  3.28 us
    pallas_call x1, Pallas kernels, joint_pass(): on_core(passed_kernel, whole_part, [SMALL] + [WHOLE] * 4, scratch=(pltpu....  3.14 us
    ppermute x5, waiting for transfers between devices, over_bank(): return lax.ppermute(block, 'bank', route)  2.12 us
  transfers between devices with their start and end apart: 15, of which 7 were waited for; matrix products, arithmetic and copies ran while one was open for 0% of the time, Pallas kernels for 20%

profile of v2, /device:TPU:8, one launch (start us, length us, event | category | flops | bytes accessed | tf_op | source)
XLA Modules:
  0.0 83.9 jit_solution(14224559346735780177)
XLA Ops:
  0.6 0.1 collective-permute-start
  0.7 2.1 %collective-permute-done.refs_1_ = bf16[2,64,2048]{2,1,0:T(8,128)(2,1)S(1)} collective-permute-done((bf16[2,64,2048]{2,1,0:T(8,128)(2,1)}, bf16[2,64,2048]{2,1,0:T(8,128)(2,1)S(1)}, u32[]{:S(2)}, u32[]{:S(2)}) %collective-permute-start) | collective-permute-done | bytes 524320 | tf_op jit(solution)/shard_map/ppermute | solution.py:373
  2.8 1.5 %collective-permute-start.7 = (bf16[2,64,2048]{2,1,0:T(8,128)(2,1)}, bf16[2,64,2048]{2,1,0:T(8,128)(2,1)S(1)}, u32[]{:S(2)}, u32[]{:S(2)}) collective-permute-start(bf16[2,64,2048]{2,1,0:T(8,128)(2,1)} %refs_0_.4), channel_id=1, source_target_pairs={{0,16},{4,20},{8,24},{12,28},{16,0},{20,4},{24,8},{28,12},{1,17},{... | collective-permute-start | bytes 1572872 | tf_op jit(solution)/shard_map/ppermute | solution.py:373
  4.3 1.5 %collective-permute-start.6 = (bf16[2,64,2048]{2,1,0:T(8,128)(2,1)}, bf16[2,64,2048]{2,1,0:T(8,128)(2,1)S(1)}, u32[]{:S(2)}, u32[]{:S(2)}) collective-permute-start(bf16[2,64,2048]{2,1,0:T(8,128)(2,1)} %refs_0_.4), channel_id=1, source_target_pairs={{0,8},{4,12},{8,0},{12,4},{16,24},{20,28},{24,16},{28,20},{1,9},{5... | collective-permute-start | bytes 1572872 | tf_op jit(solution)/shard_map/ppermute | solution.py:373
  5.8 0.7 collective-permute-start.5
  6.5 5.3 %collective-permute-start.2 = (bf16[192,1024]{1,0:T(8,128)(2,1)}, bf16[192,1024]{1,0:T(8,128)(2,1)S(1)}, u32[]{:S(2)}, u32[]{:S(2)}) collective-permute-start(bf16[192,1024]{1,0:T(8,128)(2,1)} %bitcast.26), channel_id=1, source_target_pairs={{0,1},{1,0},{2,3},{3,2},{4,5},{5,4},{6,7},{7,6},{8,9},{9,8},{10,11... | collective-permute-start | bytes 1179656 | tf_op jit(solution)/shard_map/ppermute | solution.py:369
  11.8 1.9 %collective-permute-start.1 = (bf16[192,1024]{1,0:T(8,128)(2,1)}, bf16[192,1024]{1,0:T(8,128)(2,1)S(1)}, u32[]{:S(2)}, u32[]{:S(2)}) collective-permute-start(bf16[192,1024]{1,0:T(8,128)(2,1)} %bitcast.27), channel_id=1, source_target_pairs={{1,2},{2,1},{5,6},{6,5},{9,10},{10,9},{13,14},{14,13},{17,18},{18,... | collective-permute-start | bytes 1179656 | tf_op jit(solution)/shard_map/ppermute | solution.py:369
  14.4 0.0 copy-start
  14.4 1.1 %copy-done = bf16[1,384,1024]{2,1,0:T(8,128)(2,1)S(1)} copy-done((bf16[1,384,1024]{2,1,0:T(8,128)(2,1)S(1)}, bf16[1,384,1024]{2,1,0:T(8,128)(2,1)}, u32[]{:S(2)}) %copy-start) | copy-done | bytes 786456
  15.5 1.1 %copy-done.2 = bf16[1,384,1024]{2,1,0:T(8,128)(2,1)S(1)} copy-done((bf16[1,384,1024]{2,1,0:T(8,128)(2,1)S(1)}, bf16[1,384,1024]{2,1,0:T(8,128)(2,1)}, u32[]{:S(2)}) %copy-start.2) | copy-done | bytes 786456
  16.7 1.0 %copy-done.6 = bf16[1,192,1024]{2,1,0:T(8,128)(2,1)S(1)} copy-done((bf16[1,192,1024]{2,1,0:T(8,128)(2,1)S(1)}, bf16[1,192,1024]{2,1,0:T(8,128)(2,1)}, u32[]{:S(2)}) %copy-start.6) | copy-done | bytes 393240
  17.7 2.4 %own.1.own_ref = bf16[2,200,512]{2,1,0:T(8,128)(2,1)S(1)} custom-call(s32[1,1]{1,0:T(1,128)S(6)} %copy.10.filled_ref.refs_0_, bf16[192,1024]{1,0:T(8,128)(2,1)S(1)} %bitcast.28, bf16[384,1024]{1,0:T(8,128)(2,1)S(1)} %bitcast.12, bf16[384,1024]{1,0:T(8,128)(2,1)S(1)} %bitcast.18), custom_call_target="tpu_custom_call" | custom-call | flops 1 | bytes 1 | tf_op jit(solution)/shard_map/own/pallas_call | solution.py:376
  20.1 0.0 collective-permute-done.5.refs_1_
  20.1 8.9 %collective-permute-done.2.query_ref = bf16[192,1024]{1,0:T(8,128)(2,1)S(1)} collective-permute-done((bf16[192,1024]{1,0:T(8,128)(2,1)}, bf16[192,1024]{1,0:T(8,128)(2,1)S(1)}, u32[]{:S(2)}, u32[]{:S(2)}) %collective-permute-start.2) | collective-permute-done | bytes 393248 | tf_op jit(solution)/shard_map/ppermute | solution.py:369
  29.1 0.0 collective-permute-done.1.refs_1_
  29.1 0.0 collective-permute-done.7
  29.1 0.0 collective-permute-done.6
  29.1 0.0 copy-done.1
  29.1 0.0 copy-done.3
  29.1 0.0 copy-done.4
  29.1 0.5 collective-permute-start.11
  29.7 1.3 %collective-permute-start.8 = (bf16[2,200,512]{2,1,0:T(8,128)(2,1)S(1)}, bf16[2,200,512]{2,1,0:T(8,128)(2,1)S(1)}, u32[]{:S(2)}, u32[]{:S(2)}) collective-permute-start(bf16[2,200,512]{2,1,0:T(8,128)(2,1)S(1)} %far.1), channel_id=1, source_target_pairs={{0,1},{3,2},{4,5},{7,6},{8,9},{11,10},{12,13},{15,14},{16,17},{19,... | collective-permute-start | bytes 1228808 | tf_op jit(solution)/shard_map/ppermute | solution.py:369
  31.0 3.3 %collective-permute-start.3 = (bf16[192,1024]{1,0:T(8,128)(2,1)S(1)}, bf16[192,1024]{1,0:T(8,128)(2,1)S(1)}, u32[]{:S(2)}, u32[]{:S(2)}) collective-permute-start(bf16[192,1024]{1,0:T(8,128)(2,1)S(1)} %collective-permute-done.2.query_ref), channel_id=1, source_target_pairs={{1,2},{2,1},{5,6},{6,5},{9,10},{10,9},{13,14},{14,13},{17,18},{18,... | collective-permute-start | bytes 1179656 | tf_op jit(solution)/shard_map/ppermute | solution.py:369
  34.3 2.0 %collective-permute-start.4 = (bf16[192,1024]{1,0:T(8,128)(2,1)S(1)}, bf16[192,1024]{1,0:T(8,128)(2,1)S(1)}, u32[]{:S(2)}, u32[]{:S(2)}) collective-permute-start(bf16[192,1024]{1,0:T(8,128)(2,1)S(1)} %collective-permute-done.1.refs_1_), channel_id=1, source_target_pairs={{1,0},{2,3},{5,4},{6,7},{9,8},{10,11},{13,12},{14,15},{17,16},{18,... | collective-permute-start | bytes 1179656 | tf_op jit(solution)/shard_map/ppermute | solution.py:369
  36.2 7.0 %collective-permute-done.3.query_ref = bf16[192,1024]{1,0:T(8,128)(2,1)S(1)} collective-permute-done((bf16[192,1024]{1,0:T(8,128)(2,1)S(1)}, bf16[192,1024]{1,0:T(8,128)(2,1)S(1)}, u32[]{:S(2)}, u32[]{:S(2)}) %collective-permute-start.3) | collective-permute-done | bytes 393248 | tf_op jit(solution)/shard_map/ppermute | solution.py:369
  43.3 1.2 %collective-permute-done.4.refs_1_ = bf16[192,1024]{1,0:T(8,128)(2,1)S(1)} collective-permute-done((bf16[192,1024]{1,0:T(8,128)(2,1)S(1)}, bf16[192,1024]{1,0:T(8,128)(2,1)S(1)}, u32[]{:S(2)}, u32[]{:S(2)}) %collective-permute-start.4) | collective-permute-done | bytes 393248 | tf_op jit(solution)/shard_map/ppermute | solution.py:369
  44.5 0.0 collective-permute-done.8.other_ref
  44.5 3.1 %passed.1 = bf16[2,200,512]{2,1,0:T(8,128)(2,1)S(1)} custom-call(s32[1,1]{1,0:T(1,128)S(6)} %copy.10.filled_ref.refs_0_, bf16[192,1024]{1,0:T(8,128)(2,1)S(1)} %collective-permute-done.3.query_ref, bf16[384,1024]{1,0:T(8,128)(2,1)S(1)} %bitcast.15, bf16[384,1024]{1,0:T(8,128)(2,1)S(1)} %bitcast.21, bf16[2,200,512]{2,1,0:T(8,128)(2,1)S(1)} %collective-permute-done.8.other_ref), custom_call_target="tpu_custom_call" | custom-call | flops 1 | bytes 1 | tf_op jit(solution)/shard_map/passed/pallas_call | solution.py:400
  47.6 0.0 collective-permute-done.11
  47.6 0.2 pad_maximum_fusion.refs_2_
  47.8 0.1 collective-permute-start.12
  47.9 1.3 %collective-permute-start.9 = (bf16[2,200,512]{2,1,0:T(8,128)(2,1)S(1)}, bf16[2,200,512]{2,1,0:T(8,128)(2,1)S(1)}, u32[]{:S(2)}, u32[]{:S(2)}) collective-permute-start(bf16[2,200,512]{2,1,0:T(8,128)(2,1)S(1)} %turned.1), channel_id=1, source_target_pairs={{0,1},{3,2},{4,5},{7,6},{8,9},{11,10},{12,13},{15,14},{16,17},{19,... | collective-permute-start | bytes 1228808 | tf_op jit(solution)/shard_map/ppermute | solution.py:369
  49.2 3.1 %collective-permute-start.10 = (bf16[2,200,512]{2,1,0:T(8,128)(2,1)S(1)}, bf16[2,200,512]{2,1,0:T(8,128)(2,1)S(1)}, u32[]{:S(2)}, u32[]{:S(2)}) collective-permute-start(bf16[2,200,512]{2,1,0:T(8,128)(2,1)S(1)} %passed.1), channel_id=1, source_target_pairs={{1,2},{2,1},{5,6},{6,5},{9,10},{10,9},{13,14},{14,13},{17,18},{18,... | collective-permute-start | bytes 1228808 | tf_op jit(solution)/shard_map/ppermute | solution.py:369
  52.2 9.4 %collective-permute-done.9.outer_ref = bf16[2,200,512]{2,1,0:T(8,128)(2,1)S(1)} collective-permute-done((bf16[2,200,512]{2,1,0:T(8,128)(2,1)S(1)}, bf16[2,200,512]{2,1,0:T(8,128)(2,1)S(1)}, u32[]{:S(2)}, u32[]{:S(2)}) %collective-permute-start.9) | collective-permute-done | bytes 409632 | tf_op jit(solution)/shard_map/ppermute | solution.py:369
  61.6 2.4 %side.1.side_ref = bf16[2,200,512]{2,1,0:T(8,128)(2,1)S(1)} custom-call(s32[1,1]{1,0:T(1,128)S(6)} %copy.10.filled_ref.refs_0_, bf16[192,1024]{1,0:T(8,128)(2,1)S(1)} %collective-permute-done.2.query_ref, bf16[384,1024]{1,0:T(8,128)(2,1)S(1)} %bitcast.16, bf16[384,1024]{1,0:T(8,128)(2,1)S(1)} %bitcast.22), custom_call_target="tpu_custom_call" | custom-call | flops 1 | bytes 1 | tf_op jit(solution)/shard_map/side/pallas_call | solution.py:376
  64.1 0.0 copy-start.8
  64.1 2.6 %middle.1.middle_ref = bf16[2,200,512]{2,1,0:T(8,128)(2,1)S(1)} custom-call(s32[1,1]{1,0:T(1,128)S(6)} %copy.10.filled_ref.refs_0_, bf16[192,1024]{1,0:T(8,128)(2,1)S(1)} %collective-permute-done.1.refs_1_, bf16[384,1024]{1,0:T(8,128)(2,1)S(1)} %bitcast.17, bf16[384,1024]{1,0:T(8,128)(2,1)S(1)} %bitcast.23), custom_call_target="tpu_custom_call" | custom-call | flops 1 | bytes 1 | tf_op jit(solution)/shard_map/middle/pallas_call | solution.py:376
  66.7 0.0 collective-permute-done.10.inner_ref
  66.7 1.5 %join.1 = (bf16[2,200,512]{2,1,0:T(8,128)(2,1)S(1)}, bf16[2,200,512]{2,1,0:T(8,128)(2,1)S(1)}) custom-call(bf16[2,200,512]{2,1,0:T(8,128)(2,1)S(1)} %middle.1.middle_ref, bf16[2,200,512]{2,1,0:T(8,128)(2,1)S(1)} %collective-permute-done.9.outer_ref, bf16[2,200,512]{2,1,0:T(8,128)(2,1)S(1)} %side.1.side_ref, ...), custom_call_target="tpu_custom_call" | custom-call | flops 1 | bytes 1 | tf_op jit(solution)/shard_map/join/pallas_call | solution.py:412
  68.3 3.0 %collective-permute-start.14 = (bf16[2,200,512]{2,1,0:T(8,128)(2,1)S(1)}, bf16[2,200,512]{2,1,0:T(8,128)(2,1)S(1)}, u32[]{:S(2)}, u32[]{:S(2)}) collective-permute-start(bf16[2,200,512]{2,1,0:T(8,128)(2,1)S(1)} %get-tuple-element.27), channel_id=1, source_target_pairs={{1,2},{2,1},{5,6},{6,5},{9,10},{10,9},{13,14},{14,13},{17,18},{18,... | collective-permute-start | bytes 1228808 | tf_op jit(solution)/shard_map/ppermute | solution.py:369
  71.3 0.1 collective-permute-start.13
  71.4 0.0 collective-permute-done.12.refs_3_
  71.4 0.0 copy-done.5
  71.4 0.0 copy-done.7
  71.5 4.9 %spans.1 = bf16[192,1024]{1,0:T(8,128)(2,1)} custom-call(s32[16]{0:T(128)S(1)} %copy-done.8, s32[2,12]{1,0:T(2,128)S(1)} %bitcast.29, bf16[192,1024]{1,0:T(8,128)(2,1)S(1)} %bitcast.24, bf16[2,64,2048]{2,1,0:T(8,128)(2,1)S(1)} %copy-done.4, bf16[2,64,2048]{2,1,0:T(8,128)(2,1)S(1)} %collective-permute-done.refs_1_, ...), custom_call_target="tpu_custom_call" | custom-call | flops 1 | bytes 1 | tf_op jit(solution)/shard_map/spans/pallas_call | solution.py:418
  76.4 4.9 %collective-permute-done.14.middle_ref = bf16[2,200,512]{2,1,0:T(8,128)(2,1)S(1)} collective-permute-done((bf16[2,200,512]{2,1,0:T(8,128)(2,1)S(1)}, bf16[2,200,512]{2,1,0:T(8,128)(2,1)S(1)}, u32[]{:S(2)}, u32[]{:S(2)}) %collective-permute-start.14) | collective-permute-done | bytes 409632 | tf_op jit(solution)/shard_map/ppermute | solution.py:369
  81.3 1.0 %collective-permute-done.13.side_ref = bf16[2,200,512]{2,1,0:T(8,128)(2,1)S(1)} collective-permute-done((bf16[2,200,512]{2,1,0:T(8,128)(2,1)S(1)}, bf16[2,200,512]{2,1,0:T(8,128)(2,1)S(1)}, u32[]{:S(2)}, u32[]{:S(2)}) %collective-permute-start.13) | collective-permute-done | bytes 409632 | tf_op jit(solution)/shard_map/ppermute | solution.py:369
  82.2 1.7 %closing.1 = bf16[192,1024]{1,0:T(8,128)(2,1)} custom-call(bf16[2,200,512]{2,1,0:T(8,128)(2,1)S(1)} %own.1.own_ref, bf16[2,200,512]{2,1,0:T(8,128)(2,1)S(1)} %collective-permute-done.13.side_ref, bf16[2,200,512]{2,1,0:T(8,128)(2,1)S(1)} %collective-permute-done.14.middle_ref), custom_call_target="tpu_custom_call" | custom-call | flops 1 | bytes 1 | tf_op jit(solution)/shard_map/closing/pallas_call | solution.py:425
  (10 shorter events, 0.0 us)
Async XLA Ops:
  0.6 2.2 %collective-permute-start = (bf16[2,64,2048]{2,1,0:T(8,128)(2,1)}, bf16[2,64,2048]{2,1,0:T(8,128)(2,1)S(1)}, u32[]{:S(2)}, u32[]{:S(2)}) collective-permute-start(bf16[2,64,2048]{2,1,0:T(8,128)(2,1)} %refs_0_.4), channel_id=1, source_target_pairs={{0,4},{4,0},{8,12},{12,8},{16,20},{20,16},{24,28},{28,24},{1,5},{5... | collective-permute-start | bytes 1572872 | tf_op jit(solution)/shard_map/ppermute | solution.py:373
  2.8 26.2 %collective-permute-start.7 = (bf16[2,64,2048]{2,1,0:T(8,128)(2,1)}, bf16[2,64,2048]{2,1,0:T(8,128)(2,1)S(1)}, u32[]{:S(2)}, u32[]{:S(2)}) collective-permute-start(bf16[2,64,2048]{2,1,0:T(8,128)(2,1)} %refs_0_.4), channel_id=1, source_target_pairs={{0,16},{4,20},{8,24},{12,28},{16,0},{20,4},{24,8},{28,12},{1,17},{... | collective-permute-start | bytes 1572872 | tf_op jit(solution)/shard_map/ppermute | solution.py:373
  4.3 24.7 %collective-permute-start.6 = (bf16[2,64,2048]{2,1,0:T(8,128)(2,1)}, bf16[2,64,2048]{2,1,0:T(8,128)(2,1)S(1)}, u32[]{:S(2)}, u32[]{:S(2)}) collective-permute-start(bf16[2,64,2048]{2,1,0:T(8,128)(2,1)} %refs_0_.4), channel_id=1, source_target_pairs={{0,8},{4,12},{8,0},{12,4},{16,24},{20,28},{24,16},{28,20},{1,9},{5... | collective-permute-start | bytes 1572872 | tf_op jit(solution)/shard_map/ppermute | solution.py:373
  5.8 14.3 %collective-permute-start.5 = (bf16[192,1024]{1,0:T(8,128)(2,1)}, bf16[192,1024]{1,0:T(8,128)(2,1)S(1)}, u32[]{:S(2)}, u32[]{:S(2)}) collective-permute-start(bf16[192,1024]{1,0:T(8,128)(2,1)} %bitcast.25), channel_id=1, source_target_pairs={{0,3},{3,0},{4,7},{7,4},{8,11},{11,8},{12,15},{15,12},{16,19},{19,... | collective-permute-start | bytes 1179656 | tf_op jit(solution)/shard_map/ppermute | solution.py:369
  6.5 22.5 %collective-permute-start.2 = (bf16[192,1024]{1,0:T(8,128)(2,1)}, bf16[192,1024]{1,0:T(8,128)(2,1)S(1)}, u32[]{:S(2)}, u32[]{:S(2)}) collective-permute-start(bf16[192,1024]{1,0:T(8,128)(2,1)} %bitcast.26), channel_id=1, source_target_pairs={{0,1},{1,0},{2,3},{3,2},{4,5},{5,4},{6,7},{7,6},{8,9},{9,8},{10,11... | collective-permute-start | bytes 1179656 | tf_op jit(solution)/shard_map/ppermute | solution.py:369
  11.8 17.2 %collective-permute-start.1 = (bf16[192,1024]{1,0:T(8,128)(2,1)}, bf16[192,1024]{1,0:T(8,128)(2,1)S(1)}, u32[]{:S(2)}, u32[]{:S(2)}) collective-permute-start(bf16[192,1024]{1,0:T(8,128)(2,1)} %bitcast.27), channel_id=1, source_target_pairs={{1,2},{2,1},{5,6},{6,5},{9,10},{10,9},{13,14},{14,13},{17,18},{18,... | collective-permute-start | bytes 1179656 | tf_op jit(solution)/shard_map/ppermute | solution.py:369
  14.4 1.1 %copy-start = (bf16[1,384,1024]{2,1,0:T(8,128)(2,1)S(1)}, bf16[1,384,1024]{2,1,0:T(8,128)(2,1)}, u32[]{:S(2)}) copy-start(bf16[1,384,1024]{2,1,0:T(8,128)(2,1)} %param.9) | copy-start | bytes 2359300
  15.5 1.1 %copy-start.2 = (bf16[1,384,1024]{2,1,0:T(8,128)(2,1)S(1)}, bf16[1,384,1024]{2,1,0:T(8,128)(2,1)}, u32[]{:S(2)}) copy-start(bf16[1,384,1024]{2,1,0:T(8,128)(2,1)} %param.10) | copy-start | bytes 2359300
  16.7 1.0 %copy-start.6 = (bf16[1,192,1024]{2,1,0:T(8,128)(2,1)S(1)}, bf16[1,192,1024]{2,1,0:T(8,128)(2,1)}, u32[]{:S(2)}) copy-start(bf16[1,192,1024]{2,1,0:T(8,128)(2,1)} %param.8) | copy-start | bytes 1179652
  17.7 11.4 %copy-start.1 = (bf16[1,384,1024]{2,1,0:T(8,128)(2,1)S(1)}, bf16[1,384,1024]{2,1,0:T(8,128)(2,1)}, u32[]{:S(2)}) copy-start(bf16[1,384,1024]{2,1,0:T(8,128)(2,1)} %param.9) | copy-start | bytes 2359300
  17.7 11.4 %copy-start.3 = (bf16[1,384,1024]{2,1,0:T(8,128)(2,1)S(1)}, bf16[1,384,1024]{2,1,0:T(8,128)(2,1)}, u32[]{:S(2)}) copy-start(bf16[1,384,1024]{2,1,0:T(8,128)(2,1)} %param.10) | copy-start | bytes 2359300
  20.1 9.0 %copy-start.4 = (bf16[2,64,2048]{2,1,0:T(8,128)(2,1)S(1)}, bf16[2,64,2048]{2,1,0:T(8,128)(2,1)}, u32[]{:S(2)}) copy-start(bf16[2,64,2048]{2,1,0:T(8,128)(2,1)} %refs_0_.4) | copy-start | bytes 1572868
  29.1 18.5 %collective-permute-start.11 = (bf16[2,64,2048]{2,1,0:T(8,128)(2,1)S(1)}, bf16[2,64,2048]{2,1,0:T(8,128)(2,1)S(1)}, u32[]{:S(2)}, u32[]{:S(2)}) collective-permute-start(bf16[2,64,2048]{2,1,0:T(8,128)(2,1)S(1)} %copy-done.4), channel_id=1, source_target_pairs={{0,24},{4,28},{8,16},{12,20},{16,8},{20,12},{24,0},{28,4},{1,25},{... | collective-permute-start | bytes 1572872 | tf_op jit(solution)/shard_map/ppermute | solution.py:373
  29.7 14.8 %collective-permute-start.8 = (bf16[2,200,512]{2,1,0:T(8,128)(2,1)S(1)}, bf16[2,200,512]{2,1,0:T(8,128)(2,1)S(1)}, u32[]{:S(2)}, u32[]{:S(2)}) collective-permute-start(bf16[2,200,512]{2,1,0:T(8,128)(2,1)S(1)} %far.1), channel_id=1, source_target_pairs={{0,1},{3,2},{4,5},{7,6},{8,9},{11,10},{12,13},{15,14},{16,17},{19,... | collective-permute-start | bytes 1228808 | tf_op jit(solution)/shard_map/ppermute | solution.py:369
  31.0 12.3 %collective-permute-start.3 = (bf16[192,1024]{1,0:T(8,128)(2,1)S(1)}, bf16[192,1024]{1,0:T(8,128)(2,1)S(1)}, u32[]{:S(2)}, u32[]{:S(2)}) collective-permute-start(bf16[192,1024]{1,0:T(8,128)(2,1)S(1)} %collective-permute-done.2.query_ref), channel_id=1, source_target_pairs={{1,2},{2,1},{5,6},{6,5},{9,10},{10,9},{13,14},{14,13},{17,18},{18,... | collective-permute-start | bytes 1179656 | tf_op jit(solution)/shard_map/ppermute | solution.py:369
  34.3 10.2 %collective-permute-start.4 = (bf16[192,1024]{1,0:T(8,128)(2,1)S(1)}, bf16[192,1024]{1,0:T(8,128)(2,1)S(1)}, u32[]{:S(2)}, u32[]{:S(2)}) collective-permute-start(bf16[192,1024]{1,0:T(8,128)(2,1)S(1)} %collective-permute-done.1.refs_1_), channel_id=1, source_target_pairs={{1,0},{2,3},{5,4},{6,7},{9,8},{10,11},{13,12},{14,15},{17,16},{18,... | collective-permute-start | bytes 1179656 | tf_op jit(solution)/shard_map/ppermute | solution.py:369
  47.8 23.6 %collective-permute-start.12 = (bf16[3,2,64,2048]{3,2,1,0:T(8,128)(2,1)S(1)}, bf16[3,2,64,2048]{3,2,1,0:T(8,128)(2,1)S(1)}, u32[]{:S(2)}, u32[]{:S(2)}) collective-permute-start(bf16[3,2,64,2048]{3,2,1,0:T(8,128)(2,1)S(1)} %pad_maximum_fusion.refs_2_), channel_id=1, source_target_pairs={{0,4},{4,0},{8,12},{12,8},{16,20},{20,16},{24,28},{28,24},{1,5},{5... | collective-permute-start | bytes 4718600 | tf_op jit(solution)/shard_map/ppermute | solution.py:373
  47.9 13.7 %collective-permute-start.9 = (bf16[2,200,512]{2,1,0:T(8,128)(2,1)S(1)}, bf16[2,200,512]{2,1,0:T(8,128)(2,1)S(1)}, u32[]{:S(2)}, u32[]{:S(2)}) collective-permute-start(bf16[2,200,512]{2,1,0:T(8,128)(2,1)S(1)} %turned.1), channel_id=1, source_target_pairs={{0,1},{3,2},{4,5},{7,6},{8,9},{11,10},{12,13},{15,14},{16,17},{19,... | collective-permute-start | bytes 1228808 | tf_op jit(solution)/shard_map/ppermute | solution.py:369
  49.2 17.6 %collective-permute-start.10 = (bf16[2,200,512]{2,1,0:T(8,128)(2,1)S(1)}, bf16[2,200,512]{2,1,0:T(8,128)(2,1)S(1)}, u32[]{:S(2)}, u32[]{:S(2)}) collective-permute-start(bf16[2,200,512]{2,1,0:T(8,128)(2,1)S(1)} %passed.1), channel_id=1, source_target_pairs={{1,2},{2,1},{5,6},{6,5},{9,10},{10,9},{13,14},{14,13},{17,18},{18,... | collective-permute-start | bytes 1228808 | tf_op jit(solution)/shard_map/ppermute | solution.py:369
  64.1 7.4 %copy-start.5 = (bf16[1,192,1024]{2,1,0:T(8,128)(2,1)S(1)}, bf16[1,192,1024]{2,1,0:T(8,128)(2,1)}, u32[]{:S(2)}) copy-start(bf16[1,192,1024]{2,1,0:T(8,128)(2,1)} %param.12) | copy-start | bytes 1179652
  64.1 7.4 %copy-start.7 = (s32[1,12,2]{1,2,0:T(2,128)S(1)}, s32[1,12,2]{1,2,0:T(2,128)}, u32[]{:S(2)}) copy-start(s32[1,12,2]{1,2,0:T(2,128)} %param.15) | copy-start | bytes 292
  64.1 7.4 %copy-start.8 = (s32[16]{0:T(128)S(1)}, s32[16]{0:T(128)}, u32[]{:S(2)}) copy-start(s32[16]{0:T(128)} %home_ref.1) | copy-start | bytes 196
  68.3 13.0 %collective-permute-start.14 = (bf16[2,200,512]{2,1,0:T(8,128)(2,1)S(1)}, bf16[2,200,512]{2,1,0:T(8,128)(2,1)S(1)}, u32[]{:S(2)}, u32[]{:S(2)}) collective-permute-start(bf16[2,200,512]{2,1,0:T(8,128)(2,1)S(1)} %get-tuple-element.27), channel_id=1, source_target_pairs={{1,2},{2,1},{5,6},{6,5},{9,10},{10,9},{13,14},{14,13},{17,18},{18,... | collective-permute-start | bytes 1228808 | tf_op jit(solution)/shard_map/ppermute | solution.py:369
  71.3 10.9 %collective-permute-start.13 = (bf16[2,200,512]{2,1,0:T(8,128)(2,1)S(1)}, bf16[2,200,512]{2,1,0:T(8,128)(2,1)S(1)}, u32[]{:S(2)}, u32[]{:S(2)}) collective-permute-start(bf16[2,200,512]{2,1,0:T(8,128)(2,1)S(1)} %get-tuple-element.22), channel_id=1, source_target_pairs={{0,1},{1,0},{2,3},{3,2},{4,5},{5,4},{6,7},{7,6},{8,9},{9,8},{10,11... | collective-permute-start | bytes 1228808 | tf_op jit(solution)/shard_map/ppermute | solution.py:369

commit v3 on v2

--- a/solution.py
+++ b/solution.py
@@ -252,12 +252,11 @@
         whole_kernel(*refs)
 
 
-def passed_kernel(filled_ref, query_ref, key_ref, value_ref, other_ref, out_ref, own_ref):
+def meet_kernel(own_ref, other_ref, out_ref):
     @when_inner
     def _():
         for half in range(2):
-            attend(query_ref, key_ref, value_ref, filled_ref, half, own_ref)
-            merge((own_ref, other_ref.at[half]), out_ref.at[half], 0, out_ref.at[half])
+            merge((own_ref.at[half], other_ref.at[half]), out_ref.at[half], 0, out_ref.at[half])
 
 
 def join_kernel(middle_ref, outer_ref, side_ref, inner_ref, to_middle_ref, to_side_ref):
@@ -382,38 +381,31 @@
     outward = ((1, 0), (2, 3))
 
     far = over_blk(queries, *swap_far)
-    core_c = over_bank(bank_kv, 1)
-    near = after(queries, core_c)
-    side = over_blk(near, *swap_side)
-    middle = over_blk(near, *swap_middle)
-    near_bank = after(bank_kv, core_c)
-    bank_x = over_bank(near_bank, 2)
-    bank_y = over_bank(near_bank, 4)
-    own = attention(whole_kernel, "own", near)
-    passed_in = over_blk(side, *swap_middle)
-    passed_out = over_blk(middle, *outward)
-    far_part = attention(outer_kernel, "far", after(far, own, side, middle, bank_x, bank_y))
+    side = over_blk(queries, *swap_side)
+    middle = over_blk(queries, *swap_middle)
+    own = attention(whole_kernel, "own", queries)
+    far_part = attention(outer_kernel, "far", after(far, own))
     far_sent = over_blk(far_part, *inward)
+    passed_in = over_blk(after(side, far_part), *swap_middle)
+    passed_out = over_blk(after(middle, far_part), *outward)
+    bank_x = over_bank(after(bank_kv, far_part), 2)
+    bank_y = over_bank(after(bank_kv, far_part), 4)
     turned = attention(outer_kernel, "turned", after(passed_out, passed_in))
-    bank_xy = over_bank(after(bank_kv, far_part), 6)
     from_outer = over_blk(turned, *inward)
-    met = on_core(
-        passed_kernel,
-        whole_part,
-        [SMALL] + [WHOLE] * 4,
-        scratch=(pltpu.VMEM(whole_part.shape[1:], whole_part.dtype),),
-        name="passed",
-    )(filled, after(passed_in, turned), keys, values, far_sent)
+    passed = attention(inner_kernel, "passed", after(passed_in, turned))
+    met = on_core(meet_kernel, whole_part, [WHOLE] * 2, name="met")(passed, far_sent)
     from_middle = over_blk(met, *swap_middle)
-    others = after(jnp.stack((bank_x, bank_y, bank_xy)), met)
-    core_others = over_bank(others, 1)
-    side_part = attention(whole_kernel, "side", after(side, met, from_outer))
+    side_part = attention(whole_kernel, "side", after(side, met))
     middle_part = attention(inner_kernel, "middle", after(middle, side_part))
+    bank_xy = over_bank(after(bank_kv, met, bank_x, bank_y), 6)
+    core_c = over_bank(after(bank_kv, met), 1)
     to_middle, to_side = on_core(join_kernel, (whole_part, whole_part), [WHOLE] * 4, name="join")(
         middle_part, from_outer, side_part, from_middle
     )
     home_middle = over_blk(to_middle, *swap_middle)
     home_side = over_blk(to_side, *swap_side)
+    others = after(jnp.stack((bank_x, bank_y, bank_xy)), to_side)
+    core_others = over_bank(others, 1)
 
     retrieved = on_core(
         spans_kernel,

time: 85.3 us -> 70.9 us (0.83); the launches traced: 83.9 us -> 70.4 us
  waiting for transfers between devices: 34.5 us -> 20.6 us
  local copies, waits for them, and re-layouts: 3.28 us -> 4.28 us
    ppermute x10, waiting for transfers between devices: 32.4 us -> 19.6 us  [over_blk(): return lax.ppermute(block, 'blk', route)]
    ppermute x10, starting transfers between devices: 21.9 us -> 19.1 us  [over_blk(): return lax.ppermute(block, 'blk', route)]
    ppermute x5, starting transfers between devices: 3.7 us -> 6.09 us  [over_bank(): return lax.ppermute(block, 'bank', route)]
    pallas_call x1, Pallas kernels: 3.14 us -> 0.82 us  [joint_pass(): on_core(meet_kernel, whole_part, [WHOLE] * 2, name='met')(passed, far_sent)]
    pallas_call x5 -> x6, Pallas kernels: 7.53 us -> 9.75 us  [attention(): on_core(kernel, whole_part, [SMALL] + [WHOLE] * 3, name=name)]
    ppermute x5, waiting for transfers between devices: 2.12 us -> 1.01 us  [over_bank(): return lax.ppermute(block, 'bank', route)]
    unnamed x18, local copies, waits for them, and re-layouts: 3.28 us -> 4.28 us
  transfers between devices with their start and end apart: 15 -> 15, of which waited for: 7 -> 7; matrix products, arithmetic and copies ran while one was open for 0% -> 0% of each run, Pallas kernels for 20% -> 24%
where the time goes in v3:
time: 70.9 us; the launch traced here: 70.4 us
  starting transfers between devices  25.2 us (36%)
  waiting for transfers between devices  20.6 us (29%)
  Pallas kernels  18.7 us (26%)
  local copies, waits for them, and re-layouts  4.28 us (6%)
  between operations  1.5 us (2%)
    ppermute x10, waiting for transfers between devices, over_blk(): return lax.ppermute(block, 'blk', route)  19.6 us
    ppermute x10, starting transfers between devices, over_blk(): return lax.ppermute(block, 'blk', route)  19.1 us
    pallas_call x6, Pallas kernels, attention(): on_core(kernel, whole_part, [SMALL] + [WHOLE] * 3, name=name)  9.75 us
    ppermute x5, starting transfers between devices, over_bank(): return lax.ppermute(block, 'bank', route)  6.09 us
    pallas_call x1, Pallas kernels, joint_pass(): on_core(spans_kernel, plain, [SMALL, SMALL, WHOLE] + [AWAY] * 4, scratch=...  4.88 us
    unnamed x18, local copies, waits for them, and re-layouts  4.28 us
    pallas_call x1, Pallas kernels, joint_pass(): on_core(closing_kernel, plain, [WHOLE] * 3, name='closing')  1.69 us
    pallas_call x1, Pallas kernels, joint_pass(): on_core(join_kernel, (whole_part, whole_part), [WHOLE] * 4, name='join')  1.53 us
  transfers between devices with their start and end apart: 15, of which 7 were waited for; matrix products, arithmetic and copies ran while one was open for 0% of the time, Pallas kernels for 24%

profile of v3, /device:TPU:8, one launch (start us, length us, event | category | flops | bytes accessed | tf_op | source)
XLA Modules:
  0.0 70.4 jit_solution(444460573370813561)
XLA Ops:
  0.6 0.7 collective-permute-start.2
  1.3 5.3 %collective-permute-start.1 = (bf16[192,1024]{1,0:T(8,128)(2,1)}, bf16[192,1024]{1,0:T(8,128)(2,1)S(1)}, u32[]{:S(2)}, u32[]{:S(2)}) collective-permute-start(bf16[192,1024]{1,0:T(8,128)(2,1)} %bitcast.26), channel_id=1, source_target_pairs={{0,1},{1,0},{2,3},{3,2},{4,5},{5,4},{6,7},{7,6},{8,9},{9,8},{10,11... | collective-permute-start | bytes 1179656 | tf_op jit(solution)/shard_map/ppermute | solution.py:368
  6.7 1.9 %collective-permute-start = (bf16[192,1024]{1,0:T(8,128)(2,1)}, bf16[192,1024]{1,0:T(8,128)(2,1)S(1)}, u32[]{:S(2)}, u32[]{:S(2)}) collective-permute-start(bf16[192,1024]{1,0:T(8,128)(2,1)} %bitcast.27), channel_id=1, source_target_pairs={{1,2},{2,1},{5,6},{6,5},{9,10},{10,9},{13,14},{14,13},{17,18},{18,... | collective-permute-start | bytes 1179656 | tf_op jit(solution)/shard_map/ppermute | solution.py:368
  9.2 0.0 copy-start
  9.2 1.1 %copy-done = bf16[1,384,1024]{2,1,0:T(8,128)(2,1)S(1)} copy-done((bf16[1,384,1024]{2,1,0:T(8,128)(2,1)S(1)}, bf16[1,384,1024]{2,1,0:T(8,128)(2,1)}, u32[]{:S(2)}) %copy-start) | copy-done | bytes 786456
  10.4 1.1 %copy-done.2 = bf16[1,384,1024]{2,1,0:T(8,128)(2,1)S(1)} copy-done((bf16[1,384,1024]{2,1,0:T(8,128)(2,1)S(1)}, bf16[1,384,1024]{2,1,0:T(8,128)(2,1)}, u32[]{:S(2)}) %copy-start.2) | copy-done | bytes 786456
  11.5 1.0 %copy-done.6 = bf16[1,192,1024]{2,1,0:T(8,128)(2,1)S(1)} copy-done((bf16[1,192,1024]{2,1,0:T(8,128)(2,1)S(1)}, bf16[1,192,1024]{2,1,0:T(8,128)(2,1)}, u32[]{:S(2)}) %copy-start.6) | copy-done | bytes 393240
  12.5 2.4 %own.1.own_ref = bf16[2,200,512]{2,1,0:T(8,128)(2,1)S(1)} custom-call(s32[1,1]{1,0:T(1,128)S(6)} %copy.10.filled_ref.refs_0_, bf16[192,1024]{1,0:T(8,128)(2,1)S(1)} %bitcast.28, bf16[384,1024]{1,0:T(8,128)(2,1)S(1)} %bitcast.12, bf16[384,1024]{1,0:T(8,128)(2,1)S(1)} %bitcast.18), custom_call_target="tpu_custom_call" | custom-call | flops 1 | bytes 1 | tf_op jit(solution)/shard_map/own/pallas_call | solution.py:375
  14.9 0.0 collective-permute-done.2.refs_1_
  15.0 1.0 %copy-done.4 = bf16[2,64,2048]{2,1,0:T(8,128)(2,1)S(1)} copy-done((bf16[2,64,2048]{2,1,0:T(8,128)(2,1)S(1)}, bf16[2,64,2048]{2,1,0:T(8,128)(2,1)}, u32[]{:S(2)}) %copy-start.4) | copy-done | bytes 524312
  16.0 1.5 %collective-permute-start.10 = (bf16[2,64,2048]{2,1,0:T(8,128)(2,1)S(1)}, bf16[2,64,2048]{2,1,0:T(8,128)(2,1)S(1)}, u32[]{:S(2)}, u32[]{:S(2)}) collective-permute-start(bf16[2,64,2048]{2,1,0:T(8,128)(2,1)S(1)} %copy-done.4), channel_id=1, source_target_pairs={{0,16},{4,20},{8,24},{12,28},{16,0},{20,4},{24,8},{28,12},{1,17},{... | collective-permute-start | bytes 1572872 | tf_op jit(solution)/shard_map/ppermute | solution.py:372
  17.5 1.5 %collective-permute-start.9 = (bf16[2,64,2048]{2,1,0:T(8,128)(2,1)S(1)}, bf16[2,64,2048]{2,1,0:T(8,128)(2,1)S(1)}, u32[]{:S(2)}, u32[]{:S(2)}) collective-permute-start(bf16[2,64,2048]{2,1,0:T(8,128)(2,1)S(1)} %copy-done.4), channel_id=1, source_target_pairs={{0,8},{4,12},{8,0},{12,4},{16,24},{20,28},{24,16},{28,20},{1,9},{5... | collective-permute-start | bytes 1572872 | tf_op jit(solution)/shard_map/ppermute | solution.py:372
  19.0 1.3 %collective-permute-start.5 = (bf16[2,200,512]{2,1,0:T(8,128)(2,1)S(1)}, bf16[2,200,512]{2,1,0:T(8,128)(2,1)S(1)}, u32[]{:S(2)}, u32[]{:S(2)}) collective-permute-start(bf16[2,200,512]{2,1,0:T(8,128)(2,1)S(1)} %far.1), channel_id=1, source_target_pairs={{0,1},{3,2},{4,5},{7,6},{8,9},{11,10},{12,13},{15,14},{16,17},{19,... | collective-permute-start | bytes 1228808 | tf_op jit(solution)/shard_map/ppermute | solution.py:368
  20.3 5.0 %collective-permute-done.1.query_ref = bf16[192,1024]{1,0:T(8,128)(2,1)S(1)} collective-permute-done((bf16[192,1024]{1,0:T(8,128)(2,1)}, bf16[192,1024]{1,0:T(8,128)(2,1)S(1)}, u32[]{:S(2)}, u32[]{:S(2)}) %collective-permute-start.1) | collective-permute-done | bytes 393248 | tf_op jit(solution)/shard_map/ppermute | solution.py:368
  25.3 1.9 %collective-permute-start.3 = (bf16[192,1024]{1,0:T(8,128)(2,1)S(1)}, bf16[192,1024]{1,0:T(8,128)(2,1)S(1)}, u32[]{:S(2)}, u32[]{:S(2)}) collective-permute-start(bf16[192,1024]{1,0:T(8,128)(2,1)S(1)} %collective-permute-done.1.query_ref), channel_id=1, source_target_pairs={{1,2},{2,1},{5,6},{6,5},{9,10},{10,9},{13,14},{14,13},{17,18},{18,... | collective-permute-start | bytes 1179656 | tf_op jit(solution)/shard_map/ppermute | solution.py:368
  27.2 0.0 collective-permute-done.refs_1_
  27.2 1.3 %collective-permute-start.4 = (bf16[192,1024]{1,0:T(8,128)(2,1)S(1)}, bf16[192,1024]{1,0:T(8,128)(2,1)S(1)}, u32[]{:S(2)}, u32[]{:S(2)}) collective-permute-start(bf16[192,1024]{1,0:T(8,128)(2,1)S(1)} %collective-permute-done.refs_1_), channel_id=1, source_target_pairs={{1,0},{2,3},{5,4},{6,7},{9,8},{10,11},{13,12},{14,15},{17,16},{18,... | collective-permute-start | bytes 1179656 | tf_op jit(solution)/shard_map/ppermute | solution.py:368
  28.5 7.5 %collective-permute-done.3.refs_1_ = bf16[192,1024]{1,0:T(8,128)(2,1)S(1)} collective-permute-done((bf16[192,1024]{1,0:T(8,128)(2,1)S(1)}, bf16[192,1024]{1,0:T(8,128)(2,1)S(1)}, u32[]{:S(2)}, u32[]{:S(2)}) %collective-permute-start.3) | collective-permute-done | bytes 393248 | tf_op jit(solution)/shard_map/ppermute | solution.py:368
  36.0 0.0 collective-permute-done.4.refs_1_
  36.0 2.4 %passed.1.own_ref = bf16[2,200,512]{2,1,0:T(8,128)(2,1)S(1)} custom-call(s32[1,1]{1,0:T(1,128)S(6)} %copy.10.filled_ref.refs_0_, bf16[192,1024]{1,0:T(8,128)(2,1)S(1)} %collective-permute-done.3.refs_1_, bf16[384,1024]{1,0:T(8,128)(2,1)S(1)} %bitcast.15, bf16[384,1024]{1,0:T(8,128)(2,1)S(1)} %bitcast.21), custom_call_target="tpu_custom_call" | custom-call | flops 1 | bytes 1 | tf_op jit(solution)/shard_map/passed/pallas_call | solution.py:375
  38.4 0.0 collective-permute-done.5.other_ref
  38.4 0.8 %met.1 = bf16[2,200,512]{2,1,0:T(8,128)(2,1)S(1)} custom-call(bf16[2,200,512]{2,1,0:T(8,128)(2,1)S(1)} %passed.1.own_ref, bf16[2,200,512]{2,1,0:T(8,128)(2,1)S(1)} %collective-permute-done.5.other_ref), custom_call_target="tpu_custom_call" | custom-call | flops 1 | bytes 1 | tf_op jit(solution)/shard_map/met/pallas_call | solution.py:396
  39.3 0.0 collective-permute-done.10
  39.3 0.0 collective-permute-done.9
  39.3 2.5 %collective-permute-start.11 = (bf16[2,64,2048]{2,1,0:T(8,128)(2,1)S(1)}, bf16[2,64,2048]{2,1,0:T(8,128)(2,1)S(1)}, u32[]{:S(2)}, u32[]{:S(2)}) collective-permute-start(bf16[2,64,2048]{2,1,0:T(8,128)(2,1)S(1)} %copy-done.4), channel_id=1, source_target_pairs={{0,24},{4,28},{8,16},{12,20},{16,8},{20,12},{24,0},{28,4},{1,25},{... | collective-permute-start | bytes 1572872 | tf_op jit(solution)/shard_map/ppermute | solution.py:372
  41.8 1.3 %collective-permute-start.6 = (bf16[2,200,512]{2,1,0:T(8,128)(2,1)S(1)}, bf16[2,200,512]{2,1,0:T(8,128)(2,1)S(1)}, u32[]{:S(2)}, u32[]{:S(2)}) collective-permute-start(bf16[2,200,512]{2,1,0:T(8,128)(2,1)S(1)} %turned.1), channel_id=1, source_target_pairs={{0,1},{3,2},{4,5},{7,6},{8,9},{11,10},{12,13},{15,14},{16,17},{19,... | collective-permute-start | bytes 1228808 | tf_op jit(solution)/shard_map/ppermute | solution.py:368
  43.1 2.8 %collective-permute-start.7 = (bf16[2,200,512]{2,1,0:T(8,128)(2,1)S(1)}, bf16[2,200,512]{2,1,0:T(8,128)(2,1)S(1)}, u32[]{:S(2)}, u32[]{:S(2)}) collective-permute-start(bf16[2,200,512]{2,1,0:T(8,128)(2,1)S(1)} %met.1), channel_id=1, source_target_pairs={{1,2},{2,1},{5,6},{6,5},{9,10},{10,9},{13,14},{14,13},{17,18},{18,... | collective-permute-start | bytes 1228808 | tf_op jit(solution)/shard_map/ppermute | solution.py:368
  45.9 2.4 %side.1.side_ref = bf16[2,200,512]{2,1,0:T(8,128)(2,1)S(1)} custom-call(s32[1,1]{1,0:T(1,128)S(6)} %copy.10.filled_ref.refs_0_, bf16[192,1024]{1,0:T(8,128)(2,1)S(1)} %collective-permute-done.1.query_ref, bf16[384,1024]{1,0:T(8,128)(2,1)S(1)} %bitcast.16, bf16[384,1024]{1,0:T(8,128)(2,1)S(1)} %bitcast.22), custom_call_target="tpu_custom_call" | custom-call | flops 1 | bytes 1 | tf_op jit(solution)/shard_map/side/pallas_call | solution.py:375
  48.3 2.4 %middle.1.middle_ref = bf16[2,200,512]{2,1,0:T(8,128)(2,1)S(1)} custom-call(s32[1,1]{1,0:T(1,128)S(6)} %copy.10.filled_ref.refs_0_, bf16[192,1024]{1,0:T(8,128)(2,1)S(1)} %collective-permute-done.refs_1_, bf16[384,1024]{1,0:T(8,128)(2,1)S(1)} %bitcast.17, bf16[384,1024]{1,0:T(8,128)(2,1)S(1)} %bitcast.23), custom_call_target="tpu_custom_call" | custom-call | flops 1 | bytes 1 | tf_op jit(solution)/shard_map/middle/pallas_call | solution.py:375
  50.7 1.0 %collective-permute-done.6.outer_ref = bf16[2,200,512]{2,1,0:T(8,128)(2,1)S(1)} collective-permute-done((bf16[2,200,512]{2,1,0:T(8,128)(2,1)S(1)}, bf16[2,200,512]{2,1,0:T(8,128)(2,1)S(1)}, u32[]{:S(2)}, u32[]{:S(2)}) %collective-permute-start.6) | collective-permute-done | bytes 409632 | tf_op jit(solution)/shard_map/ppermute | solution.py:368
  51.8 1.3 %collective-permute-done.7.inner_ref = bf16[2,200,512]{2,1,0:T(8,128)(2,1)S(1)} collective-permute-done((bf16[2,200,512]{2,1,0:T(8,128)(2,1)S(1)}, bf16[2,200,512]{2,1,0:T(8,128)(2,1)S(1)}, u32[]{:S(2)}, u32[]{:S(2)}) %collective-permute-start.7) | collective-permute-done | bytes 409632 | tf_op jit(solution)/shard_map/ppermute | solution.py:368
  53.1 1.5 %join.1 = (bf16[2,200,512]{2,1,0:T(8,128)(2,1)S(1)}, bf16[2,200,512]{2,1,0:T(8,128)(2,1)S(1)}) custom-call(bf16[2,200,512]{2,1,0:T(8,128)(2,1)S(1)} %middle.1.middle_ref, bf16[2,200,512]{2,1,0:T(8,128)(2,1)S(1)} %collective-permute-done.6.outer_ref, bf16[2,200,512]{2,1,0:T(8,128)(2,1)S(1)} %side.1.side_ref, ...), custom_call_target="tpu_custom_call" | custom-call | flops 1 | bytes 1 | tf_op jit(solution)/shard_map/join/pallas_call | solution.py:402
  54.6 0.0 collective-permute-done.11
  54.6 0.0 copy-start.5
  54.6 0.0 copy-start.7
  54.6 0.0 copy-start.8
  54.7 0.2 pad_maximum_fusion.refs_2_
  54.8 0.1 collective-permute-start.12
  54.9 0.5 collective-permute-start.8
  55.4 0.0 collective-permute-start.13
  55.4 2.6 %collective-permute-start.14 = (bf16[2,200,512]{2,1,0:T(8,128)(2,1)S(1)}, bf16[2,200,512]{2,1,0:T(8,128)(2,1)S(1)}, u32[]{:S(2)}, u32[]{:S(2)}) collective-permute-start(bf16[2,200,512]{2,1,0:T(8,128)(2,1)S(1)} %get-tuple-element.31), channel_id=1, source_target_pairs={{1,2},{2,1},{5,6},{6,5},{9,10},{10,9},{13,14},{14,13},{17,18},{18,... | collective-permute-start | bytes 1228808 | tf_op jit(solution)/shard_map/ppermute | solution.py:368
  58.1 1.0 %collective-permute-done.8.refs_1_ = bf16[2,64,2048]{2,1,0:T(8,128)(2,1)S(1)} collective-permute-done((bf16[2,64,2048]{2,1,0:T(8,128)(2,1)S(1)}, bf16[2,64,2048]{2,1,0:T(8,128)(2,1)S(1)}, u32[]{:S(2)}, u32[]{:S(2)}) %collective-permute-start.8) | collective-permute-done | bytes 524320 | tf_op jit(solution)/shard_map/ppermute | solution.py:372
  59.1 0.0 collective-permute-done.12.refs_3_
  59.1 0.0 copy-done.7
  59.1 4.9 %spans.1 = bf16[192,1024]{1,0:T(8,128)(2,1)} custom-call(s32[16]{0:T(128)S(1)} %copy-done.8, s32[2,12]{1,0:T(2,128)S(1)} %bitcast.29, bf16[192,1024]{1,0:T(8,128)(2,1)S(1)} %bitcast.24, bf16[2,64,2048]{2,1,0:T(8,128)(2,1)S(1)} %copy-done.4, bf16[2,64,2048]{2,1,0:T(8,128)(2,1)S(1)} %collective-permute-done.8.refs_1_, ...), custom_call_target="tpu_custom_call" | custom-call | flops 1 | bytes 1 | tf_op jit(solution)/shard_map/spans/pallas_call | solution.py:410
  64.0 2.9 %collective-permute-done.13.side_ref = bf16[2,200,512]{2,1,0:T(8,128)(2,1)S(1)} collective-permute-done((bf16[2,200,512]{2,1,0:T(8,128)(2,1)S(1)}, bf16[2,200,512]{2,1,0:T(8,128)(2,1)S(1)}, u32[]{:S(2)}, u32[]{:S(2)}) %collective-permute-start.13) | collective-permute-done | bytes 409632 | tf_op jit(solution)/shard_map/ppermute | solution.py:368
  66.9 1.9 %collective-permute-done.14.middle_ref = bf16[2,200,512]{2,1,0:T(8,128)(2,1)S(1)} collective-permute-done((bf16[2,200,512]{2,1,0:T(8,128)(2,1)S(1)}, bf16[2,200,512]{2,1,0:T(8,128)(2,1)S(1)}, u32[]{:S(2)}, u32[]{:S(2)}) %collective-permute-start.14) | collective-permute-done | bytes 409632 | tf_op jit(solution)/shard_map/ppermute | solution.py:368
  68.8 1.7 %closing.1 = bf16[192,1024]{1,0:T(8,128)(2,1)} custom-call(bf16[2,200,512]{2,1,0:T(8,128)(2,1)S(1)} %own.1.own_ref, bf16[2,200,512]{2,1,0:T(8,128)(2,1)S(1)} %collective-permute-done.13.side_ref, bf16[2,200,512]{2,1,0:T(8,128)(2,1)S(1)} %collective-permute-done.14.middle_ref), custom_call_target="tpu_custom_call" | custom-call | flops 1 | bytes 1 | tf_op jit(solution)/shard_map/closing/pallas_call | solution.py:417
  (11 shorter events, 0.0 us)
Async XLA Ops:
  0.6 14.3 %collective-permute-start.2 = (bf16[192,1024]{1,0:T(8,128)(2,1)}, bf16[192,1024]{1,0:T(8,128)(2,1)S(1)}, u32[]{:S(2)}, u32[]{:S(2)}) collective-permute-start(bf16[192,1024]{1,0:T(8,128)(2,1)} %bitcast.25), channel_id=1, source_target_pairs={{0,3},{3,0},{4,7},{7,4},{8,11},{11,8},{12,15},{15,12},{16,19},{19,... | collective-permute-start | bytes 1179656 | tf_op jit(solution)/shard_map/ppermute | solution.py:368
  1.3 24.0 %collective-permute-start.1 = (bf16[192,1024]{1,0:T(8,128)(2,1)}, bf16[192,1024]{1,0:T(8,128)(2,1)S(1)}, u32[]{:S(2)}, u32[]{:S(2)}) collective-permute-start(bf16[192,1024]{1,0:T(8,128)(2,1)} %bitcast.26), channel_id=1, source_target_pairs={{0,1},{1,0},{2,3},{3,2},{4,5},{5,4},{6,7},{7,6},{8,9},{9,8},{10,11... | collective-permute-start | bytes 1179656 | tf_op jit(solution)/shard_map/ppermute | solution.py:368
  6.7 20.5 %collective-permute-start = (bf16[192,1024]{1,0:T(8,128)(2,1)}, bf16[192,1024]{1,0:T(8,128)(2,1)S(1)}, u32[]{:S(2)}, u32[]{:S(2)}) collective-permute-start(bf16[192,1024]{1,0:T(8,128)(2,1)} %bitcast.27), channel_id=1, source_target_pairs={{1,2},{2,1},{5,6},{6,5},{9,10},{10,9},{13,14},{14,13},{17,18},{18,... | collective-permute-start | bytes 1179656 | tf_op jit(solution)/shard_map/ppermute | solution.py:368
  9.2 1.1 %copy-start = (bf16[1,384,1024]{2,1,0:T(8,128)(2,1)S(1)}, bf16[1,384,1024]{2,1,0:T(8,128)(2,1)}, u32[]{:S(2)}) copy-start(bf16[1,384,1024]{2,1,0:T(8,128)(2,1)} %param.9) | copy-start | bytes 2359300
  10.4 1.1 %copy-start.2 = (bf16[1,384,1024]{2,1,0:T(8,128)(2,1)S(1)}, bf16[1,384,1024]{2,1,0:T(8,128)(2,1)}, u32[]{:S(2)}) copy-start(bf16[1,384,1024]{2,1,0:T(8,128)(2,1)} %param.10) | copy-start | bytes 2359300
  11.5 1.0 %copy-start.6 = (bf16[1,192,1024]{2,1,0:T(8,128)(2,1)S(1)}, bf16[1,192,1024]{2,1,0:T(8,128)(2,1)}, u32[]{:S(2)}) copy-start(bf16[1,192,1024]{2,1,0:T(8,128)(2,1)} %param.8) | copy-start | bytes 1179652
  12.5 2.5 %copy-start.1 = (bf16[1,384,1024]{2,1,0:T(8,128)(2,1)S(1)}, bf16[1,384,1024]{2,1,0:T(8,128)(2,1)}, u32[]{:S(2)}) copy-start(bf16[1,384,1024]{2,1,0:T(8,128)(2,1)} %param.9) | copy-start | bytes 2359300
  12.5 2.5 %copy-start.3 = (bf16[1,384,1024]{2,1,0:T(8,128)(2,1)S(1)}, bf16[1,384,1024]{2,1,0:T(8,128)(2,1)}, u32[]{:S(2)}) copy-start(bf16[1,384,1024]{2,1,0:T(8,128)(2,1)} %param.10) | copy-start | bytes 2359300
  14.9 1.1 %copy-start.4 = (bf16[2,64,2048]{2,1,0:T(8,128)(2,1)S(1)}, bf16[2,64,2048]{2,1,0:T(8,128)(2,1)}, u32[]{:S(2)}) copy-start(bf16[2,64,2048]{2,1,0:T(8,128)(2,1)} %refs_0_.5) | copy-start | bytes 1572868
  16.0 23.3 %collective-permute-start.10 = (bf16[2,64,2048]{2,1,0:T(8,128)(2,1)S(1)}, bf16[2,64,2048]{2,1,0:T(8,128)(2,1)S(1)}, u32[]{:S(2)}, u32[]{:S(2)}) collective-permute-start(bf16[2,64,2048]{2,1,0:T(8,128)(2,1)S(1)} %copy-done.4), channel_id=1, source_target_pairs={{0,16},{4,20},{8,24},{12,28},{16,0},{20,4},{24,8},{28,12},{1,17},{... | collective-permute-start | bytes 1572872 | tf_op jit(solution)/shard_map/ppermute | solution.py:372
  17.5 21.8 %collective-permute-start.9 = (bf16[2,64,2048]{2,1,0:T(8,128)(2,1)S(1)}, bf16[2,64,2048]{2,1,0:T(8,128)(2,1)S(1)}, u32[]{:S(2)}, u32[]{:S(2)}) collective-permute-start(bf16[2,64,2048]{2,1,0:T(8,128)(2,1)S(1)} %copy-done.4), channel_id=1, source_target_pairs={{0,8},{4,12},{8,0},{12,4},{16,24},{20,28},{24,16},{28,20},{1,9},{5... | collective-permute-start | bytes 1572872 | tf_op jit(solution)/shard_map/ppermute | solution.py:372
  19.0 19.4 %collective-permute-start.5 = (bf16[2,200,512]{2,1,0:T(8,128)(2,1)S(1)}, bf16[2,200,512]{2,1,0:T(8,128)(2,1)S(1)}, u32[]{:S(2)}, u32[]{:S(2)}) collective-permute-start(bf16[2,200,512]{2,1,0:T(8,128)(2,1)S(1)} %far.1), channel_id=1, source_target_pairs={{0,1},{3,2},{4,5},{7,6},{8,9},{11,10},{12,13},{15,14},{16,17},{19,... | collective-permute-start | bytes 1228808 | tf_op jit(solution)/shard_map/ppermute | solution.py:368
  25.3 10.7 %collective-permute-start.3 = (bf16[192,1024]{1,0:T(8,128)(2,1)S(1)}, bf16[192,1024]{1,0:T(8,128)(2,1)S(1)}, u32[]{:S(2)}, u32[]{:S(2)}) collective-permute-start(bf16[192,1024]{1,0:T(8,128)(2,1)S(1)} %collective-permute-done.1.query_ref), channel_id=1, source_target_pairs={{1,2},{2,1},{5,6},{6,5},{9,10},{10,9},{13,14},{14,13},{17,18},{18,... | collective-permute-start | bytes 1179656 | tf_op jit(solution)/shard_map/ppermute | solution.py:368
  27.2 8.8 %collective-permute-start.4 = (bf16[192,1024]{1,0:T(8,128)(2,1)S(1)}, bf16[192,1024]{1,0:T(8,128)(2,1)S(1)}, u32[]{:S(2)}, u32[]{:S(2)}) collective-permute-start(bf16[192,1024]{1,0:T(8,128)(2,1)S(1)} %collective-permute-done.refs_1_), channel_id=1, source_target_pairs={{1,0},{2,3},{5,4},{6,7},{9,8},{10,11},{13,12},{14,15},{17,16},{18,... | collective-permute-start | bytes 1179656 | tf_op jit(solution)/shard_map/ppermute | solution.py:368
  39.3 15.3 %collective-permute-start.11 = (bf16[2,64,2048]{2,1,0:T(8,128)(2,1)S(1)}, bf16[2,64,2048]{2,1,0:T(8,128)(2,1)S(1)}, u32[]{:S(2)}, u32[]{:S(2)}) collective-permute-start(bf16[2,64,2048]{2,1,0:T(8,128)(2,1)S(1)} %copy-done.4), channel_id=1, source_target_pairs={{0,24},{4,28},{8,16},{12,20},{16,8},{20,12},{24,0},{28,4},{1,25},{... | collective-permute-start | bytes 1572872 | tf_op jit(solution)/shard_map/ppermute | solution.py:372
  41.8 10.0 %collective-permute-start.6 = (bf16[2,200,512]{2,1,0:T(8,128)(2,1)S(1)}, bf16[2,200,512]{2,1,0:T(8,128)(2,1)S(1)}, u32[]{:S(2)}, u32[]{:S(2)}) collective-permute-start(bf16[2,200,512]{2,1,0:T(8,128)(2,1)S(1)} %turned.1), channel_id=1, source_target_pairs={{0,1},{3,2},{4,5},{7,6},{8,9},{11,10},{12,13},{15,14},{16,17},{19,... | collective-permute-start | bytes 1228808 | tf_op jit(solution)/shard_map/ppermute | solution.py:368
  43.1 10.0 %collective-permute-start.7 = (bf16[2,200,512]{2,1,0:T(8,128)(2,1)S(1)}, bf16[2,200,512]{2,1,0:T(8,128)(2,1)S(1)}, u32[]{:S(2)}, u32[]{:S(2)}) collective-permute-start(bf16[2,200,512]{2,1,0:T(8,128)(2,1)S(1)} %met.1), channel_id=1, source_target_pairs={{1,2},{2,1},{5,6},{6,5},{9,10},{10,9},{13,14},{14,13},{17,18},{18,... | collective-permute-start | bytes 1228808 | tf_op jit(solution)/shard_map/ppermute | solution.py:368
  54.6 4.4 %copy-start.5 = (bf16[1,192,1024]{2,1,0:T(8,128)(2,1)S(1)}, bf16[1,192,1024]{2,1,0:T(8,128)(2,1)}, u32[]{:S(2)}) copy-start(bf16[1,192,1024]{2,1,0:T(8,128)(2,1)} %param.12) | copy-start | bytes 1179652
  54.6 4.4 %copy-start.7 = (s32[1,12,2]{1,2,0:T(2,128)S(1)}, s32[1,12,2]{1,2,0:T(2,128)}, u32[]{:S(2)}) copy-start(s32[1,12,2]{1,2,0:T(2,128)} %param.15) | copy-start | bytes 292
  54.6 4.4 %copy-start.8 = (s32[16]{0:T(128)S(1)}, s32[16]{0:T(128)}, u32[]{:S(2)}) copy-start(s32[16]{0:T(128)} %home_ref.1) | copy-start | bytes 196
  54.8 4.2 %collective-permute-start.12 = (bf16[3,2,64,2048]{3,2,1,0:T(8,128)(2,1)S(1)}, bf16[3,2,64,2048]{3,2,1,0:T(8,128)(2,1)S(1)}, u32[]{:S(2)}, u32[]{:S(2)}) collective-permute-start(bf16[3,2,64,2048]{3,2,1,0:T(8,128)(2,1)S(1)} %pad_maximum_fusion.refs_2_), channel_id=1, source_target_pairs={{0,4},{4,0},{8,12},{12,8},{16,20},{20,16},{24,28},{28,24},{1,5},{5... | collective-permute-start | bytes 4718600 | tf_op jit(solution)/shard_map/ppermute | solution.py:372
  54.9 4.1 %collective-permute-start.8 = (bf16[2,64,2048]{2,1,0:T(8,128)(2,1)S(1)}, bf16[2,64,2048]{2,1,0:T(8,128)(2,1)S(1)}, u32[]{:S(2)}, u32[]{:S(2)}) collective-permute-start(bf16[2,64,2048]{2,1,0:T(8,128)(2,1)S(1)} %copy-done.4), channel_id=1, source_target_pairs={{0,4},{4,0},{8,12},{12,8},{16,20},{20,16},{24,28},{28,24},{1,5},{5... | collective-permute-start | bytes 1572872 | tf_op jit(solution)/shard_map/ppermute | solution.py:372
  55.4 11.4 %collective-permute-start.13 = (bf16[2,200,512]{2,1,0:T(8,128)(2,1)S(1)}, bf16[2,200,512]{2,1,0:T(8,128)(2,1)S(1)}, u32[]{:S(2)}, u32[]{:S(2)}) collective-permute-start(bf16[2,200,512]{2,1,0:T(8,128)(2,1)S(1)} %get-tuple-element.24), channel_id=1, source_target_pairs={{0,1},{1,0},{2,3},{3,2},{4,5},{5,4},{6,7},{7,6},{8,9},{9,8},{10,11... | collective-permute-start | bytes 1228808 | tf_op jit(solution)/shard_map/ppermute | solution.py:368
  55.4 13.3 %collective-permute-start.14 = (bf16[2,200,512]{2,1,0:T(8,128)(2,1)S(1)}, bf16[2,200,512]{2,1,0:T(8,128)(2,1)S(1)}, u32[]{:S(2)}, u32[]{:S(2)}) collective-permute-start(bf16[2,200,512]{2,1,0:T(8,128)(2,1)S(1)} %get-tuple-element.31), channel_id=1, source_target_pairs={{1,2},{2,1},{5,6},{6,5},{9,10},{10,9},{13,14},{14,13},{17,18},{18,... | collective-permute-start | bytes 1228808 | tf_op jit(solution)/shard_map/ppermute | solution.py:368

commit v4 on v3

--- a/solution.py
+++ b/solution.py
@@ -172,7 +172,7 @@
 
 
 def attend(query_ref, key_ref, value_ref, filled_ref, half, out_ref):
-    rows = query_ref.shape[0]
+    rows = out_ref.shape[0] - TAIL
     width = key_ref.shape[0]
     position = lax.broadcasted_iota(jnp.int32, (1, width), 1)
     hidden = jnp.where(position < filled_ref[0, 0], 0.0, FAR)
@@ -181,8 +181,12 @@
     totals = jnp.ones((rows, 128), jnp.float32)
     for place in range(HALF):
         columns = head_columns(half * HALF + place)
+        if len(query_ref.shape) == 2:
+            query = query_ref[:rows, columns]
+        else:
+            query = query_ref[half, :rows, head_columns(place)]
         scores = lax.dot_general(
-            query_ref[:, columns],
+            query,
             key_ref[:, columns],
             (((1,), (1,)), ((), ())),
             preferred_element_type=jnp.float32,
@@ -246,6 +250,19 @@
         whole_kernel(*refs)
 
 
+def far_kernel(filled_ref, query_ref, key_ref, value_ref, middle_ref, out_ref):
+    @when_outer
+    def _():
+        whole_kernel(filled_ref, query_ref, key_ref, value_ref, out_ref)
+
+    @when_inner
+    def _():
+        rows = middle_ref.shape[0]
+        for half in range(2):
+            out_ref[half, :rows] = middle_ref[:, half * HALF_WIDTH : (half + 1) * HALF_WIDTH]
+            out_ref[half, rows:] = jnp.zeros((TAIL, HALF_WIDTH), jnp.bfloat16)
+
+
 def inner_kernel(*refs):
     @when_inner
     def _():
@@ -259,17 +276,15 @@
             merge((own_ref.at[half], other_ref.at[half]), out_ref.at[half], 0, out_ref.at[half])
 
 
-def join_kernel(middle_ref, outer_ref, side_ref, inner_ref, to_middle_ref, to_side_ref):
+def join_kernel(own_ref, other_ref, out_ref):
     @when_outer
     def _():
-        to_side_ref[...] = side_ref[...]
+        out_ref[...] = own_ref[...]
 
     @when_inner
     def _():
         for half in range(2):
-            to_middle, to_side = to_middle_ref.at[half], to_side_ref.at[half]
-            merge((middle_ref.at[half], outer_ref.at[half]), to_middle, 0, to_middle)
-            merge((side_ref.at[half], inner_ref.at[half]), to_side, 0, to_side)
+            merge((own_ref.at[half], other_ref.at[half]), out_ref.at[half], 0, out_ref.at[half])
 
 
 def closing_kernel(own_ref, side_ref, middle_ref, out_ref):
@@ -378,32 +393,33 @@
     swap_side = ((0, 1), (1, 0), (2, 3), (3, 2))
     swap_middle = ((1, 2), (2, 1))
     inward = ((0, 1), (3, 2))
-    outward = ((1, 0), (2, 3))
 
     far = over_blk(queries, *swap_far)
     side = over_blk(queries, *swap_side)
     middle = over_blk(queries, *swap_middle)
     own = attention(whole_kernel, "own", queries)
-    far_part = attention(outer_kernel, "far", after(far, own))
-    far_sent = over_blk(far_part, *inward)
-    passed_in = over_blk(after(side, far_part), *swap_middle)
-    passed_out = over_blk(after(middle, far_part), *outward)
-    bank_x = over_bank(after(bank_kv, far_part), 2)
-    bank_y = over_bank(after(bank_kv, far_part), 4)
-    turned = attention(outer_kernel, "turned", after(passed_out, passed_in))
+    far_part = on_core(far_kernel, whole_part, [SMALL] + [WHOLE] * 4, name="far")(
+        filled, after(far, own), keys, values, middle
+    )
+    crossed = over_blk(far_part, *swap_side)
+    passed_in = over_blk(side, *swap_middle)
+    bank_kv_late = after(bank_kv, far, own)
+    bank_x = over_bank(bank_kv_late, 2)
+    bank_y = over_bank(bank_kv_late, 4)
+    bank_xy = over_bank(after(bank_kv_late, bank_x, bank_y), 6)
+    side_part = attention(whole_kernel, "side", after(side, far_part, bank_x, bank_y))
+    middle_part = attention(inner_kernel, "middle", after(middle, side_part))
+    turned = attention(outer_kernel, "turned", after(crossed, passed_in, middle_part))
     from_outer = over_blk(turned, *inward)
     passed = attention(inner_kernel, "passed", after(passed_in, turned))
-    met = on_core(meet_kernel, whole_part, [WHOLE] * 2, name="met")(passed, far_sent)
+    met = on_core(meet_kernel, whole_part, [WHOLE] * 2, name="met")(passed, crossed)
     from_middle = over_blk(met, *swap_middle)
-    side_part = attention(whole_kernel, "side", after(side, met))
-    middle_part = attention(inner_kernel, "middle", after(middle, side_part))
-    bank_xy = over_bank(after(bank_kv, met, bank_x, bank_y), 6)
+    join = on_core(join_kernel, whole_part, [WHOLE] * 2, name="join")
+    to_middle = join(middle_part, from_outer)
+    home_middle = over_blk(to_middle, *swap_middle)
+    to_side = join(after(side_part, to_middle), from_middle)
+    home_side = over_blk(to_side, *swap_side)
     core_c = over_bank(after(bank_kv, met), 1)
-    to_middle, to_side = on_core(join_kernel, (whole_part, whole_part), [WHOLE] * 4, name="join")(
-        middle_part, from_outer, side_part, from_middle
-    )
-    home_middle = over_blk(to_middle, *swap_middle)
-    home_side = over_blk(to_side, *swap_side)
     others = after(jnp.stack((bank_x, bank_y, bank_xy)), to_side)
     core_others = over_bank(others, 1)
 

time: 70.9 us -> 68.9 us (0.972)
  starting transfers between devices: 25.2 us -> 20.6 us
  waiting for transfers between devices: 20.6 us -> 24.2 us
  local copies, waits for them, and re-layouts: 4.28 us -> 3.29 us
    ppermute x10 -> x9, starting transfers between devices: 19.1 us -> 15.5 us  [over_blk(): return lax.ppermute(block, 'blk', route)]
    ppermute x10 -> x9, waiting for transfers between devices: 19.6 us -> 21.8 us  [over_blk(): return lax.ppermute(block, 'blk', route)]
    ppermute x5, waiting for transfers between devices: 1.01 us -> 2.43 us  [over_bank(): return lax.ppermute(block, 'bank', route)]
    unnamed x18, local copies, waits for them, and re-layouts: 4.28 us -> 3.29 us
    ppermute x5, starting transfers between devices: 6.09 us -> 5.14 us  [over_bank(): return lax.ppermute(block, 'bank', route)]
    pallas_call x2 -> x4, Pallas kernels: 2.35 us -> 2.46 us  [the longest x1 0.82 us: joint_pass(): on_core(meet_kernel, whole_part, [WHOLE] * 2, name='met')(passed, crossed)]
    pallas_call x6 -> x5, Pallas kernels: 9.75 us -> 9.75 us  [attention(): on_core(kernel, whole_part, [SMALL] + [WHOLE] * 3, name=name)]
  transfers between devices with their start and end apart: 15 -> 14, of which waited for: 7 -> 9; matrix products, arithmetic and copies ran while one was open for 0% -> 0% of each run, Pallas kernels for 24% -> 25%
where the time goes in v4:
time: 68.9 us; the launch traced here: 68.5 us
  waiting for transfers between devices  24.2 us (35%)
  starting transfers between devices  20.6 us (30%)
  Pallas kernels  18.8 us (27%)
  local copies, waits for them, and re-layouts  3.29 us (5%)
  between operations  1.47 us (2%)
    ppermute x9, waiting for transfers between devices, over_blk(): return lax.ppermute(block, 'blk', route)  21.8 us
    ppermute x9, starting transfers between devices, over_blk(): return lax.ppermute(block, 'blk', route)  15.5 us
    pallas_call x5, Pallas kernels, attention(): on_core(kernel, whole_part, [SMALL] + [WHOLE] * 3, name=name)  9.75 us
    ppermute x5, starting transfers between devices, over_bank(): return lax.ppermute(block, 'bank', route)  5.14 us
    pallas_call x1, Pallas kernels, joint_pass(): on_core(spans_kernel, plain, [SMALL, SMALL, WHOLE] + [AWAY] * 4, scratch=...  4.88 us
    unnamed x18, local copies, waits for them, and re-layouts  3.29 us
    ppermute x5, waiting for transfers between devices, over_bank(): return lax.ppermute(block, 'bank', route)  2.43 us
    pallas_call x1, Pallas kernels, joint_pass(): on_core(closing_kernel, plain, [WHOLE] * 3, name='closing')  1.69 us
  transfers between devices with their start and end apart: 14, of which 9 were waited for; matrix products, arithmetic and copies ran while one was open for 0% of the time, Pallas kernels for 25%

profile of v4, /device:TPU:8, one launch (start us, length us, event | category | flops | bytes accessed | tf_op | source)
XLA Modules:
  0.0 68.5 jit_solution(3457618486111327827)
XLA Ops:
  0.6 0.7 %collective-permute-start.1 = (bf16[192,1024]{1,0:T(8,128)(2,1)}, bf16[192,1024]{1,0:T(8,128)(2,1)S(1)}, u32[]{:S(2)}, u32[]{:S(2)}) collective-permute-start(bf16[192,1024]{1,0:T(8,128)(2,1)} %bitcast.25), channel_id=1, source_target_pairs={{0,3},{3,0},{4,7},{7,4},{8,11},{11,8},{12,15},{15,12},{16,19},{19,... | collective-permute-start | bytes 1179656 | tf_op jit(solution)/shard_map/ppermute | solution.py:383
  1.3 3.5 %collective-permute-start.2 = (bf16[192,1024]{1,0:T(8,128)(2,1)}, bf16[192,1024]{1,0:T(8,128)(2,1)S(1)}, u32[]{:S(2)}, u32[]{:S(2)}) collective-permute-start(bf16[192,1024]{1,0:T(8,128)(2,1)} %bitcast.26), channel_id=1, source_target_pairs={{1,2},{2,1},{5,6},{6,5},{9,10},{10,9},{13,14},{14,13},{17,18},{18,... | collective-permute-start | bytes 1179656 | tf_op jit(solution)/shard_map/ppermute | solution.py:383
  4.8 2.5 %collective-permute-start = (bf16[192,1024]{1,0:T(8,128)(2,1)}, bf16[192,1024]{1,0:T(8,128)(2,1)S(1)}, u32[]{:S(2)}, u32[]{:S(2)}) collective-permute-start(bf16[192,1024]{1,0:T(8,128)(2,1)} %bitcast.27), channel_id=1, source_target_pairs={{0,1},{1,0},{2,3},{3,2},{4,5},{5,4},{6,7},{7,6},{8,9},{9,8},{10,11... | collective-permute-start | bytes 1179656 | tf_op jit(solution)/shard_map/ppermute | solution.py:383
  8.0 0.0 copy-start
  8.0 1.1 %copy-done = bf16[1,384,1024]{2,1,0:T(8,128)(2,1)S(1)} copy-done((bf16[1,384,1024]{2,1,0:T(8,128)(2,1)S(1)}, bf16[1,384,1024]{2,1,0:T(8,128)(2,1)}, u32[]{:S(2)}) %copy-start) | copy-done | bytes 786456
  9.1 1.1 %copy-done.2 = bf16[1,384,1024]{2,1,0:T(8,128)(2,1)S(1)} copy-done((bf16[1,384,1024]{2,1,0:T(8,128)(2,1)S(1)}, bf16[1,384,1024]{2,1,0:T(8,128)(2,1)}, u32[]{:S(2)}) %copy-start.2) | copy-done | bytes 786456
  10.3 1.0 %copy-done.6 = bf16[1,192,1024]{2,1,0:T(8,128)(2,1)S(1)} copy-done((bf16[1,192,1024]{2,1,0:T(8,128)(2,1)S(1)}, bf16[1,192,1024]{2,1,0:T(8,128)(2,1)}, u32[]{:S(2)}) %copy-start.6) | copy-done | bytes 393240
  11.3 2.4 %own.1.own_ref = bf16[2,200,512]{2,1,0:T(8,128)(2,1)S(1)} custom-call(s32[1,1]{1,0:T(1,128)S(6)} %copy.10.filled_ref.refs_0_, bf16[192,1024]{1,0:T(8,128)(2,1)S(1)} %bitcast.28, bf16[384,1024]{1,0:T(8,128)(2,1)S(1)} %bitcast.12, bf16[384,1024]{1,0:T(8,128)(2,1)S(1)} %bitcast.18), custom_call_target="tpu_custom_call" | custom-call | flops 1 | bytes 1 | tf_op jit(solution)/shard_map/own/pallas_call | solution.py:390
  13.7 0.0 collective-permute-done.1.query_ref
  13.7 0.0 copy-done.4
  13.7 1.6 %collective-permute-start.3 = (bf16[2,64,2048]{2,1,0:T(8,128)(2,1)S(1)}, bf16[2,64,2048]{2,1,0:T(8,128)(2,1)S(1)}, u32[]{:S(2)}, u32[]{:S(2)}) collective-permute-start(bf16[2,64,2048]{2,1,0:T(8,128)(2,1)S(1)} %copy-done.4), channel_id=1, source_target_pairs={{0,8},{4,12},{8,0},{12,4},{16,24},{20,28},{24,16},{28,20},{1,9},{5... | collective-permute-start | bytes 1572872 | tf_op jit(solution)/shard_map/ppermute | solution.py:387
  15.3 1.5 %collective-permute-start.4 = (bf16[2,64,2048]{2,1,0:T(8,128)(2,1)S(1)}, bf16[2,64,2048]{2,1,0:T(8,128)(2,1)S(1)}, u32[]{:S(2)}, u32[]{:S(2)}) collective-permute-start(bf16[2,64,2048]{2,1,0:T(8,128)(2,1)S(1)} %copy-done.4), channel_id=1, source_target_pairs={{0,16},{4,20},{8,24},{12,28},{16,0},{20,4},{24,8},{28,12},{1,17},{... | collective-permute-start | bytes 1572872 | tf_op jit(solution)/shard_map/ppermute | solution.py:387
  16.8 5.9 %collective-permute-done.2.middle_ref.refs_1_ = bf16[192,1024]{1,0:T(8,128)(2,1)S(1)} collective-permute-done((bf16[192,1024]{1,0:T(8,128)(2,1)}, bf16[192,1024]{1,0:T(8,128)(2,1)S(1)}, u32[]{:S(2)}, u32[]{:S(2)}) %collective-permute-start.2) | collective-permute-done | bytes 393248 | tf_op jit(solution)/shard_map/ppermute | solution.py:383
  22.7 0.0 copy-done.3
  22.7 0.1 collective-permute-start.5
  22.8 1.3 %collective-permute-done.query_ref = bf16[192,1024]{1,0:T(8,128)(2,1)S(1)} collective-permute-done((bf16[192,1024]{1,0:T(8,128)(2,1)}, bf16[192,1024]{1,0:T(8,128)(2,1)S(1)}, u32[]{:S(2)}, u32[]{:S(2)}) %collective-permute-start) | collective-permute-done | bytes 393248 | tf_op jit(solution)/shard_map/ppermute | solution.py:383
  24.1 3.0 %collective-permute-start.6 = (bf16[192,1024]{1,0:T(8,128)(2,1)S(1)}, bf16[192,1024]{1,0:T(8,128)(2,1)S(1)}, u32[]{:S(2)}, u32[]{:S(2)}) collective-permute-start(bf16[192,1024]{1,0:T(8,128)(2,1)S(1)} %collective-permute-done.query_ref), channel_id=1, source_target_pairs={{1,2},{2,1},{5,6},{6,5},{9,10},{10,9},{13,14},{14,13},{17,18},{18,... | collective-permute-start | bytes 1179656 | tf_op jit(solution)/shard_map/ppermute | solution.py:383
  27.1 0.0 collective-permute-done.3
  27.1 1.0 %collective-permute-done.4 = bf16[2,64,2048]{2,1,0:T(8,128)(2,1)S(1)} collective-permute-done((bf16[2,64,2048]{2,1,0:T(8,128)(2,1)S(1)}, bf16[2,64,2048]{2,1,0:T(8,128)(2,1)S(1)}, u32[]{:S(2)}, u32[]{:S(2)}) %collective-permute-start.4) | collective-permute-done | bytes 524320 | tf_op jit(solution)/shard_map/ppermute | solution.py:387
  28.1 1.5 %collective-permute-start.10 = (bf16[2,64,2048]{2,1,0:T(8,128)(2,1)S(1)}, bf16[2,64,2048]{2,1,0:T(8,128)(2,1)S(1)}, u32[]{:S(2)}, u32[]{:S(2)}) collective-permute-start(bf16[2,64,2048]{2,1,0:T(8,128)(2,1)S(1)} %copy-done.4), channel_id=1, source_target_pairs={{0,24},{4,28},{8,16},{12,20},{16,8},{20,12},{24,0},{28,4},{1,25},{... | collective-permute-start | bytes 1572872 | tf_op jit(solution)/shard_map/ppermute | solution.py:387
  29.6 2.4 %side.1.own_ref = bf16[2,200,512]{2,1,0:T(8,128)(2,1)S(1)} custom-call(s32[1,1]{1,0:T(1,128)S(6)} %copy.10.filled_ref.refs_0_, bf16[192,1024]{1,0:T(8,128)(2,1)S(1)} %collective-permute-done.query_ref, bf16[384,1024]{1,0:T(8,128)(2,1)S(1)} %bitcast.14, bf16[384,1024]{1,0:T(8,128)(2,1)S(1)} %bitcast.20), custom_call_target="tpu_custom_call" | custom-call | flops 1 | bytes 1 | tf_op jit(solution)/shard_map/side/pallas_call | solution.py:390
  32.0 2.4 %middle.1.own_ref = bf16[2,200,512]{2,1,0:T(8,128)(2,1)S(1)} custom-call(s32[1,1]{1,0:T(1,128)S(6)} %copy.10.filled_ref.refs_0_, bf16[192,1024]{1,0:T(8,128)(2,1)S(1)} %collective-permute-done.2.middle_ref.refs_1_, bf16[384,1024]{1,0:T(8,128)(2,1)S(1)} %bitcast.15, bf16[384,1024]{1,0:T(8,128)(2,1)S(1)} %bitcast.21), custom_call_target="tpu_custom_call" | custom-call | flops 1 | bytes 1 | tf_op jit(solution)/shard_map/middle/pallas_call | solution.py:390
  34.5 1.5 %collective-permute-done.6.refs_1_ = bf16[192,1024]{1,0:T(8,128)(2,1)S(1)} collective-permute-done((bf16[192,1024]{1,0:T(8,128)(2,1)S(1)}, bf16[192,1024]{1,0:T(8,128)(2,1)S(1)}, u32[]{:S(2)}, u32[]{:S(2)}) %collective-permute-start.6) | collective-permute-done | bytes 393248 | tf_op jit(solution)/shard_map/ppermute | solution.py:383
  36.0 0.0 collective-permute-done.5.refs_1_.other_ref
  36.0 1.3 %collective-permute-start.7 = (bf16[2,200,512]{2,1,0:T(8,128)(2,1)S(1)}, bf16[2,200,512]{2,1,0:T(8,128)(2,1)S(1)}, u32[]{:S(2)}, u32[]{:S(2)}) collective-permute-start(bf16[2,200,512]{2,1,0:T(8,128)(2,1)S(1)} %turned.1), channel_id=1, source_target_pairs={{0,1},{3,2},{4,5},{7,6},{8,9},{11,10},{12,13},{15,14},{16,17},{19,... | collective-permute-start | bytes 1228808 | tf_op jit(solution)/shard_map/ppermute | solution.py:383
  37.3 2.4 %passed.1.own_ref = bf16[2,200,512]{2,1,0:T(8,128)(2,1)S(1)} custom-call(s32[1,1]{1,0:T(1,128)S(6)} %copy.10.filled_ref.refs_0_, bf16[192,1024]{1,0:T(8,128)(2,1)S(1)} %collective-permute-done.6.refs_1_, bf16[384,1024]{1,0:T(8,128)(2,1)S(1)} %bitcast.17, bf16[384,1024]{1,0:T(8,128)(2,1)S(1)} %bitcast.23), custom_call_target="tpu_custom_call" | custom-call | flops 1 | bytes 1 | tf_op jit(solution)/shard_map/passed/pallas_call | solution.py:390
  39.7 0.8 %met.1 = bf16[2,200,512]{2,1,0:T(8,128)(2,1)S(1)} custom-call(bf16[2,200,512]{2,1,0:T(8,128)(2,1)S(1)} %passed.1.own_ref, bf16[2,200,512]{2,1,0:T(8,128)(2,1)S(1)} %collective-permute-done.5.refs_1_.other_ref), custom_call_target="tpu_custom_call" | custom-call | flops 1 | bytes 1 | tf_op jit(solution)/shard_map/met/pallas_call | solution.py:415
  40.6 2.2 %collective-permute-start.8 = (bf16[2,200,512]{2,1,0:T(8,128)(2,1)S(1)}, bf16[2,200,512]{2,1,0:T(8,128)(2,1)S(1)}, u32[]{:S(2)}, u32[]{:S(2)}) collective-permute-start(bf16[2,200,512]{2,1,0:T(8,128)(2,1)S(1)} %met.1), channel_id=1, source_target_pairs={{1,2},{2,1},{5,6},{6,5},{9,10},{10,9},{13,14},{14,13},{17,18},{18,... | collective-permute-start | bytes 1228808 | tf_op jit(solution)/shard_map/ppermute | solution.py:383
  42.8 4.6 %collective-permute-done.7.other_ref = bf16[2,200,512]{2,1,0:T(8,128)(2,1)S(1)} collective-permute-done((bf16[2,200,512]{2,1,0:T(8,128)(2,1)S(1)}, bf16[2,200,512]{2,1,0:T(8,128)(2,1)S(1)}, u32[]{:S(2)}, u32[]{:S(2)}) %collective-permute-start.7) | collective-permute-done | bytes 409632 | tf_op jit(solution)/shard_map/ppermute | solution.py:383
  47.3 0.8 %join.2 = bf16[2,200,512]{2,1,0:T(8,128)(2,1)S(1)} custom-call(bf16[2,200,512]{2,1,0:T(8,128)(2,1)S(1)} %middle.1.own_ref, bf16[2,200,512]{2,1,0:T(8,128)(2,1)S(1)} %collective-permute-done.7.other_ref), custom_call_target="tpu_custom_call" | custom-call | flops 1 | bytes 1 | tf_op jit(solution)/shard_map/join/pallas_call | solution.py:418
  48.1 3.8 %collective-permute-done.8.other_ref = bf16[2,200,512]{2,1,0:T(8,128)(2,1)S(1)} collective-permute-done((bf16[2,200,512]{2,1,0:T(8,128)(2,1)S(1)}, bf16[2,200,512]{2,1,0:T(8,128)(2,1)S(1)}, u32[]{:S(2)}, u32[]{:S(2)}) %collective-permute-start.8) | collective-permute-done | bytes 409632 | tf_op jit(solution)/shard_map/ppermute | solution.py:383
  51.9 0.8 %join.3 = bf16[2,200,512]{2,1,0:T(8,128)(2,1)S(1)} custom-call(bf16[2,200,512]{2,1,0:T(8,128)(2,1)S(1)} %side.1.own_ref, bf16[2,200,512]{2,1,0:T(8,128)(2,1)S(1)} %collective-permute-done.8.other_ref), custom_call_target="tpu_custom_call" | custom-call | flops 1 | bytes 1 | tf_op jit(solution)/shard_map/join/pallas_call | solution.py:420
  52.7 0.0 collective-permute-done.10
  52.7 0.0 copy-start.5
  52.7 0.0 copy-start.7
  52.7 0.0 copy-start.8
  52.8 0.2 pad_maximum_fusion.refs_2_
  52.9 0.1 collective-permute-start.11
  53.0 0.5 collective-permute-start.9
  53.5 0.0 collective-permute-start.12
  53.5 2.2 %collective-permute-start.13 = (bf16[2,200,512]{2,1,0:T(8,128)(2,1)S(1)}, bf16[2,200,512]{2,1,0:T(8,128)(2,1)S(1)}, u32[]{:S(2)}, u32[]{:S(2)}) collective-permute-start(bf16[2,200,512]{2,1,0:T(8,128)(2,1)S(1)} %join.2), channel_id=1, source_target_pairs={{1,2},{2,1},{5,6},{6,5},{9,10},{10,9},{13,14},{14,13},{17,18},{18,... | collective-permute-start | bytes 1228808 | tf_op jit(solution)/shard_map/ppermute | solution.py:383
  55.7 1.4 %collective-permute-done.9.refs_1_ = bf16[2,64,2048]{2,1,0:T(8,128)(2,1)S(1)} collective-permute-done((bf16[2,64,2048]{2,1,0:T(8,128)(2,1)S(1)}, bf16[2,64,2048]{2,1,0:T(8,128)(2,1)S(1)}, u32[]{:S(2)}, u32[]{:S(2)}) %collective-permute-start.9) | collective-permute-done | bytes 524320 | tf_op jit(solution)/shard_map/ppermute | solution.py:387
  57.2 0.0 collective-permute-done.11.refs_3_
  57.2 0.0 copy-done.5
  57.2 4.9 %spans.1 = bf16[192,1024]{1,0:T(8,128)(2,1)} custom-call(s32[16]{0:T(128)S(1)} %copy-done.8, s32[2,12]{1,0:T(2,128)S(1)} %bitcast.29, bf16[192,1024]{1,0:T(8,128)(2,1)S(1)} %bitcast.24, bf16[2,64,2048]{2,1,0:T(8,128)(2,1)S(1)} %copy-done.4, bf16[2,64,2048]{2,1,0:T(8,128)(2,1)S(1)} %collective-permute-done.9.refs_1_, ...), custom_call_target="tpu_custom_call" | custom-call | flops 1 | bytes 1 | tf_op jit(solution)/shard_map/spans/pallas_call | solution.py:426
  62.1 2.9 %collective-permute-done.12.side_ref = bf16[2,200,512]{2,1,0:T(8,128)(2,1)S(1)} collective-permute-done((bf16[2,200,512]{2,1,0:T(8,128)(2,1)S(1)}, bf16[2,200,512]{2,1,0:T(8,128)(2,1)S(1)}, u32[]{:S(2)}, u32[]{:S(2)}) %collective-permute-start.12) | collective-permute-done | bytes 409632 | tf_op jit(solution)/shard_map/ppermute | solution.py:383
  65.0 1.9 %collective-permute-done.13.middle_ref = bf16[2,200,512]{2,1,0:T(8,128)(2,1)S(1)} collective-permute-done((bf16[2,200,512]{2,1,0:T(8,128)(2,1)S(1)}, bf16[2,200,512]{2,1,0:T(8,128)(2,1)S(1)}, u32[]{:S(2)}, u32[]{:S(2)}) %collective-permute-start.13) | collective-permute-done | bytes 409632 | tf_op jit(solution)/shard_map/ppermute | solution.py:383
  66.8 1.7 %closing.1 = bf16[192,1024]{1,0:T(8,128)(2,1)} custom-call(bf16[2,200,512]{2,1,0:T(8,128)(2,1)S(1)} %own.1.own_ref, bf16[2,200,512]{2,1,0:T(8,128)(2,1)S(1)} %collective-permute-done.12.side_ref, bf16[2,200,512]{2,1,0:T(8,128)(2,1)S(1)} %collective-permute-done.13.middle_ref), custom_call_target="tpu_custom_call" | custom-call | flops 1 | bytes 1 | tf_op jit(solution)/shard_map/closing/pallas_call | solution.py:433
  (10 shorter events, 0.0 us)
Async XLA Ops:
  0.6 13.1 %collective-permute-start.1 = (bf16[192,1024]{1,0:T(8,128)(2,1)}, bf16[192,1024]{1,0:T(8,128)(2,1)S(1)}, u32[]{:S(2)}, u32[]{:S(2)}) collective-permute-start(bf16[192,1024]{1,0:T(8,128)(2,1)} %bitcast.25), channel_id=1, source_target_pairs={{0,3},{3,0},{4,7},{7,4},{8,11},{11,8},{12,15},{15,12},{16,19},{19,... | collective-permute-start | bytes 1179656 | tf_op jit(solution)/shard_map/ppermute | solution.py:383
  1.3 21.4 %collective-permute-start.2 = (bf16[192,1024]{1,0:T(8,128)(2,1)}, bf16[192,1024]{1,0:T(8,128)(2,1)S(1)}, u32[]{:S(2)}, u32[]{:S(2)}) collective-permute-start(bf16[192,1024]{1,0:T(8,128)(2,1)} %bitcast.26), channel_id=1, source_target_pairs={{1,2},{2,1},{5,6},{6,5},{9,10},{10,9},{13,14},{14,13},{17,18},{18,... | collective-permute-start | bytes 1179656 | tf_op jit(solution)/shard_map/ppermute | solution.py:383
  4.8 19.3 %collective-permute-start = (bf16[192,1024]{1,0:T(8,128)(2,1)}, bf16[192,1024]{1,0:T(8,128)(2,1)S(1)}, u32[]{:S(2)}, u32[]{:S(2)}) collective-permute-start(bf16[192,1024]{1,0:T(8,128)(2,1)} %bitcast.27), channel_id=1, source_target_pairs={{0,1},{1,0},{2,3},{3,2},{4,5},{5,4},{6,7},{7,6},{8,9},{9,8},{10,11... | collective-permute-start | bytes 1179656 | tf_op jit(solution)/shard_map/ppermute | solution.py:383
  8.0 1.1 %copy-start = (bf16[1,384,1024]{2,1,0:T(8,128)(2,1)S(1)}, bf16[1,384,1024]{2,1,0:T(8,128)(2,1)}, u32[]{:S(2)}) copy-start(bf16[1,384,1024]{2,1,0:T(8,128)(2,1)} %param.9) | copy-start | bytes 2359300
  9.1 1.1 %copy-start.2 = (bf16[1,384,1024]{2,1,0:T(8,128)(2,1)S(1)}, bf16[1,384,1024]{2,1,0:T(8,128)(2,1)}, u32[]{:S(2)}) copy-start(bf16[1,384,1024]{2,1,0:T(8,128)(2,1)} %param.10) | copy-start | bytes 2359300
  10.3 1.0 %copy-start.6 = (bf16[1,192,1024]{2,1,0:T(8,128)(2,1)S(1)}, bf16[1,192,1024]{2,1,0:T(8,128)(2,1)}, u32[]{:S(2)}) copy-start(bf16[1,192,1024]{2,1,0:T(8,128)(2,1)} %param.8) | copy-start | bytes 1179652
  11.3 2.4 %copy-start.4 = (bf16[2,64,2048]{2,1,0:T(8,128)(2,1)S(1)}, bf16[2,64,2048]{2,1,0:T(8,128)(2,1)}, u32[]{:S(2)}) copy-start(bf16[2,64,2048]{2,1,0:T(8,128)(2,1)} %refs_0_.4) | copy-start | bytes 1572868
  11.3 11.4 %copy-start.1 = (bf16[1,384,1024]{2,1,0:T(8,128)(2,1)S(1)}, bf16[1,384,1024]{2,1,0:T(8,128)(2,1)}, u32[]{:S(2)}) copy-start(bf16[1,384,1024]{2,1,0:T(8,128)(2,1)} %param.9) | copy-start | bytes 2359300
  11.3 11.4 %copy-start.3 = (bf16[1,384,1024]{2,1,0:T(8,128)(2,1)S(1)}, bf16[1,384,1024]{2,1,0:T(8,128)(2,1)}, u32[]{:S(2)}) copy-start(bf16[1,384,1024]{2,1,0:T(8,128)(2,1)} %param.10) | copy-start | bytes 2359300
  13.7 13.4 %collective-permute-start.3 = (bf16[2,64,2048]{2,1,0:T(8,128)(2,1)S(1)}, bf16[2,64,2048]{2,1,0:T(8,128)(2,1)S(1)}, u32[]{:S(2)}, u32[]{:S(2)}) collective-permute-start(bf16[2,64,2048]{2,1,0:T(8,128)(2,1)S(1)} %copy-done.4), channel_id=1, source_target_pairs={{0,8},{4,12},{8,0},{12,4},{16,24},{20,28},{24,16},{28,20},{1,9},{5... | collective-permute-start | bytes 1572872 | tf_op jit(solution)/shard_map/ppermute | solution.py:387
  15.3 12.8 %collective-permute-start.4 = (bf16[2,64,2048]{2,1,0:T(8,128)(2,1)S(1)}, bf16[2,64,2048]{2,1,0:T(8,128)(2,1)S(1)}, u32[]{:S(2)}, u32[]{:S(2)}) collective-permute-start(bf16[2,64,2048]{2,1,0:T(8,128)(2,1)S(1)} %copy-done.4), channel_id=1, source_target_pairs={{0,16},{4,20},{8,24},{12,28},{16,0},{20,4},{24,8},{28,12},{1,17},{... | collective-permute-start | bytes 1572872 | tf_op jit(solution)/shard_map/ppermute | solution.py:387
  22.7 13.2 %collective-permute-start.5 = (bf16[2,200,512]{2,1,0:T(8,128)(2,1)S(1)}, bf16[2,200,512]{2,1,0:T(8,128)(2,1)S(1)}, u32[]{:S(2)}, u32[]{:S(2)}) collective-permute-start(bf16[2,200,512]{2,1,0:T(8,128)(2,1)S(1)} %far.1), channel_id=1, source_target_pairs={{0,1},{1,0},{2,3},{3,2},{4,5},{5,4},{6,7},{7,6},{8,9},{9,8},{10,11... | collective-permute-start | bytes 1228808 | tf_op jit(solution)/shard_map/ppermute | solution.py:383
  24.1 11.9 %collective-permute-start.6 = (bf16[192,1024]{1,0:T(8,128)(2,1)S(1)}, bf16[192,1024]{1,0:T(8,128)(2,1)S(1)}, u32[]{:S(2)}, u32[]{:S(2)}) collective-permute-start(bf16[192,1024]{1,0:T(8,128)(2,1)S(1)} %collective-permute-done.query_ref), channel_id=1, source_target_pairs={{1,2},{2,1},{5,6},{6,5},{9,10},{10,9},{13,14},{14,13},{17,18},{18,... | collective-permute-start | bytes 1179656 | tf_op jit(solution)/shard_map/ppermute | solution.py:383
  28.1 24.6 %collective-permute-start.10 = (bf16[2,64,2048]{2,1,0:T(8,128)(2,1)S(1)}, bf16[2,64,2048]{2,1,0:T(8,128)(2,1)S(1)}, u32[]{:S(2)}, u32[]{:S(2)}) collective-permute-start(bf16[2,64,2048]{2,1,0:T(8,128)(2,1)S(1)} %copy-done.4), channel_id=1, source_target_pairs={{0,24},{4,28},{8,16},{12,20},{16,8},{20,12},{24,0},{28,4},{1,25},{... | collective-permute-start | bytes 1572872 | tf_op jit(solution)/shard_map/ppermute | solution.py:387
  36.0 11.3 %collective-permute-start.7 = (bf16[2,200,512]{2,1,0:T(8,128)(2,1)S(1)}, bf16[2,200,512]{2,1,0:T(8,128)(2,1)S(1)}, u32[]{:S(2)}, u32[]{:S(2)}) collective-permute-start(bf16[2,200,512]{2,1,0:T(8,128)(2,1)S(1)} %turned.1), channel_id=1, source_target_pairs={{0,1},{3,2},{4,5},{7,6},{8,9},{11,10},{12,13},{15,14},{16,17},{19,... | collective-permute-start | bytes 1228808 | tf_op jit(solution)/shard_map/ppermute | solution.py:383
  40.6 11.3 %collective-permute-start.8 = (bf16[2,200,512]{2,1,0:T(8,128)(2,1)S(1)}, bf16[2,200,512]{2,1,0:T(8,128)(2,1)S(1)}, u32[]{:S(2)}, u32[]{:S(2)}) collective-permute-start(bf16[2,200,512]{2,1,0:T(8,128)(2,1)S(1)} %met.1), channel_id=1, source_target_pairs={{1,2},{2,1},{5,6},{6,5},{9,10},{10,9},{13,14},{14,13},{17,18},{18,... | collective-permute-start | bytes 1228808 | tf_op jit(solution)/shard_map/ppermute | solution.py:383
  52.7 4.4 %copy-start.5 = (bf16[1,192,1024]{2,1,0:T(8,128)(2,1)S(1)}, bf16[1,192,1024]{2,1,0:T(8,128)(2,1)}, u32[]{:S(2)}) copy-start(bf16[1,192,1024]{2,1,0:T(8,128)(2,1)} %param.12) | copy-start | bytes 1179652
  52.7 4.4 %copy-start.7 = (s32[1,12,2]{1,2,0:T(2,128)S(1)}, s32[1,12,2]{1,2,0:T(2,128)}, u32[]{:S(2)}) copy-start(s32[1,12,2]{1,2,0:T(2,128)} %param.15) | copy-start | bytes 292
  52.7 4.4 %copy-start.8 = (s32[16]{0:T(128)S(1)}, s32[16]{0:T(128)}, u32[]{:S(2)}) copy-start(s32[16]{0:T(128)} %home_ref.1) | copy-start | bytes 196
  52.9 4.2 %collective-permute-start.11 = (bf16[3,2,64,2048]{3,2,1,0:T(8,128)(2,1)S(1)}, bf16[3,2,64,2048]{3,2,1,0:T(8,128)(2,1)S(1)}, u32[]{:S(2)}, u32[]{:S(2)}) collective-permute-start(bf16[3,2,64,2048]{3,2,1,0:T(8,128)(2,1)S(1)} %pad_maximum_fusion.refs_2_), channel_id=1, source_target_pairs={{0,4},{4,0},{8,12},{12,8},{16,20},{20,16},{24,28},{28,24},{1,5},{5... | collective-permute-start | bytes 4718600 | tf_op jit(solution)/shard_map/ppermute | solution.py:387
  53.0 4.1 %collective-permute-start.9 = (bf16[2,64,2048]{2,1,0:T(8,128)(2,1)S(1)}, bf16[2,64,2048]{2,1,0:T(8,128)(2,1)S(1)}, u32[]{:S(2)}, u32[]{:S(2)}) collective-permute-start(bf16[2,64,2048]{2,1,0:T(8,128)(2,1)S(1)} %copy-done.4), channel_id=1, source_target_pairs={{0,4},{4,0},{8,12},{12,8},{16,20},{20,16},{24,28},{28,24},{1,5},{5... | collective-permute-start | bytes 1572872 | tf_op jit(solution)/shard_map/ppermute | solution.py:387
  53.5 11.4 %collective-permute-start.12 = (bf16[2,200,512]{2,1,0:T(8,128)(2,1)S(1)}, bf16[2,200,512]{2,1,0:T(8,128)(2,1)S(1)}, u32[]{:S(2)}, u32[]{:S(2)}) collective-permute-start(bf16[2,200,512]{2,1,0:T(8,128)(2,1)S(1)} %join.3), channel_id=1, source_target_pairs={{0,1},{1,0},{2,3},{3,2},{4,5},{5,4},{6,7},{7,6},{8,9},{9,8},{10,11... | collective-permute-start | bytes 1228808 | tf_op jit(solution)/shard_map/ppermute | solution.py:383
  53.5 13.3 %collective-permute-start.13 = (bf16[2,200,512]{2,1,0:T(8,128)(2,1)S(1)}, bf16[2,200,512]{2,1,0:T(8,128)(2,1)S(1)}, u32[]{:S(2)}, u32[]{:S(2)}) collective-permute-start(bf16[2,200,512]{2,1,0:T(8,128)(2,1)S(1)} %join.2), channel_id=1, source_target_pairs={{1,2},{2,1},{5,6},{6,5},{9,10},{10,9},{13,14},{14,13},{17,18},{18,... | collective-permute-start | bytes 1228808 | tf_op jit(solution)/shard_map/ppermute | solution.py:383

commit v5 on v4

--- a/solution.py
+++ b/solution.py
@@ -144,69 +144,90 @@
 HALF_WIDTH = HALF * HD
 
 
+def padded_lanes(rows):
+    return pl.cdiv(rows, 128) * 128
+
+
 def put_logs(out_ref, logs):
-    rows = logs.shape[0]
-    lanes = pl.cdiv(rows, 128) * 128
-    padded = jnp.concatenate((logs, jnp.zeros((lanes - rows, 128), jnp.float32)), axis=0)
-    whole = jnp.transpose(padded)[:TAIL]
-    first = whole.astype(jnp.bfloat16).astype(jnp.float32)
-    rest = whole - first
+    rows = out_ref.shape[1] - TAIL
+    lanes = logs.shape[1]
+    first = logs.astype(jnp.bfloat16).astype(jnp.float32)
+    rest = logs - first
     second = rest.astype(jnp.bfloat16).astype(jnp.float32)
-    upper = lax.broadcasted_iota(jnp.int32, (TAIL, lanes), 0) < HALF
-    out_ref[rows:, :lanes] = jnp.where(upper, first, rest - second).astype(jnp.bfloat16)
-    out_ref[rows:, lanes : 2 * lanes] = second.astype(jnp.bfloat16)
+    out_ref[0, rows:, :lanes] = first.astype(jnp.bfloat16)
+    out_ref[0, rows:, lanes : 2 * lanes] = second.astype(jnp.bfloat16)
+    out_ref[1, rows:, :lanes] = (rest - second).astype(jnp.bfloat16)
+    out_ref[1, rows:, lanes : 2 * lanes] = jnp.zeros((TAIL, lanes), jnp.bfloat16)
 
 
 def get_logs(part_ref):
-    rows = part_ref.shape[0] - TAIL
-    lanes = pl.cdiv(rows, 128) * 128
-    first = part_ref[rows:, :lanes].astype(jnp.float32)
-    second = part_ref[rows:, lanes : 2 * lanes].astype(jnp.float32)
-    whole = (pltpu.roll(first, HALF, 0) + second) + first
-    padded = jnp.concatenate((whole, jnp.zeros((128 - TAIL, lanes), jnp.float32)), axis=0)
-    return jnp.transpose(padded)[:rows]
+    rows = part_ref.shape[1] - TAIL
+    lanes = padded_lanes(rows)
+    first = part_ref[0, rows:, :lanes].astype(jnp.float32)
+    second = part_ref[0, rows:, lanes : 2 * lanes].astype(jnp.float32)
+    third = part_ref[1, rows:, :lanes].astype(jnp.float32)
+    return (third + second) + first
 
 
 def head_columns(head):
     return slice(head * HD, (head + 1) * HD)
 
 
-def attend(query_ref, key_ref, value_ref, filled_ref, half, out_ref):
-    rows = out_ref.shape[0] - TAIL
+def head_place(head):
+    return head // HALF, head_columns(head % HALF)
+
+
+def attend(query_ref, key_ref, value_ref, filled_ref, out_ref):
+    rows = out_ref.shape[1] - TAIL
     width = key_ref.shape[0]
     position = lax.broadcasted_iota(jnp.int32, (1, width), 1)
     hidden = jnp.where(position < filled_ref[0, 0], 0.0, FAR)
     lane = lax.broadcasted_iota(jnp.int32, (rows, 128), 1)
-    tops = jnp.zeros((rows, 128), jnp.float32)
-    totals = jnp.ones((rows, 128), jnp.float32)
-    for place in range(HALF):
-        columns = head_columns(half * HALF + place)
-        if len(query_ref.shape) == 2:
-            query = query_ref[:rows, columns]
+
+    def score(head):
+        half, columns = head_place(head)
+        if len(query_ref.shape) == 3:
+            query = query_ref[half, :rows, columns]
         else:
-            query = query_ref[half, :rows, head_columns(place)]
-        scores = lax.dot_general(
+            query = query_ref[:, head_columns(head)]
+        return lax.dot_general(
             query,
-            key_ref[:, columns],
+            key_ref[:, head_columns(head)],
             (((1,), (1,)), ((), ())),
             preferred_element_type=jnp.float32,
         )
-        scores = scores * (HD ** (-0.5) * LOG2E) + hidden
+
+    def finish(head, weights, total):
+        half, columns = head_place(head)
+        summed = jnp.dot(weights, value_ref[:, head_columns(head)], preferred_element_type=jnp.float32)
+        out_ref[half, :rows, columns] = (summed * (1.0 / total)).astype(jnp.bfloat16)
+
+    ready = [score(0), score(1)]
+    late = None
+    tops = jnp.zeros((rows, 128), jnp.float32)
+    totals = jnp.ones((rows, 128), jnp.float32)
+    for head in range(HEADS):
+        if head + 2 < HEADS:
+            ready.append(score(head + 2))
+        scores = ready.pop(0) * (HD ** (-0.5) * LOG2E) + hidden
         top = jnp.max(scores, axis=1, keepdims=True)
         expo = jnp.exp2(scores - top)
         total = jnp.sum(expo, axis=1, keepdims=True)
-        summed = jnp.dot(
-            expo.astype(jnp.bfloat16), value_ref[:, columns], preferred_element_type=jnp.float32
-        )
-        out_ref[:rows, head_columns(place)] = (summed * (1.0 / total)).astype(jnp.bfloat16)
-        chosen = (lane == place) | (lane == place + HALF)
-        tops = jnp.where(chosen, top, tops)
-        totals = jnp.where(chosen, total, totals)
-    put_logs(out_ref, tops + jnp.log(totals) * LOG2E)
-
-
-def merge(refs, out_ref, columns, log_ref=None):
-    rows = refs[0].shape[0] - TAIL
+        if late is not None:
+            finish(*late)
+        late = (head, expo.astype(jnp.bfloat16), total)
+        tops = jnp.where(lane == head, top, tops)
+        totals = jnp.where(lane == head, total, totals)
+    finish(*late)
+    logs = tops + jnp.log(totals) * LOG2E
+    lanes = padded_lanes(rows)
+    if lanes > rows:
+        logs = jnp.concatenate((logs, jnp.zeros((lanes - rows, 128), jnp.float32)), axis=0)
+    put_logs(out_ref, jnp.transpose(logs)[:HEADS])
+
+
+def merge(refs, put, log_ref=None):
+    rows = refs[0].shape[1] - TAIL
     logs = [get_logs(ref) for ref in refs]
     best = logs[0]
     for log in logs[1:]:
@@ -217,13 +238,27 @@
         put_logs(log_ref, best + jnp.log(total) * LOG2E)
     inverse = 1.0 / total
     factors = [factor * inverse for factor in factors]
-    for place in range(HALF):
-        terms = [
-            ref[:rows, head_columns(place)].astype(jnp.float32) * factor[:, place : place + 1]
-            for ref, factor in zip(refs, factors)
-        ]
-        joined = sum(terms[1:], terms[0]).astype(jnp.bfloat16)
-        out_ref[:rows, slice(columns + place * HD, columns + (place + 1) * HD)] = joined
+    missing = 128 - HEADS * len(factors)
+    factors.append(jnp.zeros((missing, factors[0].shape[1]), jnp.float32))
+    columns = jnp.transpose(jnp.concatenate(factors, axis=0))[:rows]
+    for head in range(HEADS):
+        half, place = head_place(head)
+        joined = None
+        for which, ref in enumerate(refs):
+            lane = which * HEADS + head
+            term = ref[half, :rows, place].astype(jnp.float32) * columns[:, lane : lane + 1]
+            joined = term if joined is None else joined + term
+        put(head, joined.astype(jnp.bfloat16))
+
+
+def merge_packed(refs, out_ref):
+    rows = out_ref.shape[1] - TAIL
+
+    def put(head, block):
+        half, place = head_place(head)
+        out_ref[half, :rows, place] = block
+
+    merge(refs, put, out_ref)
 
 
 def is_outer():
@@ -240,8 +275,7 @@
 
 
 def whole_kernel(filled_ref, query_ref, key_ref, value_ref, out_ref):
-    for half in range(2):
-        attend(query_ref, key_ref, value_ref, filled_ref, half, out_ref.at[half])
+    attend(query_ref, key_ref, value_ref, filled_ref, out_ref)
 
 
 def outer_kernel(*refs):
@@ -272,8 +306,7 @@
 def meet_kernel(own_ref, other_ref, out_ref):
     @when_inner
     def _():
-        for half in range(2):
-            merge((own_ref.at[half], other_ref.at[half]), out_ref.at[half], 0, out_ref.at[half])
+        merge_packed((own_ref, other_ref), out_ref)
 
 
 def join_kernel(own_ref, other_ref, out_ref):
@@ -283,21 +316,20 @@
 
     @when_inner
     def _():
-        for half in range(2):
-            merge((own_ref.at[half], other_ref.at[half]), out_ref.at[half], 0, out_ref.at[half])
+        merge_packed((own_ref, other_ref), out_ref)
 
 
 def closing_kernel(own_ref, side_ref, middle_ref, out_ref):
+    def put(head, block):
+        out_ref[:, head_columns(head)] = block
+
     @when_outer
     def _():
-        for half in range(2):
-            merge((own_ref.at[half], side_ref.at[half]), out_ref, half * HALF_WIDTH)
+        merge((own_ref, side_ref), put)
 
     @when_inner
     def _():
-        for half in range(2):
-            parts = (own_ref.at[half], side_ref.at[half], middle_ref.at[half])
-            merge(parts, out_ref, half * HALF_WIDTH)
+        merge((own_ref, side_ref, middle_ref), put)
 
 
 def spans_kernel(home_ref, wanted_ref, cross_ref, *refs):

time: 68.9 us -> 67.1 us (0.974)
  Pallas kernels: 18.8 us -> 12.8 us
  waiting for transfers between devices: 24.2 us -> 28.6 us
    pallas_call x5, Pallas kernels: 9.75 us -> 4.48 us  [attention(): on_core(kernel, whole_part, [SMALL] + [WHOLE] * 3, name=name)]
    ppermute x9, waiting for transfers between devices: 21.8 us -> 26.7 us  [over_blk(): return lax.ppermute(block, 'blk', route)]
    ppermute x9, starting transfers between devices: 15.5 us -> 14.7 us  [over_blk(): return lax.ppermute(block, 'blk', route)]
  transfers between devices with their start and end apart: 14 -> 14, of which waited for: 9 -> 9; matrix products, arithmetic and copies ran while one was open for 0% -> 0% of each run, Pallas kernels for 25% -> 17%
where the time goes in v5:
time: 67.1 us; the launch traced here: 66.7 us
  waiting for transfers between devices  28.6 us (43%)
  starting transfers between devices  20.4 us (30%)
  Pallas kernels  12.8 us (19%)
  local copies, waits for them, and re-layouts  3.28 us (5%)
  between operations  1.46 us (2%)
    ppermute x9, waiting for transfers between devices, over_blk(): return lax.ppermute(block, 'blk', route)  26.7 us
    ppermute x9, starting transfers between devices, over_blk(): return lax.ppermute(block, 'blk', route)  14.7 us
    ppermute x5, starting transfers between devices, over_bank(): return lax.ppermute(block, 'bank', route)  5.73 us
    pallas_call x1, Pallas kernels, joint_pass(): on_core(spans_kernel, plain, [SMALL, SMALL, WHOLE] + [AWAY] * 4, scratch=...  4.88 us
    pallas_call x5, Pallas kernels, attention(): on_core(kernel, whole_part, [SMALL] + [WHOLE] * 3, name=name)  4.48 us
    unnamed x18, local copies, waits for them, and re-layouts  3.28 us
    ppermute x5, waiting for transfers between devices, over_bank(): return lax.ppermute(block, 'bank', route)  1.9 us
    pallas_call x1, Pallas kernels, joint_pass(): on_core(closing_kernel, plain, [WHOLE] * 3, name='closing')  1.59 us
  transfers between devices with their start and end apart: 14, of which 9 were waited for; matrix products, arithmetic and copies ran while one was open for 0% of the time, Pallas kernels for 17%

profile of v5, /device:TPU:8, one launch (start us, length us, event | category | flops | bytes accessed | tf_op | source)
XLA Modules:
  0.0 66.7 jit_solution(6714912996975275409)
XLA Ops:
  0.6 0.7 %collective-permute-start.1 = (bf16[192,1024]{1,0:T(8,128)(2,1)}, bf16[192,1024]{1,0:T(8,128)(2,1)S(1)}, u32[]{:S(2)}, u32[]{:S(2)}) collective-permute-start(bf16[192,1024]{1,0:T(8,128)(2,1)} %bitcast.25), channel_id=1, source_target_pairs={{0,3},{3,0},{4,7},{7,4},{8,11},{11,8},{12,15},{15,12},{16,19},{19,... | collective-permute-start | bytes 1179656 | tf_op jit(solution)/shard_map/ppermute | solution.py:415
  1.3 3.5 %collective-permute-start.2 = (bf16[192,1024]{1,0:T(8,128)(2,1)}, bf16[192,1024]{1,0:T(8,128)(2,1)S(1)}, u32[]{:S(2)}, u32[]{:S(2)}) collective-permute-start(bf16[192,1024]{1,0:T(8,128)(2,1)} %bitcast.26), channel_id=1, source_target_pairs={{1,2},{2,1},{5,6},{6,5},{9,10},{10,9},{13,14},{14,13},{17,18},{18,... | collective-permute-start | bytes 1179656 | tf_op jit(solution)/shard_map/ppermute | solution.py:415
  4.8 2.5 %collective-permute-start = (bf16[192,1024]{1,0:T(8,128)(2,1)}, bf16[192,1024]{1,0:T(8,128)(2,1)S(1)}, u32[]{:S(2)}, u32[]{:S(2)}) collective-permute-start(bf16[192,1024]{1,0:T(8,128)(2,1)} %bitcast.27), channel_id=1, source_target_pairs={{0,1},{1,0},{2,3},{3,2},{4,5},{5,4},{6,7},{7,6},{8,9},{9,8},{10,11... | collective-permute-start | bytes 1179656 | tf_op jit(solution)/shard_map/ppermute | solution.py:415
  8.0 0.0 copy-start
  8.0 1.1 %copy-done = bf16[1,384,1024]{2,1,0:T(8,128)(2,1)S(1)} copy-done((bf16[1,384,1024]{2,1,0:T(8,128)(2,1)S(1)}, bf16[1,384,1024]{2,1,0:T(8,128)(2,1)}, u32[]{:S(2)}) %copy-start) | copy-done | bytes 786456
  9.1 1.1 %copy-done.2 = bf16[1,384,1024]{2,1,0:T(8,128)(2,1)S(1)} copy-done((bf16[1,384,1024]{2,1,0:T(8,128)(2,1)S(1)}, bf16[1,384,1024]{2,1,0:T(8,128)(2,1)}, u32[]{:S(2)}) %copy-start.2) | copy-done | bytes 786456
  10.3 1.0 %copy-done.6 = bf16[1,192,1024]{2,1,0:T(8,128)(2,1)S(1)} copy-done((bf16[1,192,1024]{2,1,0:T(8,128)(2,1)S(1)}, bf16[1,192,1024]{2,1,0:T(8,128)(2,1)}, u32[]{:S(2)}) %copy-start.6) | copy-done | bytes 393240
  11.3 1.1 %own.1.own_ref = bf16[2,200,512]{2,1,0:T(8,128)(2,1)S(1)} custom-call(s32[1,1]{1,0:T(1,128)S(6)} %copy.10.filled_ref.refs_0_, bf16[192,1024]{1,0:T(8,128)(2,1)S(1)} %bitcast.28, bf16[384,1024]{1,0:T(8,128)(2,1)S(1)} %bitcast.12, bf16[384,1024]{1,0:T(8,128)(2,1)S(1)} %bitcast.18), custom_call_target="tpu_custom_call" | custom-call | flops 1 | bytes 1 | tf_op jit(solution)/shard_map/own/pallas_call | solution.py:422
  12.4 0.0 collective-permute-done.1.query_ref
  12.4 0.0 copy-done.4
  12.4 1.6 %collective-permute-start.3 = (bf16[2,64,2048]{2,1,0:T(8,128)(2,1)S(1)}, bf16[2,64,2048]{2,1,0:T(8,128)(2,1)S(1)}, u32[]{:S(2)}, u32[]{:S(2)}) collective-permute-start(bf16[2,64,2048]{2,1,0:T(8,128)(2,1)S(1)} %copy-done.4), channel_id=1, source_target_pairs={{0,8},{4,12},{8,0},{12,4},{16,24},{20,28},{24,16},{28,20},{1,9},{5... | collective-permute-start | bytes 1572872 | tf_op jit(solution)/shard_map/ppermute | solution.py:419
  13.9 1.5 %collective-permute-start.4 = (bf16[2,64,2048]{2,1,0:T(8,128)(2,1)S(1)}, bf16[2,64,2048]{2,1,0:T(8,128)(2,1)S(1)}, u32[]{:S(2)}, u32[]{:S(2)}) collective-permute-start(bf16[2,64,2048]{2,1,0:T(8,128)(2,1)S(1)} %copy-done.4), channel_id=1, source_target_pairs={{0,16},{4,20},{8,24},{12,28},{16,0},{20,4},{24,8},{28,12},{1,17},{... | collective-permute-start | bytes 1572872 | tf_op jit(solution)/shard_map/ppermute | solution.py:419
  15.5 7.2 %collective-permute-done.2.middle_ref.refs_1_ = bf16[192,1024]{1,0:T(8,128)(2,1)S(1)} collective-permute-done((bf16[192,1024]{1,0:T(8,128)(2,1)}, bf16[192,1024]{1,0:T(8,128)(2,1)S(1)}, u32[]{:S(2)}, u32[]{:S(2)}) %collective-permute-start.2) | collective-permute-done | bytes 393248 | tf_op jit(solution)/shard_map/ppermute | solution.py:415
  22.7 0.0 copy-done.3
  22.7 0.1 collective-permute-start.5
  22.8 1.3 %collective-permute-done.query_ref = bf16[192,1024]{1,0:T(8,128)(2,1)S(1)} collective-permute-done((bf16[192,1024]{1,0:T(8,128)(2,1)}, bf16[192,1024]{1,0:T(8,128)(2,1)S(1)}, u32[]{:S(2)}, u32[]{:S(2)}) %collective-permute-start) | collective-permute-done | bytes 393248 | tf_op jit(solution)/shard_map/ppermute | solution.py:415
  24.1 2.2 %collective-permute-start.6 = (bf16[192,1024]{1,0:T(8,128)(2,1)S(1)}, bf16[192,1024]{1,0:T(8,128)(2,1)S(1)}, u32[]{:S(2)}, u32[]{:S(2)}) collective-permute-start(bf16[192,1024]{1,0:T(8,128)(2,1)S(1)} %collective-permute-done.query_ref), channel_id=1, source_target_pairs={{1,2},{2,1},{5,6},{6,5},{9,10},{10,9},{13,14},{14,13},{17,18},{18,... | collective-permute-start | bytes 1179656 | tf_op jit(solution)/shard_map/ppermute | solution.py:415
  26.3 0.0 collective-permute-done.3
  26.3 0.4 collective-permute-done.4
  26.8 2.1 %collective-permute-start.10 = (bf16[2,64,2048]{2,1,0:T(8,128)(2,1)S(1)}, bf16[2,64,2048]{2,1,0:T(8,128)(2,1)S(1)}, u32[]{:S(2)}, u32[]{:S(2)}) collective-permute-start(bf16[2,64,2048]{2,1,0:T(8,128)(2,1)S(1)} %copy-done.4), channel_id=1, source_target_pairs={{0,24},{4,28},{8,16},{12,20},{16,8},{20,12},{24,0},{28,4},{1,25},{... | collective-permute-start | bytes 1572872 | tf_op jit(solution)/shard_map/ppermute | solution.py:419
  28.9 1.1 %side.1.own_ref = bf16[2,200,512]{2,1,0:T(8,128)(2,1)S(1)} custom-call(s32[1,1]{1,0:T(1,128)S(6)} %copy.10.filled_ref.refs_0_, bf16[192,1024]{1,0:T(8,128)(2,1)S(1)} %collective-permute-done.query_ref, bf16[384,1024]{1,0:T(8,128)(2,1)S(1)} %bitcast.14, bf16[384,1024]{1,0:T(8,128)(2,1)S(1)} %bitcast.20), custom_call_target="tpu_custom_call" | custom-call | flops 1 | bytes 1 | tf_op jit(solution)/shard_map/side/pallas_call | solution.py:422
  30.0 1.1 %middle.1.own_ref = bf16[2,200,512]{2,1,0:T(8,128)(2,1)S(1)} custom-call(s32[1,1]{1,0:T(1,128)S(6)} %copy.10.filled_ref.refs_0_, bf16[192,1024]{1,0:T(8,128)(2,1)S(1)} %collective-permute-done.2.middle_ref.refs_1_, bf16[384,1024]{1,0:T(8,128)(2,1)S(1)} %bitcast.15, bf16[384,1024]{1,0:T(8,128)(2,1)S(1)} %bitcast.21), custom_call_target="tpu_custom_call" | custom-call | flops 1 | bytes 1 | tf_op jit(solution)/shard_map/middle/pallas_call | solution.py:422
  31.1 4.9 %collective-permute-done.6.refs_1_ = bf16[192,1024]{1,0:T(8,128)(2,1)S(1)} collective-permute-done((bf16[192,1024]{1,0:T(8,128)(2,1)S(1)}, bf16[192,1024]{1,0:T(8,128)(2,1)S(1)}, u32[]{:S(2)}, u32[]{:S(2)}) %collective-permute-start.6) | collective-permute-done | bytes 393248 | tf_op jit(solution)/shard_map/ppermute | solution.py:415
  36.0 0.0 collective-permute-done.5.refs_1_.other_ref
  36.0 1.3 %collective-permute-start.7 = (bf16[2,200,512]{2,1,0:T(8,128)(2,1)S(1)}, bf16[2,200,512]{2,1,0:T(8,128)(2,1)S(1)}, u32[]{:S(2)}, u32[]{:S(2)}) collective-permute-start(bf16[2,200,512]{2,1,0:T(8,128)(2,1)S(1)} %turned.1), channel_id=1, source_target_pairs={{0,1},{3,2},{4,5},{7,6},{8,9},{11,10},{12,13},{15,14},{16,17},{19,... | collective-permute-start | bytes 1228808 | tf_op jit(solution)/shard_map/ppermute | solution.py:415
  37.3 1.1 %passed.1.own_ref = bf16[2,200,512]{2,1,0:T(8,128)(2,1)S(1)} custom-call(s32[1,1]{1,0:T(1,128)S(6)} %copy.10.filled_ref.refs_0_, bf16[192,1024]{1,0:T(8,128)(2,1)S(1)} %collective-permute-done.6.refs_1_, bf16[384,1024]{1,0:T(8,128)(2,1)S(1)} %bitcast.17, bf16[384,1024]{1,0:T(8,128)(2,1)S(1)} %bitcast.23), custom_call_target="tpu_custom_call" | custom-call | flops 1 | bytes 1 | tf_op jit(solution)/shard_map/passed/pallas_call | solution.py:422
  38.4 0.6 met.1
  39.0 2.2 %collective-permute-start.8 = (bf16[2,200,512]{2,1,0:T(8,128)(2,1)S(1)}, bf16[2,200,512]{2,1,0:T(8,128)(2,1)S(1)}, u32[]{:S(2)}, u32[]{:S(2)}) collective-permute-start(bf16[2,200,512]{2,1,0:T(8,128)(2,1)S(1)} %met.1), channel_id=1, source_target_pairs={{1,2},{2,1},{5,6},{6,5},{9,10},{10,9},{13,14},{14,13},{17,18},{18,... | collective-permute-start | bytes 1228808 | tf_op jit(solution)/shard_map/ppermute | solution.py:415
  41.2 6.1 %collective-permute-done.7.other_ref = bf16[2,200,512]{2,1,0:T(8,128)(2,1)S(1)} collective-permute-done((bf16[2,200,512]{2,1,0:T(8,128)(2,1)S(1)}, bf16[2,200,512]{2,1,0:T(8,128)(2,1)S(1)}, u32[]{:S(2)}, u32[]{:S(2)}) %collective-permute-start.7) | collective-permute-done | bytes 409632 | tf_op jit(solution)/shard_map/ppermute | solution.py:415
  47.3 0.6 join.2
  47.9 2.4 %collective-permute-done.8.other_ref = bf16[2,200,512]{2,1,0:T(8,128)(2,1)S(1)} collective-permute-done((bf16[2,200,512]{2,1,0:T(8,128)(2,1)S(1)}, bf16[2,200,512]{2,1,0:T(8,128)(2,1)S(1)}, u32[]{:S(2)}, u32[]{:S(2)}) %collective-permute-start.8) | collective-permute-done | bytes 409632 | tf_op jit(solution)/shard_map/ppermute | solution.py:415
  50.4 0.6 join.3
  51.0 0.0 collective-permute-done.10
  51.0 0.0 copy-start.5
  51.0 0.0 copy-start.7
  51.0 0.0 copy-start.8
  51.0 0.2 pad_maximum_fusion.refs_2_
  51.2 0.1 collective-permute-start.11
  51.3 0.5 collective-permute-start.9
  51.8 0.0 collective-permute-start.12
  51.8 2.2 %collective-permute-start.13 = (bf16[2,200,512]{2,1,0:T(8,128)(2,1)S(1)}, bf16[2,200,512]{2,1,0:T(8,128)(2,1)S(1)}, u32[]{:S(2)}, u32[]{:S(2)}) collective-permute-start(bf16[2,200,512]{2,1,0:T(8,128)(2,1)S(1)} %join.2), channel_id=1, source_target_pairs={{1,2},{2,1},{5,6},{6,5},{9,10},{10,9},{13,14},{14,13},{17,18},{18,... | collective-permute-start | bytes 1228808 | tf_op jit(solution)/shard_map/ppermute | solution.py:415
  54.0 1.4 %collective-permute-done.9.refs_1_ = bf16[2,64,2048]{2,1,0:T(8,128)(2,1)S(1)} collective-permute-done((bf16[2,64,2048]{2,1,0:T(8,128)(2,1)S(1)}, bf16[2,64,2048]{2,1,0:T(8,128)(2,1)S(1)}, u32[]{:S(2)}, u32[]{:S(2)}) %collective-permute-start.9) | collective-permute-done | bytes 524320 | tf_op jit(solution)/shard_map/ppermute | solution.py:419
  55.4 0.0 collective-permute-done.11.refs_3_
  55.4 0.0 copy-done.7
  55.4 4.9 %spans.1 = bf16[192,1024]{1,0:T(8,128)(2,1)} custom-call(s32[16]{0:T(128)S(1)} %copy-done.8, s32[2,12]{1,0:T(2,128)S(1)} %bitcast.29, bf16[192,1024]{1,0:T(8,128)(2,1)S(1)} %bitcast.24, bf16[2,64,2048]{2,1,0:T(8,128)(2,1)S(1)} %copy-done.4, bf16[2,64,2048]{2,1,0:T(8,128)(2,1)S(1)} %collective-permute-done.9.refs_1_, ...), custom_call_target="tpu_custom_call" | custom-call | flops 1 | bytes 1 | tf_op jit(solution)/shard_map/spans/pallas_call | solution.py:458
  60.3 2.9 %collective-permute-done.12.side_ref = bf16[2,200,512]{2,1,0:T(8,128)(2,1)S(1)} collective-permute-done((bf16[2,200,512]{2,1,0:T(8,128)(2,1)S(1)}, bf16[2,200,512]{2,1,0:T(8,128)(2,1)S(1)}, u32[]{:S(2)}, u32[]{:S(2)}) %collective-permute-start.12) | collective-permute-done | bytes 409632 | tf_op jit(solution)/shard_map/ppermute | solution.py:415
  63.2 1.9 %collective-permute-done.13.middle_ref = bf16[2,200,512]{2,1,0:T(8,128)(2,1)S(1)} collective-permute-done((bf16[2,200,512]{2,1,0:T(8,128)(2,1)S(1)}, bf16[2,200,512]{2,1,0:T(8,128)(2,1)S(1)}, u32[]{:S(2)}, u32[]{:S(2)}) %collective-permute-start.13) | collective-permute-done | bytes 409632 | tf_op jit(solution)/shard_map/ppermute | solution.py:415
  65.1 1.6 %closing.1 = bf16[192,1024]{1,0:T(8,128)(2,1)} custom-call(bf16[2,200,512]{2,1,0:T(8,128)(2,1)S(1)} %own.1.own_ref, bf16[2,200,512]{2,1,0:T(8,128)(2,1)S(1)} %collective-permute-done.12.side_ref, bf16[2,200,512]{2,1,0:T(8,128)(2,1)S(1)} %collective-permute-done.13.middle_ref), custom_call_target="tpu_custom_call" | custom-call | flops 1 | bytes 1 | tf_op jit(solution)/shard_map/closing/pallas_call | solution.py:465
  (10 shorter events, 0.0 us)
Async XLA Ops:
  0.6 11.8 %collective-permute-start.1 = (bf16[192,1024]{1,0:T(8,128)(2,1)}, bf16[192,1024]{1,0:T(8,128)(2,1)S(1)}, u32[]{:S(2)}, u32[]{:S(2)}) collective-permute-start(bf16[192,1024]{1,0:T(8,128)(2,1)} %bitcast.25), channel_id=1, source_target_pairs={{0,3},{3,0},{4,7},{7,4},{8,11},{11,8},{12,15},{15,12},{16,19},{19,... | collective-permute-start | bytes 1179656 | tf_op jit(solution)/shard_map/ppermute | solution.py:415
  1.3 21.4 %collective-permute-start.2 = (bf16[192,1024]{1,0:T(8,128)(2,1)}, bf16[192,1024]{1,0:T(8,128)(2,1)S(1)}, u32[]{:S(2)}, u32[]{:S(2)}) collective-permute-start(bf16[192,1024]{1,0:T(8,128)(2,1)} %bitcast.26), channel_id=1, source_target_pairs={{1,2},{2,1},{5,6},{6,5},{9,10},{10,9},{13,14},{14,13},{17,18},{18,... | collective-permute-start | bytes 1179656 | tf_op jit(solution)/shard_map/ppermute | solution.py:415
  4.8 19.3 %collective-permute-start = (bf16[192,1024]{1,0:T(8,128)(2,1)}, bf16[192,1024]{1,0:T(8,128)(2,1)S(1)}, u32[]{:S(2)}, u32[]{:S(2)}) collective-permute-start(bf16[192,1024]{1,0:T(8,128)(2,1)} %bitcast.27), channel_id=1, source_target_pairs={{0,1},{1,0},{2,3},{3,2},{4,5},{5,4},{6,7},{7,6},{8,9},{9,8},{10,11... | collective-permute-start | bytes 1179656 | tf_op jit(solution)/shard_map/ppermute | solution.py:415
  8.0 1.1 %copy-start = (bf16[1,384,1024]{2,1,0:T(8,128)(2,1)S(1)}, bf16[1,384,1024]{2,1,0:T(8,128)(2,1)}, u32[]{:S(2)}) copy-start(bf16[1,384,1024]{2,1,0:T(8,128)(2,1)} %param.9) | copy-start | bytes 2359300
  9.1 1.1 %copy-start.2 = (bf16[1,384,1024]{2,1,0:T(8,128)(2,1)S(1)}, bf16[1,384,1024]{2,1,0:T(8,128)(2,1)}, u32[]{:S(2)}) copy-start(bf16[1,384,1024]{2,1,0:T(8,128)(2,1)} %param.10) | copy-start | bytes 2359300
  10.3 1.0 %copy-start.6 = (bf16[1,192,1024]{2,1,0:T(8,128)(2,1)S(1)}, bf16[1,192,1024]{2,1,0:T(8,128)(2,1)}, u32[]{:S(2)}) copy-start(bf16[1,192,1024]{2,1,0:T(8,128)(2,1)} %param.8) | copy-start | bytes 1179652
  11.3 1.1 %copy-start.4 = (bf16[2,64,2048]{2,1,0:T(8,128)(2,1)S(1)}, bf16[2,64,2048]{2,1,0:T(8,128)(2,1)}, u32[]{:S(2)}) copy-start(bf16[2,64,2048]{2,1,0:T(8,128)(2,1)} %refs_0_.4) | copy-start | bytes 1572868
  11.3 11.4 %copy-start.1 = (bf16[1,384,1024]{2,1,0:T(8,128)(2,1)S(1)}, bf16[1,384,1024]{2,1,0:T(8,128)(2,1)}, u32[]{:S(2)}) copy-start(bf16[1,384,1024]{2,1,0:T(8,128)(2,1)} %param.9) | copy-start | bytes 2359300
  11.3 11.4 %copy-start.3 = (bf16[1,384,1024]{2,1,0:T(8,128)(2,1)S(1)}, bf16[1,384,1024]{2,1,0:T(8,128)(2,1)}, u32[]{:S(2)}) copy-start(bf16[1,384,1024]{2,1,0:T(8,128)(2,1)} %param.10) | copy-start | bytes 2359300
  12.4 13.9 %collective-permute-start.3 = (bf16[2,64,2048]{2,1,0:T(8,128)(2,1)S(1)}, bf16[2,64,2048]{2,1,0:T(8,128)(2,1)S(1)}, u32[]{:S(2)}, u32[]{:S(2)}) collective-permute-start(bf16[2,64,2048]{2,1,0:T(8,128)(2,1)S(1)} %copy-done.4), channel_id=1, source_target_pairs={{0,8},{4,12},{8,0},{12,4},{16,24},{20,28},{24,16},{28,20},{1,9},{5... | collective-permute-start | bytes 1572872 | tf_op jit(solution)/shard_map/ppermute | solution.py:419
  13.9 12.8 %collective-permute-start.4 = (bf16[2,64,2048]{2,1,0:T(8,128)(2,1)S(1)}, bf16[2,64,2048]{2,1,0:T(8,128)(2,1)S(1)}, u32[]{:S(2)}, u32[]{:S(2)}) collective-permute-start(bf16[2,64,2048]{2,1,0:T(8,128)(2,1)S(1)} %copy-done.4), channel_id=1, source_target_pairs={{0,16},{4,20},{8,24},{12,28},{16,0},{20,4},{24,8},{28,12},{1,17},{... | collective-permute-start | bytes 1572872 | tf_op jit(solution)/shard_map/ppermute | solution.py:419
  22.7 13.2 %collective-permute-start.5 = (bf16[2,200,512]{2,1,0:T(8,128)(2,1)S(1)}, bf16[2,200,512]{2,1,0:T(8,128)(2,1)S(1)}, u32[]{:S(2)}, u32[]{:S(2)}) collective-permute-start(bf16[2,200,512]{2,1,0:T(8,128)(2,1)S(1)} %far.1), channel_id=1, source_target_pairs={{0,1},{1,0},{2,3},{3,2},{4,5},{5,4},{6,7},{7,6},{8,9},{9,8},{10,11... | collective-permute-start | bytes 1228808 | tf_op jit(solution)/shard_map/ppermute | solution.py:415
  24.1 11.9 %collective-permute-start.6 = (bf16[192,1024]{1,0:T(8,128)(2,1)S(1)}, bf16[192,1024]{1,0:T(8,128)(2,1)S(1)}, u32[]{:S(2)}, u32[]{:S(2)}) collective-permute-start(bf16[192,1024]{1,0:T(8,128)(2,1)S(1)} %collective-permute-done.query_ref), channel_id=1, source_target_pairs={{1,2},{2,1},{5,6},{6,5},{9,10},{10,9},{13,14},{14,13},{17,18},{18,... | collective-permute-start | bytes 1179656 | tf_op jit(solution)/shard_map/ppermute | solution.py:415
  26.8 24.2 %collective-permute-start.10 = (bf16[2,64,2048]{2,1,0:T(8,128)(2,1)S(1)}, bf16[2,64,2048]{2,1,0:T(8,128)(2,1)S(1)}, u32[]{:S(2)}, u32[]{:S(2)}) collective-permute-start(bf16[2,64,2048]{2,1,0:T(8,128)(2,1)S(1)} %copy-done.4), channel_id=1, source_target_pairs={{0,24},{4,28},{8,16},{12,20},{16,8},{20,12},{24,0},{28,4},{1,25},{... | collective-permute-start | bytes 1572872 | tf_op jit(solution)/shard_map/ppermute | solution.py:419
  36.0 11.3 %collective-permute-start.7 = (bf16[2,200,512]{2,1,0:T(8,128)(2,1)S(1)}, bf16[2,200,512]{2,1,0:T(8,128)(2,1)S(1)}, u32[]{:S(2)}, u32[]{:S(2)}) collective-permute-start(bf16[2,200,512]{2,1,0:T(8,128)(2,1)S(1)} %turned.1), channel_id=1, source_target_pairs={{0,1},{3,2},{4,5},{7,6},{8,9},{11,10},{12,13},{15,14},{16,17},{19,... | collective-permute-start | bytes 1228808 | tf_op jit(solution)/shard_map/ppermute | solution.py:415
  39.0 11.3 %collective-permute-start.8 = (bf16[2,200,512]{2,1,0:T(8,128)(2,1)S(1)}, bf16[2,200,512]{2,1,0:T(8,128)(2,1)S(1)}, u32[]{:S(2)}, u32[]{:S(2)}) collective-permute-start(bf16[2,200,512]{2,1,0:T(8,128)(2,1)S(1)} %met.1), channel_id=1, source_target_pairs={{1,2},{2,1},{5,6},{6,5},{9,10},{10,9},{13,14},{14,13},{17,18},{18,... | collective-permute-start | bytes 1228808 | tf_op jit(solution)/shard_map/ppermute | solution.py:415
  51.0 4.4 %copy-start.5 = (bf16[1,192,1024]{2,1,0:T(8,128)(2,1)S(1)}, bf16[1,192,1024]{2,1,0:T(8,128)(2,1)}, u32[]{:S(2)}) copy-start(bf16[1,192,1024]{2,1,0:T(8,128)(2,1)} %param.12) | copy-start | bytes 1179652
  51.0 4.4 %copy-start.7 = (s32[1,12,2]{1,2,0:T(2,128)S(1)}, s32[1,12,2]{1,2,0:T(2,128)}, u32[]{:S(2)}) copy-start(s32[1,12,2]{1,2,0:T(2,128)} %param.15) | copy-start | bytes 292
  51.0 4.4 %copy-start.8 = (s32[16]{0:T(128)S(1)}, s32[16]{0:T(128)}, u32[]{:S(2)}) copy-start(s32[16]{0:T(128)} %home_ref.1) | copy-start | bytes 196
  51.2 4.2 %collective-permute-start.11 = (bf16[3,2,64,2048]{3,2,1,0:T(8,128)(2,1)S(1)}, bf16[3,2,64,2048]{3,2,1,0:T(8,128)(2,1)S(1)}, u32[]{:S(2)}, u32[]{:S(2)}) collective-permute-start(bf16[3,2,64,2048]{3,2,1,0:T(8,128)(2,1)S(1)} %pad_maximum_fusion.refs_2_), channel_id=1, source_target_pairs={{0,4},{4,0},{8,12},{12,8},{16,20},{20,16},{24,28},{28,24},{1,5},{5... | collective-permute-start | bytes 4718600 | tf_op jit(solution)/shard_map/ppermute | solution.py:419
  51.3 4.1 %collective-permute-start.9 = (bf16[2,64,2048]{2,1,0:T(8,128)(2,1)S(1)}, bf16[2,64,2048]{2,1,0:T(8,128)(2,1)S(1)}, u32[]{:S(2)}, u32[]{:S(2)}) collective-permute-start(bf16[2,64,2048]{2,1,0:T(8,128)(2,1)S(1)} %copy-done.4), channel_id=1, source_target_pairs={{0,4},{4,0},{8,12},{12,8},{16,20},{20,16},{24,28},{28,24},{1,5},{5... | collective-permute-start | bytes 1572872 | tf_op jit(solution)/shard_map/ppermute | solution.py:419
  51.8 11.4 %collective-permute-start.12 = (bf16[2,200,512]{2,1,0:T(8,128)(2,1)S(1)}, bf16[2,200,512]{2,1,0:T(8,128)(2,1)S(1)}, u32[]{:S(2)}, u32[]{:S(2)}) collective-permute-start(bf16[2,200,512]{2,1,0:T(8,128)(2,1)S(1)} %join.3), channel_id=1, source_target_pairs={{0,1},{1,0},{2,3},{3,2},{4,5},{5,4},{6,7},{7,6},{8,9},{9,8},{10,11... | collective-permute-start | bytes 1228808 | tf_op jit(solution)/shard_map/ppermute | solution.py:415
  51.8 13.3 %collective-permute-start.13 = (bf16[2,200,512]{2,1,0:T(8,128)(2,1)S(1)}, bf16[2,200,512]{2,1,0:T(8,128)(2,1)S(1)}, u32[]{:S(2)}, u32[]{:S(2)}) collective-permute-start(bf16[2,200,512]{2,1,0:T(8,128)(2,1)S(1)} %join.2), channel_id=1, source_target_pairs={{1,2},{2,1},{5,6},{6,5},{9,10},{10,9},{13,14},{14,13},{17,18},{18,... | collective-permute-start | bytes 1228808 | tf_op jit(solution)/shard_map/ppermute | solution.py:415

commit v6 on v5

--- a/solution.py
+++ b/solution.py
@@ -319,24 +319,30 @@
         merge_packed((own_ref, other_ref), out_ref)
 
 
-def closing_kernel(own_ref, side_ref, middle_ref, out_ref):
+def near_kernel(own_ref, side_ref, out_ref):
+    merge_packed((own_ref, side_ref), out_ref)
+
+
+def closing_kernel(near_ref, middle_ref, out_ref):
     def put(head, block):
         out_ref[:, head_columns(head)] = block
 
     @when_outer
     def _():
-        merge((own_ref, side_ref), put)
+        for head in range(HEADS):
+            half, place = head_place(head)
+            put(head, near_ref[half, : out_ref.shape[0], place])
 
     @when_inner
     def _():
-        merge((own_ref, side_ref, middle_ref), put)
+        merge((near_ref, middle_ref), put)
 
 
 def spans_kernel(home_ref, wanted_ref, cross_ref, *refs):
-    own_ref, core_ref, others_ref, core_others_ref, out_ref, bank_ref, arrivals = refs
-    sources = [own_ref, core_ref]
-    for place in range(3):
-        sources += [others_ref.at[place], core_others_ref.at[place]]
+    same_ref, other_ref, out_ref, bank_ref, arrivals = refs
+    sources = []
+    for place in range(4):
+        sources += [same_ref.at[place], other_ref.at[place]]
     spans = wanted_ref.shape[1]
     held = bank_ref.shape[1]
     width = cross_ref.shape[1]
@@ -449,22 +455,21 @@
     join = on_core(join_kernel, whole_part, [WHOLE] * 2, name="join")
     to_middle = join(middle_part, from_outer)
     home_middle = over_blk(to_middle, *swap_middle)
-    to_side = join(after(side_part, to_middle), from_middle)
+    stacked = jnp.stack((bank_kv, bank_x, bank_y, bank_xy))
+    to_side = join(after(side_part, to_middle, stacked), from_middle)
     home_side = over_blk(to_side, *swap_side)
-    core_c = over_bank(after(bank_kv, met), 1)
-    others = after(jnp.stack((bank_x, bank_y, bank_xy)), to_side)
+    others = after(stacked, to_side)
     core_others = over_bank(others, 1)
 
     retrieved = on_core(
         spans_kernel,
         plain,
-        [SMALL, SMALL, WHOLE] + [AWAY] * 4,
+        [SMALL, SMALL, WHOLE] + [AWAY] * 2,
         scratch=(pltpu.VMEM((8, *bank_kv.shape), bank_kv.dtype), pltpu.SemaphoreType.DMA((8,))),
         name="spans",
-    )(span_home, wanted.T, after(cross, to_side), bank_kv, core_c, others, core_others)
-    context = on_core(closing_kernel, plain, [WHOLE] * 3, name="closing")(
-        after(own, retrieved), home_side, home_middle
-    )
+    )(span_home, wanted.T, after(cross, to_side), stacked, core_others)
+    partly = on_core(near_kernel, whole_part, [WHOLE] * 2, name="near")(after(own, retrieved), home_side)
+    context = on_core(closing_kernel, plain, [WHOLE] * 2, name="closing")(partly, home_middle)
     return context, retrieved
 
 

time: 67.1 us -> 66.5 us (level)
  waiting for transfers between devices: 28.6 us -> 27.8 us
    ppermute x9, waiting for transfers between devices: 26.7 us -> 25.7 us  [over_blk(): return lax.ppermute(block, 'blk', route)]
    ppermute x5 -> x4, starting transfers between devices: 5.73 us -> 5.21 us  [over_bank(): return lax.ppermute(block, 'bank', route)]
    pallas_call x3 -> x4, Pallas kernels: 7.07 us -> 7.45 us  [the longest x1 4.88 us: joint_pass(): on_core(spans_kernel, plain, [SMALL, SMALL, WHOLE] + [AWAY] * 2, scratch=...]
    ppermute x5 -> x4, waiting for transfers between devices: 1.9 us -> 2.16 us  [over_bank(): return lax.ppermute(block, 'bank', route)]
  transfers between devices with their start and end apart: 14 -> 13, of which waited for: 9 -> 9; matrix products, arithmetic and copies ran while one was open for 0% -> 0% of each run, Pallas kernels for 17% -> 17%
where the time goes in v6:
time: 66.5 us; the launch traced here: 66.2 us
  waiting for transfers between devices  27.8 us (42%)
  starting transfers between devices  20.2 us (30%)
  Pallas kernels  13.2 us (20%)
  local copies, waits for them, and re-layouts  3.28 us (5%)
  between operations  1.47 us (2%)
    ppermute x9, waiting for transfers between devices, over_blk(): return lax.ppermute(block, 'blk', route)  25.7 us
    ppermute x9, starting transfers between devices, over_blk(): return lax.ppermute(block, 'blk', route)  15 us
    ppermute x4, starting transfers between devices, over_bank(): return lax.ppermute(block, 'bank', route)  5.21 us
    pallas_call x1, Pallas kernels, joint_pass(): on_core(spans_kernel, plain, [SMALL, SMALL, WHOLE] + [AWAY] * 2, scratch=...  4.88 us
    pallas_call x5, Pallas kernels, attention(): on_core(kernel, whole_part, [SMALL] + [WHOLE] * 3, name=name)  4.46 us
    unnamed x18, local copies, waits for them, and re-layouts  3.28 us
    ppermute x4, waiting for transfers between devices, over_bank(): return lax.ppermute(block, 'bank', route)  2.16 us
    pallas_call x1, Pallas kernels, joint_pass(): on_core(closing_kernel, plain, [WHOLE] * 2, name='closing')  1.36 us
  transfers between devices with their start and end apart: 13, of which 9 were waited for; matrix products, arithmetic and copies ran while one was open for 0% of the time, Pallas kernels for 17%

profile of v6, /device:TPU:8, one launch (start us, length us, event | category | flops | bytes accessed | tf_op | source)
XLA Modules:
  0.0 66.2 jit_solution(17671358613768720329)
XLA Ops:
  0.6 0.7 %collective-permute-start.1 = (bf16[192,1024]{1,0:T(8,128)(2,1)}, bf16[192,1024]{1,0:T(8,128)(2,1)S(1)}, u32[]{:S(2)}, u32[]{:S(2)}) collective-permute-start(bf16[192,1024]{1,0:T(8,128)(2,1)} %bitcast.26), channel_id=1, source_target_pairs={{0,3},{3,0},{4,7},{7,4},{8,11},{11,8},{12,15},{15,12},{16,19},{19,... | collective-permute-start | bytes 1179656 | tf_op jit(solution)/shard_map/ppermute | solution.py:421
  1.3 3.5 %collective-permute-start.2 = (bf16[192,1024]{1,0:T(8,128)(2,1)}, bf16[192,1024]{1,0:T(8,128)(2,1)S(1)}, u32[]{:S(2)}, u32[]{:S(2)}) collective-permute-start(bf16[192,1024]{1,0:T(8,128)(2,1)} %bitcast.27), channel_id=1, source_target_pairs={{1,2},{2,1},{5,6},{6,5},{9,10},{10,9},{13,14},{14,13},{17,18},{18,... | collective-permute-start | bytes 1179656 | tf_op jit(solution)/shard_map/ppermute | solution.py:421
  4.8 2.5 %collective-permute-start = (bf16[192,1024]{1,0:T(8,128)(2,1)}, bf16[192,1024]{1,0:T(8,128)(2,1)S(1)}, u32[]{:S(2)}, u32[]{:S(2)}) collective-permute-start(bf16[192,1024]{1,0:T(8,128)(2,1)} %bitcast.28), channel_id=1, source_target_pairs={{0,1},{1,0},{2,3},{3,2},{4,5},{5,4},{6,7},{7,6},{8,9},{9,8},{10,11... | collective-permute-start | bytes 1179656 | tf_op jit(solution)/shard_map/ppermute | solution.py:421
  8.0 0.0 copy-start
  8.0 1.1 %copy-done = bf16[1,384,1024]{2,1,0:T(8,128)(2,1)S(1)} copy-done((bf16[1,384,1024]{2,1,0:T(8,128)(2,1)S(1)}, bf16[1,384,1024]{2,1,0:T(8,128)(2,1)}, u32[]{:S(2)}) %copy-start) | copy-done | bytes 786456
  9.1 1.1 %copy-done.2 = bf16[1,384,1024]{2,1,0:T(8,128)(2,1)S(1)} copy-done((bf16[1,384,1024]{2,1,0:T(8,128)(2,1)S(1)}, bf16[1,384,1024]{2,1,0:T(8,128)(2,1)}, u32[]{:S(2)}) %copy-start.2) | copy-done | bytes 786456
  10.3 1.0 %copy-done.5 = bf16[1,192,1024]{2,1,0:T(8,128)(2,1)S(1)} copy-done((bf16[1,192,1024]{2,1,0:T(8,128)(2,1)S(1)}, bf16[1,192,1024]{2,1,0:T(8,128)(2,1)}, u32[]{:S(2)}) %copy-start.5) | copy-done | bytes 393240
  11.3 1.1 %own.1.own_ref = bf16[2,200,512]{2,1,0:T(8,128)(2,1)S(1)} custom-call(s32[1,1]{1,0:T(1,128)S(6)} %copy.10.filled_ref.refs_0_, bf16[192,1024]{1,0:T(8,128)(2,1)S(1)} %bitcast.29, bf16[384,1024]{1,0:T(8,128)(2,1)S(1)} %bitcast.13, bf16[384,1024]{1,0:T(8,128)(2,1)S(1)} %bitcast.19), custom_call_target="tpu_custom_call" | custom-call | flops 1 | bytes 1 | tf_op jit(solution)/shard_map/own/pallas_call | solution.py:428
  12.4 0.0 collective-permute-done.1.query_ref
  12.4 0.0 copy-done.8
  12.4 1.6 %collective-permute-start.4 = (bf16[2,64,2048]{2,1,0:T(8,128)(2,1)S(1)}, bf16[2,64,2048]{2,1,0:T(8,128)(2,1)S(1)}, u32[]{:S(2)}, u32[]{:S(2)}) collective-permute-start(bf16[2,64,2048]{2,1,0:T(8,128)(2,1)S(1)} %copy-done.8), channel_id=1, source_target_pairs={{0,16},{4,20},{8,24},{12,28},{16,0},{20,4},{24,8},{28,12},{1,17},{... | collective-permute-start | bytes 1572872 | tf_op jit(solution)/shard_map/ppermute | solution.py:425
  14.0 1.5 %collective-permute-start.3 = (bf16[2,64,2048]{2,1,0:T(8,128)(2,1)S(1)}, bf16[2,64,2048]{2,1,0:T(8,128)(2,1)S(1)}, u32[]{:S(2)}, u32[]{:S(2)}) collective-permute-start(bf16[2,64,2048]{2,1,0:T(8,128)(2,1)S(1)} %copy-done.8), channel_id=1, source_target_pairs={{0,8},{4,12},{8,0},{12,4},{16,24},{20,28},{24,16},{28,20},{1,9},{5... | collective-permute-start | bytes 1572872 | tf_op jit(solution)/shard_map/ppermute | solution.py:425
  15.5 7.2 %collective-permute-done.2.middle_ref.refs_1_ = bf16[192,1024]{1,0:T(8,128)(2,1)S(1)} collective-permute-done((bf16[192,1024]{1,0:T(8,128)(2,1)}, bf16[192,1024]{1,0:T(8,128)(2,1)S(1)}, u32[]{:S(2)}, u32[]{:S(2)}) %collective-permute-start.2) | collective-permute-done | bytes 393248 | tf_op jit(solution)/shard_map/ppermute | solution.py:421
  22.7 0.0 copy-done.1
  22.7 0.0 copy-done.3
  22.7 0.1 collective-permute-start.5
  22.8 1.3 %collective-permute-done.query_ref = bf16[192,1024]{1,0:T(8,128)(2,1)S(1)} collective-permute-done((bf16[192,1024]{1,0:T(8,128)(2,1)}, bf16[192,1024]{1,0:T(8,128)(2,1)S(1)}, u32[]{:S(2)}, u32[]{:S(2)}) %collective-permute-start) | collective-permute-done | bytes 393248 | tf_op jit(solution)/shard_map/ppermute | solution.py:421
  24.1 2.2 %collective-permute-start.6 = (bf16[192,1024]{1,0:T(8,128)(2,1)S(1)}, bf16[192,1024]{1,0:T(8,128)(2,1)S(1)}, u32[]{:S(2)}, u32[]{:S(2)}) collective-permute-start(bf16[192,1024]{1,0:T(8,128)(2,1)S(1)} %collective-permute-done.query_ref), channel_id=1, source_target_pairs={{1,2},{2,1},{5,6},{6,5},{9,10},{10,9},{13,14},{14,13},{17,18},{18,... | collective-permute-start | bytes 1179656 | tf_op jit(solution)/shard_map/ppermute | solution.py:421
  26.3 0.0 collective-permute-done.4
  26.3 0.5 collective-permute-done.3
  26.8 2.0 %collective-permute-start.8 = (bf16[2,64,2048]{2,1,0:T(8,128)(2,1)S(1)}, bf16[2,64,2048]{2,1,0:T(8,128)(2,1)S(1)}, u32[]{:S(2)}, u32[]{:S(2)}) collective-permute-start(bf16[2,64,2048]{2,1,0:T(8,128)(2,1)S(1)} %copy-done.8), channel_id=1, source_target_pairs={{0,24},{4,28},{8,16},{12,20},{16,8},{20,12},{24,0},{28,4},{1,25},{... | collective-permute-start | bytes 1572872 | tf_op jit(solution)/shard_map/ppermute | solution.py:425
  28.9 1.1 %side.1.own_ref = bf16[2,200,512]{2,1,0:T(8,128)(2,1)S(1)} custom-call(s32[1,1]{1,0:T(1,128)S(6)} %copy.10.filled_ref.refs_0_, bf16[192,1024]{1,0:T(8,128)(2,1)S(1)} %collective-permute-done.query_ref, bf16[384,1024]{1,0:T(8,128)(2,1)S(1)} %bitcast.15, bf16[384,1024]{1,0:T(8,128)(2,1)S(1)} %bitcast.21), custom_call_target="tpu_custom_call" | custom-call | flops 1 | bytes 1 | tf_op jit(solution)/shard_map/side/pallas_call | solution.py:428
  30.0 1.1 %middle.1.own_ref = bf16[2,200,512]{2,1,0:T(8,128)(2,1)S(1)} custom-call(s32[1,1]{1,0:T(1,128)S(6)} %copy.10.filled_ref.refs_0_, bf16[192,1024]{1,0:T(8,128)(2,1)S(1)} %collective-permute-done.2.middle_ref.refs_1_, bf16[384,1024]{1,0:T(8,128)(2,1)S(1)} %bitcast.16, bf16[384,1024]{1,0:T(8,128)(2,1)S(1)} %bitcast.22), custom_call_target="tpu_custom_call" | custom-call | flops 1 | bytes 1 | tf_op jit(solution)/shard_map/middle/pallas_call | solution.py:428
  31.1 4.9 %collective-permute-done.6.refs_1_ = bf16[192,1024]{1,0:T(8,128)(2,1)S(1)} collective-permute-done((bf16[192,1024]{1,0:T(8,128)(2,1)S(1)}, bf16[192,1024]{1,0:T(8,128)(2,1)S(1)}, u32[]{:S(2)}, u32[]{:S(2)}) %collective-permute-start.6) | collective-permute-done | bytes 393248 | tf_op jit(solution)/shard_map/ppermute | solution.py:421
  36.0 0.0 collective-permute-done.5.refs_1_.other_ref
  36.0 1.3 %collective-permute-start.7 = (bf16[2,200,512]{2,1,0:T(8,128)(2,1)S(1)}, bf16[2,200,512]{2,1,0:T(8,128)(2,1)S(1)}, u32[]{:S(2)}, u32[]{:S(2)}) collective-permute-start(bf16[2,200,512]{2,1,0:T(8,128)(2,1)S(1)} %turned.1), channel_id=1, source_target_pairs={{0,1},{3,2},{4,5},{7,6},{8,9},{11,10},{12,13},{15,14},{16,17},{19,... | collective-permute-start | bytes 1228808 | tf_op jit(solution)/shard_map/ppermute | solution.py:421
  37.3 1.1 %passed.1.own_ref = bf16[2,200,512]{2,1,0:T(8,128)(2,1)S(1)} custom-call(s32[1,1]{1,0:T(1,128)S(6)} %copy.10.filled_ref.refs_0_, bf16[192,1024]{1,0:T(8,128)(2,1)S(1)} %collective-permute-done.6.refs_1_, bf16[384,1024]{1,0:T(8,128)(2,1)S(1)} %bitcast.18, bf16[384,1024]{1,0:T(8,128)(2,1)S(1)} %bitcast.24), custom_call_target="tpu_custom_call" | custom-call | flops 1 | bytes 1 | tf_op jit(solution)/shard_map/passed/pallas_call | solution.py:428
  38.4 0.6 met.1
  39.0 2.2 %collective-permute-start.9 = (bf16[2,200,512]{2,1,0:T(8,128)(2,1)S(1)}, bf16[2,200,512]{2,1,0:T(8,128)(2,1)S(1)}, u32[]{:S(2)}, u32[]{:S(2)}) collective-permute-start(bf16[2,200,512]{2,1,0:T(8,128)(2,1)S(1)} %met.1), channel_id=1, source_target_pairs={{1,2},{2,1},{5,6},{6,5},{9,10},{10,9},{13,14},{14,13},{17,18},{18,... | collective-permute-start | bytes 1228808 | tf_op jit(solution)/shard_map/ppermute | solution.py:421
  41.2 6.1 %collective-permute-done.7.other_ref = bf16[2,200,512]{2,1,0:T(8,128)(2,1)S(1)} collective-permute-done((bf16[2,200,512]{2,1,0:T(8,128)(2,1)S(1)}, bf16[2,200,512]{2,1,0:T(8,128)(2,1)S(1)}, u32[]{:S(2)}, u32[]{:S(2)}) %collective-permute-start.7) | collective-permute-done | bytes 409632 | tf_op jit(solution)/shard_map/ppermute | solution.py:421
  47.3 0.6 join.2
  47.9 0.0 collective-permute-done.8
  47.9 0.0 copy-start.4
  48.0 0.0 copy-start.6
  48.0 0.0 copy-start.7
  48.0 0.3 pad_maximum_fusion.refs_0_
  48.3 2.1 %collective-permute-done.9.other_ref = bf16[2,200,512]{2,1,0:T(8,128)(2,1)S(1)} collective-permute-done((bf16[2,200,512]{2,1,0:T(8,128)(2,1)S(1)}, bf16[2,200,512]{2,1,0:T(8,128)(2,1)S(1)}, u32[]{:S(2)}, u32[]{:S(2)}) %collective-permute-start.9) | collective-permute-done | bytes 409632 | tf_op jit(solution)/shard_map/ppermute | solution.py:421
  50.4 0.6 join.3
  51.0 0.1 collective-permute-start.10
  51.1 0.1 collective-permute-start.11
  51.1 2.4 %collective-permute-start.12 = (bf16[2,200,512]{2,1,0:T(8,128)(2,1)S(1)}, bf16[2,200,512]{2,1,0:T(8,128)(2,1)S(1)}, u32[]{:S(2)}, u32[]{:S(2)}) collective-permute-start(bf16[2,200,512]{2,1,0:T(8,128)(2,1)S(1)} %join.2), channel_id=1, source_target_pairs={{1,2},{2,1},{5,6},{6,5},{9,10},{10,9},{13,14},{14,13},{17,18},{18,... | collective-permute-start | bytes 1228808 | tf_op jit(solution)/shard_map/ppermute | solution.py:421
  53.5 1.7 %collective-permute-done.10.refs_1_ = bf16[4,2,64,2048]{3,2,1,0:T(8,128)(2,1)S(1)} collective-permute-done((bf16[4,2,64,2048]{3,2,1,0:T(8,128)(2,1)S(1)}, bf16[4,2,64,2048]{3,2,1,0:T(8,128)(2,1)S(1)}, u32[]{:S(2)}, u32[]{:S(2)}) %collective-permute-start.10) | collective-permute-done | bytes 2097184 | tf_op jit(solution)/shard_map/ppermute | solution.py:425
  55.2 0.0 copy-done.6
  55.2 4.9 %spans.1 = bf16[192,1024]{1,0:T(8,128)(2,1)} custom-call(s32[16]{0:T(128)S(1)} %copy-done.7, s32[2,12]{1,0:T(2,128)S(1)} %bitcast.30, bf16[192,1024]{1,0:T(8,128)(2,1)S(1)} %bitcast.25, bf16[4,2,64,2048]{3,2,1,0:T(8,128)(2,1)S(1)} %pad_maximum_fusion.refs_0_, bf16[4,2,64,2048]{3,2,1,0:T(8,128)(2,1)S(1)} %collective-permute-done.10.refs_1_), custom_call_target="tpu_custom_call" | custom-call | flops 1 | bytes 1 | tf_op jit(solution)/shard_map/spans/pallas_call | solution.py:464
  60.1 2.8 %collective-permute-done.11.side_ref = bf16[2,200,512]{2,1,0:T(8,128)(2,1)S(1)} collective-permute-done((bf16[2,200,512]{2,1,0:T(8,128)(2,1)S(1)}, bf16[2,200,512]{2,1,0:T(8,128)(2,1)S(1)}, u32[]{:S(2)}, u32[]{:S(2)}) %collective-permute-start.11) | collective-permute-done | bytes 409632 | tf_op jit(solution)/shard_map/ppermute | solution.py:421
  62.9 0.6 near.1.near_ref
  63.5 1.3 %collective-permute-done.12.middle_ref = bf16[2,200,512]{2,1,0:T(8,128)(2,1)S(1)} collective-permute-done((bf16[2,200,512]{2,1,0:T(8,128)(2,1)S(1)}, bf16[2,200,512]{2,1,0:T(8,128)(2,1)S(1)}, u32[]{:S(2)}, u32[]{:S(2)}) %collective-permute-start.12) | collective-permute-done | bytes 409632 | tf_op jit(solution)/shard_map/ppermute | solution.py:421
  64.8 1.4 %closing.1 = bf16[192,1024]{1,0:T(8,128)(2,1)} custom-call(bf16[2,200,512]{2,1,0:T(8,128)(2,1)S(1)} %near.1.near_ref, bf16[2,200,512]{2,1,0:T(8,128)(2,1)S(1)} %collective-permute-done.12.middle_ref), custom_call_target="tpu_custom_call" | custom-call | flops 1 | bytes 1 | tf_op jit(solution)/shard_map/closing/pallas_call | solution.py:472
  (9 shorter events, 0.0 us)
Async XLA Ops:
  0.6 11.8 %collective-permute-start.1 = (bf16[192,1024]{1,0:T(8,128)(2,1)}, bf16[192,1024]{1,0:T(8,128)(2,1)S(1)}, u32[]{:S(2)}, u32[]{:S(2)}) collective-permute-start(bf16[192,1024]{1,0:T(8,128)(2,1)} %bitcast.26), channel_id=1, source_target_pairs={{0,3},{3,0},{4,7},{7,4},{8,11},{11,8},{12,15},{15,12},{16,19},{19,... | collective-permute-start | bytes 1179656 | tf_op jit(solution)/shard_map/ppermute | solution.py:421
  1.3 21.4 %collective-permute-start.2 = (bf16[192,1024]{1,0:T(8,128)(2,1)}, bf16[192,1024]{1,0:T(8,128)(2,1)S(1)}, u32[]{:S(2)}, u32[]{:S(2)}) collective-permute-start(bf16[192,1024]{1,0:T(8,128)(2,1)} %bitcast.27), channel_id=1, source_target_pairs={{1,2},{2,1},{5,6},{6,5},{9,10},{10,9},{13,14},{14,13},{17,18},{18,... | collective-permute-start | bytes 1179656 | tf_op jit(solution)/shard_map/ppermute | solution.py:421
  4.8 19.3 %collective-permute-start = (bf16[192,1024]{1,0:T(8,128)(2,1)}, bf16[192,1024]{1,0:T(8,128)(2,1)S(1)}, u32[]{:S(2)}, u32[]{:S(2)}) collective-permute-start(bf16[192,1024]{1,0:T(8,128)(2,1)} %bitcast.28), channel_id=1, source_target_pairs={{0,1},{1,0},{2,3},{3,2},{4,5},{5,4},{6,7},{7,6},{8,9},{9,8},{10,11... | collective-permute-start | bytes 1179656 | tf_op jit(solution)/shard_map/ppermute | solution.py:421
  8.0 1.1 %copy-start = (bf16[1,384,1024]{2,1,0:T(8,128)(2,1)S(1)}, bf16[1,384,1024]{2,1,0:T(8,128)(2,1)}, u32[]{:S(2)}) copy-start(bf16[1,384,1024]{2,1,0:T(8,128)(2,1)} %param.9) | copy-start | bytes 2359300
  9.1 1.1 %copy-start.2 = (bf16[1,384,1024]{2,1,0:T(8,128)(2,1)S(1)}, bf16[1,384,1024]{2,1,0:T(8,128)(2,1)}, u32[]{:S(2)}) copy-start(bf16[1,384,1024]{2,1,0:T(8,128)(2,1)} %param.10) | copy-start | bytes 2359300
  10.3 1.0 %copy-start.5 = (bf16[1,192,1024]{2,1,0:T(8,128)(2,1)S(1)}, bf16[1,192,1024]{2,1,0:T(8,128)(2,1)}, u32[]{:S(2)}) copy-start(bf16[1,192,1024]{2,1,0:T(8,128)(2,1)} %param.8) | copy-start | bytes 1179652
  11.3 1.1 %copy-start.8 = (bf16[2,64,2048]{2,1,0:T(8,128)(2,1)S(1)}, bf16[2,64,2048]{2,1,0:T(8,128)(2,1)}, u32[]{:S(2)}) copy-start(bf16[2,64,2048]{2,1,0:T(8,128)(2,1)} %param.13) | copy-start | bytes 1572868
  11.3 11.4 %copy-start.1 = (bf16[1,384,1024]{2,1,0:T(8,128)(2,1)S(1)}, bf16[1,384,1024]{2,1,0:T(8,128)(2,1)}, u32[]{:S(2)}) copy-start(bf16[1,384,1024]{2,1,0:T(8,128)(2,1)} %param.9) | copy-start | bytes 2359300
  11.3 11.4 %copy-start.3 = (bf16[1,384,1024]{2,1,0:T(8,128)(2,1)S(1)}, bf16[1,384,1024]{2,1,0:T(8,128)(2,1)}, u32[]{:S(2)}) copy-start(bf16[1,384,1024]{2,1,0:T(8,128)(2,1)} %param.10) | copy-start | bytes 2359300
  12.4 13.9 %collective-permute-start.4 = (bf16[2,64,2048]{2,1,0:T(8,128)(2,1)S(1)}, bf16[2,64,2048]{2,1,0:T(8,128)(2,1)S(1)}, u32[]{:S(2)}, u32[]{:S(2)}) collective-permute-start(bf16[2,64,2048]{2,1,0:T(8,128)(2,1)S(1)} %copy-done.8), channel_id=1, source_target_pairs={{0,16},{4,20},{8,24},{12,28},{16,0},{20,4},{24,8},{28,12},{1,17},{... | collective-permute-start | bytes 1572872 | tf_op jit(solution)/shard_map/ppermute | solution.py:425
  14.0 12.8 %collective-permute-start.3 = (bf16[2,64,2048]{2,1,0:T(8,128)(2,1)S(1)}, bf16[2,64,2048]{2,1,0:T(8,128)(2,1)S(1)}, u32[]{:S(2)}, u32[]{:S(2)}) collective-permute-start(bf16[2,64,2048]{2,1,0:T(8,128)(2,1)S(1)} %copy-done.8), channel_id=1, source_target_pairs={{0,8},{4,12},{8,0},{12,4},{16,24},{20,28},{24,16},{28,20},{1,9},{5... | collective-permute-start | bytes 1572872 | tf_op jit(solution)/shard_map/ppermute | solution.py:425
  22.7 13.2 %collective-permute-start.5 = (bf16[2,200,512]{2,1,0:T(8,128)(2,1)S(1)}, bf16[2,200,512]{2,1,0:T(8,128)(2,1)S(1)}, u32[]{:S(2)}, u32[]{:S(2)}) collective-permute-start(bf16[2,200,512]{2,1,0:T(8,128)(2,1)S(1)} %far.1), channel_id=1, source_target_pairs={{0,1},{1,0},{2,3},{3,2},{4,5},{5,4},{6,7},{7,6},{8,9},{9,8},{10,11... | collective-permute-start | bytes 1228808 | tf_op jit(solution)/shard_map/ppermute | solution.py:421
  24.1 11.9 %collective-permute-start.6 = (bf16[192,1024]{1,0:T(8,128)(2,1)S(1)}, bf16[192,1024]{1,0:T(8,128)(2,1)S(1)}, u32[]{:S(2)}, u32[]{:S(2)}) collective-permute-start(bf16[192,1024]{1,0:T(8,128)(2,1)S(1)} %collective-permute-done.query_ref), channel_id=1, source_target_pairs={{1,2},{2,1},{5,6},{6,5},{9,10},{10,9},{13,14},{14,13},{17,18},{18,... | collective-permute-start | bytes 1179656 | tf_op jit(solution)/shard_map/ppermute | solution.py:421
  26.8 21.1 %collective-permute-start.8 = (bf16[2,64,2048]{2,1,0:T(8,128)(2,1)S(1)}, bf16[2,64,2048]{2,1,0:T(8,128)(2,1)S(1)}, u32[]{:S(2)}, u32[]{:S(2)}) collective-permute-start(bf16[2,64,2048]{2,1,0:T(8,128)(2,1)S(1)} %copy-done.8), channel_id=1, source_target_pairs={{0,24},{4,28},{8,16},{12,20},{16,8},{20,12},{24,0},{28,4},{1,25},{... | collective-permute-start | bytes 1572872 | tf_op jit(solution)/shard_map/ppermute | solution.py:425
  36.0 11.3 %collective-permute-start.7 = (bf16[2,200,512]{2,1,0:T(8,128)(2,1)S(1)}, bf16[2,200,512]{2,1,0:T(8,128)(2,1)S(1)}, u32[]{:S(2)}, u32[]{:S(2)}) collective-permute-start(bf16[2,200,512]{2,1,0:T(8,128)(2,1)S(1)} %turned.1), channel_id=1, source_target_pairs={{0,1},{3,2},{4,5},{7,6},{8,9},{11,10},{12,13},{15,14},{16,17},{19,... | collective-permute-start | bytes 1228808 | tf_op jit(solution)/shard_map/ppermute | solution.py:421
  39.0 11.3 %collective-permute-start.9 = (bf16[2,200,512]{2,1,0:T(8,128)(2,1)S(1)}, bf16[2,200,512]{2,1,0:T(8,128)(2,1)S(1)}, u32[]{:S(2)}, u32[]{:S(2)}) collective-permute-start(bf16[2,200,512]{2,1,0:T(8,128)(2,1)S(1)} %met.1), channel_id=1, source_target_pairs={{1,2},{2,1},{5,6},{6,5},{9,10},{10,9},{13,14},{14,13},{17,18},{18,... | collective-permute-start | bytes 1228808 | tf_op jit(solution)/shard_map/ppermute | solution.py:421
  47.9 7.3 %copy-start.4 = (bf16[1,192,1024]{2,1,0:T(8,128)(2,1)S(1)}, bf16[1,192,1024]{2,1,0:T(8,128)(2,1)}, u32[]{:S(2)}) copy-start(bf16[1,192,1024]{2,1,0:T(8,128)(2,1)} %param.12) | copy-start | bytes 1179652
  48.0 7.2 %copy-start.6 = (s32[1,12,2]{1,2,0:T(2,128)S(1)}, s32[1,12,2]{1,2,0:T(2,128)}, u32[]{:S(2)}) copy-start(s32[1,12,2]{1,2,0:T(2,128)} %param.15) | copy-start | bytes 292
  48.0 7.2 %copy-start.7 = (s32[16]{0:T(128)S(1)}, s32[16]{0:T(128)}, u32[]{:S(2)}) copy-start(s32[16]{0:T(128)} %home_ref.1) | copy-start | bytes 196
  51.0 4.2 %collective-permute-start.10 = (bf16[4,2,64,2048]{3,2,1,0:T(8,128)(2,1)S(1)}, bf16[4,2,64,2048]{3,2,1,0:T(8,128)(2,1)S(1)}, u32[]{:S(2)}, u32[]{:S(2)}) collective-permute-start(bf16[4,2,64,2048]{3,2,1,0:T(8,128)(2,1)S(1)} %pad_maximum_fusion.refs_0_), channel_id=1, source_target_pairs={{0,4},{4,0},{8,12},{12,8},{16,20},{20,16},{24,28},{28,24},{1,5},{5... | collective-permute-start | bytes 6291464 | tf_op jit(solution)/shard_map/ppermute | solution.py:425
  51.1 11.9 %collective-permute-start.11 = (bf16[2,200,512]{2,1,0:T(8,128)(2,1)S(1)}, bf16[2,200,512]{2,1,0:T(8,128)(2,1)S(1)}, u32[]{:S(2)}, u32[]{:S(2)}) collective-permute-start(bf16[2,200,512]{2,1,0:T(8,128)(2,1)S(1)} %join.3), channel_id=1, source_target_pairs={{0,1},{1,0},{2,3},{3,2},{4,5},{5,4},{6,7},{7,6},{8,9},{9,8},{10,11... | collective-permute-start | bytes 1228808 | tf_op jit(solution)/shard_map/ppermute | solution.py:421
  51.1 13.7 %collective-permute-start.12 = (bf16[2,200,512]{2,1,0:T(8,128)(2,1)S(1)}, bf16[2,200,512]{2,1,0:T(8,128)(2,1)S(1)}, u32[]{:S(2)}, u32[]{:S(2)}) collective-permute-start(bf16[2,200,512]{2,1,0:T(8,128)(2,1)S(1)} %join.2), channel_id=1, source_target_pairs={{1,2},{2,1},{5,6},{6,5},{9,10},{10,9},{13,14},{14,13},{17,18},{18,... | collective-permute-start | bytes 1228808 | tf_op jit(solution)/shard_map/ppermute | solution.py:421
